TPU v7x, 512 devices: a whole 4x8x8 slice. The times are simulated.
512 devices in a mesh: ctx: 64 (over z_lo, y, core), head: 8 (over x, z_hi).
Axes of the slice: x: 4, y: 8, z: 8 (z_hi: 2, z_lo: 4; z = z_hi * 4 + z_lo), core: 2. Of those that a mesh axis runs over, the one named last changes fastest.
Arguments:
- tokens: bfloat16 [32768, 3840], P('ctx', 'head'), may hold values from -18 to 18
- w_query: bfloat16 [3840, 4096], P('ctx', 'head'), may hold values from -0.09375 to 0.09375
- key_matrix: bfloat16 [3840, 2048], P('ctx', 'head'), may hold values from -0.09375 to 0.09375
- value_matrix: bfloat16 [3840, 2048], P('ctx', 'head'), may hold values from -0.09375 to 0.09375
- d_attended: bfloat16 [32768, 4096], P('ctx', 'head'), may hold values from -6 to 6
- doc_lengths: int32 [32], replicated, may hold values from 1 to 2048, 32768 in all
Outputs:
- attended: bfloat16 [32768, 4096], P('ctx', 'head')
- key_grad: bfloat16 [32768, 2048], P('ctx', 'head')
Inputs may be any that keep to these rules, and one draw needn't show every extreme that they name: `doc_lengths`: the documents lie end to end from position 0 and fill all 32768 positions.
All inputs are finite; a program needn't handle non-finite values.
Results may differ from a plain program's by a relative error of at most 0.012.
The roundings to bfloat16 on the way count: a program that leaves them out, or rounds other values in their place, can miss the bound.
Values may be sent and summed in bfloat16 or wider, within the bound.
No kernel may reach another device: no remote copies, remote signals or barrier semaphores. Data moves between devices by JAX's collectives and lax.ppermute only.
A program may use at most 64 MiB of HBM per device.

v0:
```python
import jax
import jax.numpy as jnp
from jax import lax
from jax.experimental import pallas as pl
from jax.experimental.pallas import tpu as pltpu
from jax.sharding import PartitionSpec as P


HEAD_SIZE = 256
WINDOW = 1024
NX, NY, NZL, NZH = 4, 8, 4, 2
NZ = NZL * NZH
ROWS = 60
PAD = 64
PAIR = 2 * PAD
BOTH = ("ctx", "head")
BF = jnp.bfloat16
F32 = jnp.float32


def place(x, y, z, core):
    x, y, z = x % NX, y % NY, z % NZ
    ctx = (z % NZL) * 2 * NY + 2 * y + core
    return ctx * (NX * NZH) + x * NZH + z // NZL


def hop(block, dx=0, dy=0, dz=0, swap=0, by_core=False):
    route = []
    for x in range(NX):
        for y in range(NY):
            for z in range(NZ):
                for core in range(2):
                    s = 1 - 2 * core if by_core else 1
                    route.append(
                        (
                            place(x, y, z, core),
                            place(x + s * dx, y + s * dy, z + s * dz, core ^ swap),
                        )
                    )
    return lax.ppermute(block, BOTH, route)


def along_ctx(block, distance):
    n = lax.axis_size("ctx")
    route = [(i - distance, i) for i in range(n) if 0 <= i - distance < n]
    return lax.ppermute(block, "ctx", route)


def project_body(pos, t0, t1, t2, t3, p0, p1, p2, p3, *refs, scale, swaps):
    *blocks, o_ref = refs
    own_ref, r1, r2, r3, r4 = blocks[:5]
    swapped = blocks[5:]
    x, y, zh, sign, core = pos[0], pos[1], pos[2], pos[3], pos[4]
    total = jnp.zeros(o_ref.shape, F32)

    def back(step, z):
        ref, at = swaps[step - 1]
        return swapped[ref][at + z]

    for slot, (near, far) in enumerate(((t0, p0), (t1, p1), (t2, p2), (t3, p3))):
        z = lax.rem(x - sign * slot + NX, NX)
        half = lax.rem(z, 2)

        def columns(distance):
            chip = lax.rem(y + sign * distance + NY, NY)
            at = pl.multiple_of(lax.rem(chip, 4) * PAIR, PAIR)
            return jnp.where(lax.div(chip, 4) == zh, near[:, pl.ds(at, PAIR)], far[:, pl.ds(at, PAIR)])

        left = [columns(d) for d in (0, 4, -1, 1, -2, 2, -3, 3)]
        right = [own_ref[z], jnp.where(lax.div(z, 2) == core, r4[half], back(4, half))]
        for step, ref in ((1, r1), (2, r2), (3, r3)):
            right += [ref[z], back(step, z)]
        total += jnp.dot(
            jnp.concatenate(left, axis=1),
            jnp.concatenate(right, axis=0),
            preferred_element_type=F32,
        )
    o_ref[...] = (total * scale).astype(BF)


def project(pos, near, far, ring, swapped, swaps, scale):
    rows = near[0].shape[0]
    cols = ring[0].shape[-1]
    full = pl.BlockSpec(memory_space=pltpu.VMEM)
    operands = [*near, *far, *ring, *swapped]
    return pl.pallas_call(
        lambda *refs: project_body(*refs, scale=scale, swaps=swaps),
        out_shape=jax.ShapeDtypeStruct((rows, cols), BF),
        in_specs=[pl.BlockSpec(memory_space=pltpu.SMEM)] + [full] * len(operands),
        out_specs=full,
        cost_estimate=pl.CostEstimate(
            flops=2 * rows * 4096 * cols,
            bytes_accessed=2 * (rows * 4096 + cols * 4096 + rows * cols),
            transcendentals=0,
        ),
        compiler_params=pltpu.CompilerParams(vmem_limit_bytes=48 * 1024 * 1024),
        name="project",
    )(pos, *operands)


def ring_y(block, core):
    out = [block]
    for _ in range(3):
        out.append(hop(out[-1], dy=1, by_core=True))
    half = lax.dynamic_slice_in_dim(out[-1], 2 * core, 2, 0)
    out.append(hop(half, dy=1, by_core=True))
    return out


def ring_x(block):
    out = [block]
    for _ in range(3):
        out.append(hop(out[-1], dx=1, by_core=True))
    return out


def gather_zcore(w):
    groups = [
        [z * 2 * NY + 2 * y + core for z in range(NZL) for core in range(2)] for y in range(NY)
    ]
    return lax.all_gather(w, "ctx", axis=0, tiled=False, axis_index_groups=groups)


TILE = 256
REACH = 5 * TILE


def scores_body(lead, len_ref, q_ref, own, e1, e2, g_ref, p_ref, dk0, dk1, dk2, ext, s_ref, d_ref, acc):
    rows = q_ref.shape[0]
    ext[0:rows] = e2[...]
    ext[rows : 2 * rows] = e1[...]
    ext[2 * rows : 3 * rows] = own[...]
    acc[...] = jnp.zeros_like(acc)
    docs = len_ref.shape[1]
    i0 = lax.broadcasted_iota(jnp.int32, (docs, docs), 0)
    i1 = lax.broadcasted_iota(jnp.int32, (docs, docs), 1)
    starts = jnp.sum(jnp.where(i1 < i0, len_ref[...], 0), axis=1, keepdims=True)

    @pl.loop(0, 4)
    def _(step):
        i, h = lax.rem(step, 2), lax.div(step, 2)
        row0 = pl.multiple_of(i * TILE, TILE)
        col0 = pl.multiple_of(h * HEAD_SIZE, HEAD_SIZE)
        q = q_ref[pl.ds(row0, TILE), pl.ds(col0, HEAD_SIZE)]
        g = g_ref[pl.ds(row0, TILE), pl.ds(col0, HEAD_SIZE)]
        row = row0 + lax.broadcasted_iota(jnp.int32, (1, TILE), 1)
        at = lead[0] + row
        begin = jnp.max(jnp.where(starts <= at, starts, 0), axis=0, keepdims=True)
        low = jnp.maximum(begin - lead[0] + WINDOW, row + 1)
        nt = (((1,), (1,)), ((), ()))
        peak = jnp.full((1, TILE), -1e30, F32)
        for j in range(5):
            first = pl.multiple_of(row0 + j * TILE, TILE)
            s = lax.dot_general(ext[pl.ds(first, TILE), :HEAD_SIZE], q, nt, preferred_element_type=F32)
            key = first + lax.broadcasted_iota(jnp.int32, (TILE, 1), 0)
            ok = key >= low
            if j == 4:
                ok = ok & (key <= row + WINDOW)
            s = jnp.where(ok, s, -1e30)
            s_ref[j * TILE : (j + 1) * TILE] = s
            peak = jnp.maximum(peak, jnp.max(s, axis=0, keepdims=True))
        total = jnp.zeros((1, TILE), F32)
        for j in range(5):
            e = jnp.exp(s_ref[j * TILE : (j + 1) * TILE] - peak)
            s_ref[j * TILE : (j + 1) * TILE] = e
            total += jnp.sum(e, axis=0, keepdims=True)
        inverse = 1.0 / total
        delta = jnp.zeros((1, TILE), F32)
        for j in range(5):
            first = pl.multiple_of(row0 + j * TILE, TILE)
            d = lax.dot_general(ext[pl.ds(first, TILE), HEAD_SIZE:], g, nt, preferred_element_type=F32)
            p = s_ref[j * TILE : (j + 1) * TILE] * inverse
            s_ref[j * TILE : (j + 1) * TILE] = p
            d_ref[j * TILE : (j + 1) * TILE] = d
            p_ref[step, j * TILE : (j + 1) * TILE] = p.astype(BF)
            delta += jnp.sum(p * d, axis=0, keepdims=True)
        for j in range(5):
            first = pl.multiple_of(row0 + j * TILE, TILE)
            part = slice(j * TILE, (j + 1) * TILE)
            ds = (s_ref[part] * (d_ref[part] - delta)).astype(BF)
            acc[pl.ds(first, TILE)] += jnp.dot(ds, q, preferred_element_type=F32)

    dk2[...] = acc[0:rows].astype(BF)
    dk1[...] = acc[rows : 2 * rows].astype(BF)
    dk0[...] = acc[2 * rows : 3 * rows]


def values_body(p_ref, own, e1, e2, o_ref):
    tn = (((0,), (0,)), ((), ()))
    for i in range(2):
        value = jnp.concatenate(
            [e2[i * TILE :, HEAD_SIZE:], e1[:, HEAD_SIZE:], own[: (i + 1) * TILE, HEAD_SIZE:]], axis=0
        )
        for h in range(2):
            a = lax.dot_general(p_ref[2 * h + i], value, tn, preferred_element_type=F32)
            o_ref[i * TILE : (i + 1) * TILE, h * HEAD_SIZE : (h + 1) * HEAD_SIZE] = a.astype(BF)


def attend(lead, lens, query, own, e1, e2, grad):
    rows = query.shape[0]
    full = pl.BlockSpec(memory_space=pltpu.VMEM)
    smem = pl.BlockSpec(memory_space=pltpu.SMEM)
    shape = jax.ShapeDtypeStruct
    pairs = 4 * TILE * REACH
    p, dk0, dk1, dk2 = pl.pallas_call(
        scores_body,
        out_shape=(
            shape((4, REACH, TILE), BF),
            shape((rows, HEAD_SIZE), F32),
            shape((rows, HEAD_SIZE), BF),
            shape((rows, HEAD_SIZE), BF),
        ),
        in_specs=[smem] + [full] * 6,
        out_specs=(full,) * 4,
        scratch_shapes=[
            pltpu.VMEM((3 * rows, 2 * HEAD_SIZE), BF),
            pltpu.VMEM((REACH, TILE), F32),
            pltpu.VMEM((REACH, TILE), F32),
            pltpu.VMEM((3 * rows, HEAD_SIZE), F32),
        ],
        cost_estimate=pl.CostEstimate(
            flops=6 * pairs * HEAD_SIZE, bytes_accessed=5 * rows * 1024 + 2 * pairs, transcendentals=pairs
        ),
        compiler_params=pltpu.CompilerParams(vmem_limit_bytes=48 * 1024 * 1024),
        name="scores",
    )(lead, lens, query, own, e1, e2, grad)
    out = pl.pallas_call(
        values_body,
        out_shape=shape((rows, 2 * HEAD_SIZE), BF),
        in_specs=[full] * 4,
        out_specs=full,
        cost_estimate=pl.CostEstimate(
            flops=2 * pairs * HEAD_SIZE, bytes_accessed=4 * rows * 1024 + 2 * pairs, transcendentals=0
        ),
        compiler_params=pltpu.CompilerParams(vmem_limit_bytes=48 * 1024 * 1024),
        name="values",
    )(p, own, e1, e2)
    return out, dk0, dk1, dk2


def local(tokens, w_query, key_matrix, value_matrix, d_attended, doc_lengths):
    rows = tokens.shape[0]
    ctx = lax.axis_index("ctx").astype(jnp.int32)
    head = lax.axis_index("head").astype(jnp.int32)
    core, y = ctx % 2, (ctx // 2) % NY
    x, zh = head // NZH, head % NZH
    pos = jnp.stack([x, y, zh, 1 - 2 * core, core])

    feature = jnp.arange(tokens.shape[1], dtype=jnp.int32)
    target = feature // ROWS * PAD + feature % ROWS
    spread = (target[:, None] == jnp.arange(8 * PAD, dtype=jnp.int32)[None, :]).astype(BF)
    own = jnp.dot(tokens, spread, preferred_element_type=F32).astype(BF)

    partner = hop(own, dz=NZL)
    near = ring_x(own)
    far = ring_x(partner)

    w = gather_zcore(jnp.concatenate([key_matrix, value_matrix, w_query], axis=1))
    w = jnp.pad(w, ((0, 0), (0, PAD - ROWS), (0, 0)))
    kv_cols = 2 * HEAD_SIZE
    kv = ring_y(w[:, :, :kv_cols].reshape(NZL, PAIR, kv_cols), core)
    kv_a = hop(jnp.concatenate(kv[1:3], axis=0), swap=1)
    kv_b = hop(jnp.concatenate(kv[3:], axis=0), swap=1)
    qs = ring_y(w[:, :, kv_cols:].reshape(NZL, PAIR, -1), core)
    q_a = hop(jnp.concatenate(qs[1:], axis=0), swap=1)

    joined = project(pos, near, far, kv, [kv_a, kv_b], ((0, 0), (0, 4), (1, 0), (1, 4)), 1.0)
    query = project(pos, near, far, qs, [q_a], ((0, 0), (0, 4), (0, 8), (0, 12)), 0.0625)

    e2 = along_ctx(joined, 2)
    e1 = along_ctx(joined, 1)
    lead = (ctx * rows).reshape(1)
    attended, dk0, dk1, dk2 = attend(
        lead, doc_lengths.reshape(1, -1), query, joined, e1, e2, d_attended
    )
    key_total = dk0 + along_ctx(dk2, -2).astype(F32) + along_ctx(dk1, -1).astype(F32)
    return (attended, key_total.astype(BF))


def solution(mesh):
    return jax.shard_map(
        local,
        mesh=mesh,
        in_specs=(
            P("ctx", "head"),
            P("ctx", "head"),
            P("ctx", "head"),
            P("ctx", "head"),
            P("ctx", "head"),
            P(),
        ),
        out_specs=(P("ctx", "head"), P("ctx", "head")),
        check_vma=False,
    )
```

profile of v0, /device:TPU:64, one launch (start us, length us, event | category | flops | bytes accessed | tf_op | source)
XLA Modules:
  0.0 181.7 jit_solution(12667387820454550918)
XLA Ops:
  1.6 18.9 %all-gather.1 = bf16[8,60,1024]{2,1,0:T(8,128)(2,1)S(1)} all-gather(bf16[1,60,1024]{2,1,0:T(8,128)(2,1)S(1)} %maximum_bitcast_fusion), channel_id=2, replica_groups={{0,8,128,136,256,264,384,392},{16,24,144,152,272,280,400,408},{32,40,16..., dimensions={0}, use_global_device_ids=true | all-gather | bytes 1105920 | tf_op jit(solution)/shard_map/all_gather | solution.py:121
  20.6 3.3 %collective-permute-start.7 = (bf16[4,128,512]{2,1,0:T(8,128)(2,1)S(1)}, bf16[4,128,512]{2,1,0:T(8,128)(2,1)S(1)}, u32[]{:S(2)}, u32[]{:S(2)}) collective-permute-start(bf16[4,128,512]{2,1,0:T(8,128)(2,1)S(1)} %bitcast.14), channel_id=1, source_target_pairs={{0,16},{8,120},{128,144},{136,248},{256,272},{264,376},{384,400},{... | collective-permute-start | bytes 1572872 | tf_op jit(solution)/shard_map/ppermute | solution.py:40
  23.9 3.5 %collective-permute-start.12 = (bf16[4,128,512]{2,1,0:T(8,128)(2,1)S(1)}, bf16[4,128,512]{2,1,0:T(8,128)(2,1)}, u32[]{:S(2)}, u32[]{:S(2)}) collective-permute-start(bf16[4,128,512]{2,1,0:T(8,128)(2,1)S(1)} %bitcast.16), channel_id=1, source_target_pairs={{0,16},{8,120},{128,144},{136,248},{256,272},{264,376},{384,400},{... | collective-permute-start | bytes 1572872 | tf_op jit(solution)/shard_map/ppermute | solution.py:40
  27.4 5.5 %collective-permute-done.7.refs_10_ = bf16[4,128,512]{2,1,0:T(8,128)(2,1)S(1)} collective-permute-done((bf16[4,128,512]{2,1,0:T(8,128)(2,1)S(1)}, bf16[4,128,512]{2,1,0:T(8,128)(2,1)S(1)}, u32[]{:S(2)}, u32[]{:S(2)}) %collective-permute-start.7) | collective-permute-done | bytes 524320 | tf_op jit(solution)/shard_map/ppermute | solution.py:40
  35.6 8.2 %collective-permute-start.3 = (bf16[512,512]{1,0:T(8,128)(2,1)S(1)}, bf16[512,512]{1,0:T(8,128)(2,1)S(1)}, u32[]{:S(2)}, u32[]{:S(2)}) collective-permute-start(bf16[512,512]{1,0:T(8,128)(2,1)S(1)} %fusion.refs_1_), channel_id=1, source_target_pairs={{0,1},{8,9},{128,129},{136,137},{256,257},{264,265},{384,385},{392... | collective-permute-start | bytes 1572872 | tf_op jit(solution)/shard_map/ppermute | solution.py:40
  43.8 3.5 %collective-permute-start.13 = (bf16[4,128,512]{2,1,0:T(8,128)(2,1)}, bf16[4,128,512]{2,1,0:T(8,128)(2,1)}, u32[]{:S(2)}, u32[]{:S(2)}) collective-permute-start(bf16[4,128,512]{2,1,0:T(8,128)(2,1)} %collective-permute-done.12.refs_10_), channel_id=1, source_target_pairs={{0,16},{8,120},{128,144},{136,248},{256,272},{264,376},{384,400},{... | collective-permute-start | bytes 1572872 | tf_op jit(solution)/shard_map/ppermute | solution.py:40
  47.3 3.8 %collective-permute-start.9 = (bf16[4,128,512]{2,1,0:T(8,128)(2,1)}, bf16[4,128,512]{2,1,0:T(8,128)(2,1)}, u32[]{:S(2)}, u32[]{:S(2)}) collective-permute-start(bf16[4,128,512]{2,1,0:T(8,128)(2,1)} %collective-permute-done.8.refs_11_), channel_id=1, source_target_pairs={{0,16},{8,120},{128,144},{136,248},{256,272},{264,376},{384,400},{... | collective-permute-start | bytes 1572872 | tf_op jit(solution)/shard_map/ppermute | solution.py:40
  51.1 3.4 %collective-permute-start = (bf16[512,512]{1,0:T(8,128)(2,1)S(1)}, bf16[512,512]{1,0:T(8,128)(2,1)S(1)}, u32[]{:S(2)}, u32[]{:S(2)}) collective-permute-start(bf16[512,512]{1,0:T(8,128)(2,1)S(1)} %fusion.refs_1_), channel_id=1, source_target_pairs={{0,2},{8,14},{128,130},{136,142},{256,258},{264,270},{384,386},{39... | collective-permute-start | bytes 1572872 | tf_op jit(solution)/shard_map/ppermute | solution.py:40
  54.5 12.2 %collective-permute-done.3.refs_5_ = bf16[512,512]{1,0:T(8,128)(2,1)S(1)} collective-permute-done((bf16[512,512]{1,0:T(8,128)(2,1)S(1)}, bf16[512,512]{1,0:T(8,128)(2,1)S(1)}, u32[]{:S(2)}, u32[]{:S(2)}) %collective-permute-start.3) | collective-permute-done | bytes 524320 | tf_op jit(solution)/shard_map/ppermute | solution.py:40
  66.7 3.4 %collective-permute-start.4 = (bf16[512,512]{1,0:T(8,128)(2,1)S(1)}, bf16[512,512]{1,0:T(8,128)(2,1)S(1)}, u32[]{:S(2)}, u32[]{:S(2)}) collective-permute-start(bf16[512,512]{1,0:T(8,128)(2,1)S(1)} %collective-permute-done.3.refs_5_), channel_id=1, source_target_pairs={{0,2},{8,14},{128,130},{136,142},{256,258},{264,270},{384,386},{39... | collective-permute-start | bytes 1572872 | tf_op jit(solution)/shard_map/ppermute | solution.py:40
  70.1 3.3 %collective-permute-start.14 = (bf16[4,128,512]{2,1,0:T(8,128)(2,1)}, bf16[4,128,512]{2,1,0:T(8,128)(2,1)S(1)}, u32[]{:S(2)}, u32[]{:S(2)}) collective-permute-start(bf16[4,128,512]{2,1,0:T(8,128)(2,1)} %collective-permute-done.13.refs_11_), channel_id=1, source_target_pairs={{0,16},{8,120},{128,144},{136,248},{256,272},{264,376},{384,400},{... | collective-permute-start | bytes 1572872 | tf_op jit(solution)/shard_map/ppermute | solution.py:40
  76.9 8.6 %collective-permute-done.10.refs_13_ = bf16[2,128,512]{2,1,0:T(8,128)(2,1)S(1)} collective-permute-done((bf16[2,128,512]{2,1,0:T(8,128)(2,1)S(1)}, bf16[2,128,512]{2,1,0:T(8,128)(2,1)S(1)}, u32[]{:S(2)}, u32[]{:S(2)}) %collective-permute-start.10) | collective-permute-done | bytes 262176 | tf_op jit(solution)/shard_map/ppermute | solution.py:40
  90.2 3.3 %collective-permute-start.1 = (bf16[512,512]{1,0:T(8,128)(2,1)S(1)}, bf16[512,512]{1,0:T(8,128)(2,1)}, u32[]{:S(2)}, u32[]{:S(2)}) collective-permute-start(bf16[512,512]{1,0:T(8,128)(2,1)S(1)} %collective-permute-done.refs_2_), channel_id=1, source_target_pairs={{0,2},{8,14},{128,130},{136,142},{256,258},{264,270},{384,386},{39... | collective-permute-start | bytes 1572872 | tf_op jit(solution)/shard_map/ppermute | solution.py:40
  101.0 4.0 %collective-permute-start.16 = (bf16[8,128,512]{2,1,0:T(8,128)(2,1)}, bf16[8,128,512]{2,1,0:T(8,128)(2,1)}, u32[]{:S(2)}, u32[]{:S(2)}) collective-permute-start(bf16[8,128,512]{2,1,0:T(8,128)(2,1)} %pad_maximum_fusion.1), channel_id=1, source_target_pairs={{0,8},{8,0},{128,136},{136,128},{256,264},{264,256},{384,392},{392... | collective-permute-start | bytes 3145736 | tf_op jit(solution)/shard_map/ppermute | solution.py:40
  111.4 3.5 %collective-permute-start.6 = (bf16[512,512]{1,0:T(8,128)(2,1)}, bf16[512,512]{1,0:T(8,128)(2,1)}, u32[]{:S(2)}, u32[]{:S(2)}) collective-permute-start(bf16[512,512]{1,0:T(8,128)(2,1)} %collective-permute-done.5.refs_7_), channel_id=1, source_target_pairs={{0,2},{8,14},{128,130},{136,142},{256,258},{264,270},{384,386},{39... | collective-permute-start | bytes 1572872 | tf_op jit(solution)/shard_map/ppermute | solution.py:40
  115.1 6.5 %collective-permute-done.2.refs_4_ = bf16[512,512]{1,0:T(8,128)(2,1)} collective-permute-done((bf16[512,512]{1,0:T(8,128)(2,1)}, bf16[512,512]{1,0:T(8,128)(2,1)}, u32[]{:S(2)}, u32[]{:S(2)}) %collective-permute-start.2) | collective-permute-done | bytes 524320 | tf_op jit(solution)/shard_map/ppermute | solution.py:40
  121.6 5.6 %collective-permute-done.6.refs_8_ = bf16[512,512]{1,0:T(8,128)(2,1)} collective-permute-done((bf16[512,512]{1,0:T(8,128)(2,1)}, bf16[512,512]{1,0:T(8,128)(2,1)}, u32[]{:S(2)}, u32[]{:S(2)}) %collective-permute-start.6) | collective-permute-done | bytes 524320 | tf_op jit(solution)/shard_map/ppermute | solution.py:40
  129.2 5.7 %project.3.own = bf16[512,512]{1,0:T(8,128)(2,1)} custom-call(s32[5]{0:T(128)S(1)} %stack.23.refs_0_, bf16[512,512]{1,0:T(8,128)(2,1)S(1)} %fusion.refs_1_, bf16[512,512]{1,0:T(8,128)(2,1)S(1)} %collective-permute-done.refs_2_, bf16[512,512]{1,0:T(8,128)(2,1)} %collective-permute-done.1.refs_3_, bf16[512,512]{1,0:T(8,128)(2,1)} %collective-permute-done.2.refs_4_, ...), custom_call_target="tpu_custom_call" | custom-call | flops 2147483648 | bytes 8912896 | tf_op jit(solution)/shard_map/project/pallas_call | solution.py:86
  139.9 4.9 %project.2.q_ref = bf16[512,512]{1,0:T(8,128)(2,1)S(1)} custom-call(s32[5]{0:T(128)S(1)} %stack.23.refs_0_, bf16[512,512]{1,0:T(8,128)(2,1)S(1)} %fusion.refs_1_, bf16[512,512]{1,0:T(8,128)(2,1)S(1)} %collective-permute-done.refs_2_, bf16[512,512]{1,0:T(8,128)(2,1)} %collective-permute-done.1.refs_3_, bf16[512,512]{1,0:T(8,128)(2,1)} %collective-permute-done.2.refs_4_, ...), custom_call_target="tpu_custom_call" | custom-call | flops 2147483648 | bytes 8912896 | tf_op jit(solution)/shard_map/project/pallas_call | solution.py:86
  144.8 6.2 %collective-permute-done.18.e1 = bf16[512,512]{1,0:T(8,128)(2,1)} collective-permute-done((bf16[512,512]{1,0:T(8,128)(2,1)}, bf16[512,512]{1,0:T(8,128)(2,1)}, u32[]{:S(2)}, u32[]{:S(2)}) %collective-permute-start.18) | collective-permute-done | bytes 524320 | tf_op jit(solution)/shard_map/ppermute | solution.py:46
  151.0 5.0 %collective-permute-done.19.e2 = bf16[512,512]{1,0:T(8,128)(2,1)} collective-permute-done((bf16[512,512]{1,0:T(8,128)(2,1)}, bf16[512,512]{1,0:T(8,128)(2,1)}, u32[]{:S(2)}, u32[]{:S(2)}) %collective-permute-start.19) | collective-permute-done | bytes 524320 | tf_op jit(solution)/shard_map/ppermute | solution.py:46
  156.0 8.4 %scores.1 = (bf16[4,1280,256]{2,1,0:T(8,128)(2,1)}, f32[512,256]{1,0:T(8,128)S(1)}, bf16[512,256]{1,0:T(8,128)(2,1)S(1)}, bf16[512,256]{1,0:T(8,128)(2,1)S(1)}) custom-call(s32[1]{0:T(128)} %bitcast.lead, s32[1,32]{1,0:T(1,128)S(1)} %bitcast.18, bf16[512,512]{1,0:T(8,128)(2,1)S(1)} %project.2.q_ref, bf16[512,512]{1,0:T(8,128)(2,1)} %project.3.own, ...), custom_call_target="tpu_custom_call" | custom-call | flops 2013265920 | bytes 5242880 | tf_op jit(solution)/shard_map/scores/pallas_call | solution.py:205
  164.4 4.3 %collective-permute-start.21 = (bf16[512,256]{1,0:T(8,128)(2,1)S(1)}, bf16[512,256]{1,0:T(8,128)(2,1)S(1)}, u32[]{:S(2)}, u32[]{:S(2)}) collective-permute-start(bf16[512,256]{1,0:T(8,128)(2,1)S(1)} %get-tuple-element.9), channel_id=1, source_target_pairs={{8,0},{16,8},{24,16},{32,24},{40,32},{48,40},{56,48},{64,56},{72,6... | collective-permute-start | bytes 786440 | tf_op jit(solution)/shard_map/ppermute | solution.py:46
  175.4 5.4 %collective-permute-done.20 = bf16[512,256]{1,0:T(8,128)(2,1)S(1)} collective-permute-done((bf16[512,256]{1,0:T(8,128)(2,1)S(1)}, bf16[512,256]{1,0:T(8,128)(2,1)S(1)}, u32[]{:S(2)}, u32[]{:S(2)}) %collective-permute-start.20) | collective-permute-done | bytes 262176 | tf_op jit(solution)/shard_map/ppermute | solution.py:46
  (58 shorter events, 40.1 us)
Async XLA Ops:
  0.6 34.3 %copy-start = (bf16[512,480]{0,1:T(8,128)(2,1)S(1)}, bf16[512,480]{0,1:T(8,128)(2,1)}, u32[]{:S(2)}) copy-start(bf16[512,480]{0,1:T(8,128)(2,1)} %param.6) | copy-start | bytes 1474564
  20.6 30.5 %copy-start.4 = (bf16[8,64,512]{2,1,0:T(8,128)(2,1)}, bf16[8,64,512]{2,1,0:T(8,128)(2,1)S(1)}, u32[]{:S(2)}) copy-start(bf16[8,64,512]{2,1,0:T(8,128)(2,1)S(1)} %get-tuple-element.10) | copy-start | bytes 1572868
  20.6 12.3 %collective-permute-start.7 = (bf16[4,128,512]{2,1,0:T(8,128)(2,1)S(1)}, bf16[4,128,512]{2,1,0:T(8,128)(2,1)S(1)}, u32[]{:S(2)}, u32[]{:S(2)}) collective-permute-start(bf16[4,128,512]{2,1,0:T(8,128)(2,1)S(1)} %bitcast.14), channel_id=1, source_target_pairs={{0,16},{8,120},{128,144},{136,248},{256,272},{264,376},{384,400},{... | collective-permute-start | bytes 1572872 | tf_op jit(solution)/shard_map/ppermute | solution.py:40
  23.9 19.9 %collective-permute-start.12 = (bf16[4,128,512]{2,1,0:T(8,128)(2,1)S(1)}, bf16[4,128,512]{2,1,0:T(8,128)(2,1)}, u32[]{:S(2)}, u32[]{:S(2)}) collective-permute-start(bf16[4,128,512]{2,1,0:T(8,128)(2,1)S(1)} %bitcast.16), channel_id=1, source_target_pairs={{0,16},{8,120},{128,144},{136,248},{256,272},{264,376},{384,400},{... | collective-permute-start | bytes 1572872 | tf_op jit(solution)/shard_map/ppermute | solution.py:40
  32.9 14.4 %collective-permute-start.8 = (bf16[4,128,512]{2,1,0:T(8,128)(2,1)S(1)}, bf16[4,128,512]{2,1,0:T(8,128)(2,1)}, u32[]{:S(2)}, u32[]{:S(2)}) collective-permute-start(bf16[4,128,512]{2,1,0:T(8,128)(2,1)S(1)} %collective-permute-done.7.refs_10_), channel_id=1, source_target_pairs={{0,16},{8,120},{128,144},{136,248},{256,272},{264,376},{384,400},{... | collective-permute-start | bytes 1572872 | tf_op jit(solution)/shard_map/ppermute | solution.py:40
  35.6 31.2 %collective-permute-start.3 = (bf16[512,512]{1,0:T(8,128)(2,1)S(1)}, bf16[512,512]{1,0:T(8,128)(2,1)S(1)}, u32[]{:S(2)}, u32[]{:S(2)}) collective-permute-start(bf16[512,512]{1,0:T(8,128)(2,1)S(1)} %fusion.refs_1_), channel_id=1, source_target_pairs={{0,1},{8,9},{128,129},{136,137},{256,257},{264,265},{384,385},{392... | collective-permute-start | bytes 1572872 | tf_op jit(solution)/shard_map/ppermute | solution.py:40
  43.8 26.3 %collective-permute-start.13 = (bf16[4,128,512]{2,1,0:T(8,128)(2,1)}, bf16[4,128,512]{2,1,0:T(8,128)(2,1)}, u32[]{:S(2)}, u32[]{:S(2)}) collective-permute-start(bf16[4,128,512]{2,1,0:T(8,128)(2,1)} %collective-permute-done.12.refs_10_), channel_id=1, source_target_pairs={{0,16},{8,120},{128,144},{136,248},{256,272},{264,376},{384,400},{... | collective-permute-start | bytes 1572872 | tf_op jit(solution)/shard_map/ppermute | solution.py:40
  47.3 26.1 %collective-permute-start.9 = (bf16[4,128,512]{2,1,0:T(8,128)(2,1)}, bf16[4,128,512]{2,1,0:T(8,128)(2,1)}, u32[]{:S(2)}, u32[]{:S(2)}) collective-permute-start(bf16[4,128,512]{2,1,0:T(8,128)(2,1)} %collective-permute-done.8.refs_11_), channel_id=1, source_target_pairs={{0,16},{8,120},{128,144},{136,248},{256,272},{264,376},{384,400},{... | collective-permute-start | bytes 1572872 | tf_op jit(solution)/shard_map/ppermute | solution.py:40
  51.1 39.0 %collective-permute-start = (bf16[512,512]{1,0:T(8,128)(2,1)S(1)}, bf16[512,512]{1,0:T(8,128)(2,1)S(1)}, u32[]{:S(2)}, u32[]{:S(2)}) collective-permute-start(bf16[512,512]{1,0:T(8,128)(2,1)S(1)} %fusion.refs_1_), channel_id=1, source_target_pairs={{0,2},{8,14},{128,130},{136,142},{256,258},{264,270},{384,386},{39... | collective-permute-start | bytes 1572872 | tf_op jit(solution)/shard_map/ppermute | solution.py:40
  66.7 26.7 %collective-permute-start.4 = (bf16[512,512]{1,0:T(8,128)(2,1)S(1)}, bf16[512,512]{1,0:T(8,128)(2,1)S(1)}, u32[]{:S(2)}, u32[]{:S(2)}) collective-permute-start(bf16[512,512]{1,0:T(8,128)(2,1)S(1)} %collective-permute-done.3.refs_5_), channel_id=1, source_target_pairs={{0,2},{8,14},{128,130},{136,142},{256,258},{264,270},{384,386},{39... | collective-permute-start | bytes 1572872 | tf_op jit(solution)/shard_map/ppermute | solution.py:40
  70.1 26.4 %collective-permute-start.14 = (bf16[4,128,512]{2,1,0:T(8,128)(2,1)}, bf16[4,128,512]{2,1,0:T(8,128)(2,1)S(1)}, u32[]{:S(2)}, u32[]{:S(2)}) collective-permute-start(bf16[4,128,512]{2,1,0:T(8,128)(2,1)} %collective-permute-done.13.refs_11_), channel_id=1, source_target_pairs={{0,16},{8,120},{128,144},{136,248},{256,272},{264,376},{384,400},{... | collective-permute-start | bytes 1572872 | tf_op jit(solution)/shard_map/ppermute | solution.py:40
  74.4 11.0 %collective-permute-start.10 = (bf16[2,128,512]{2,1,0:T(8,128)(2,1)S(1)}, bf16[2,128,512]{2,1,0:T(8,128)(2,1)S(1)}, u32[]{:S(2)}, u32[]{:S(2)}) collective-permute-start(bf16[2,128,512]{2,1,0:T(8,128)(2,1)S(1)} %constant_dynamic-slice_fusion.1), channel_id=1, source_target_pairs={{0,16},{8,120},{128,144},{136,248},{256,272},{264,376},{384,400},{... | collective-permute-start | bytes 786440 | tf_op jit(solution)/shard_map/ppermute | solution.py:40
  88.1 50.7 %collective-permute-start.11 = (bf16[14,128,512]{2,1,0:T(8,128)(2,1)}, bf16[14,128,512]{2,1,0:T(8,128)(2,1)}, u32[]{:S(2)}, u32[]{:S(2)}) collective-permute-start(bf16[14,128,512]{2,1,0:T(8,128)(2,1)} %pad_maximum_fusion), channel_id=1, source_target_pairs={{0,8},{8,0},{128,136},{136,128},{256,264},{264,256},{384,392},{392... | collective-permute-start | bytes 5505032 | tf_op jit(solution)/shard_map/ppermute | solution.py:40
  90.2 18.9 %collective-permute-start.1 = (bf16[512,512]{1,0:T(8,128)(2,1)S(1)}, bf16[512,512]{1,0:T(8,128)(2,1)}, u32[]{:S(2)}, u32[]{:S(2)}) collective-permute-start(bf16[512,512]{1,0:T(8,128)(2,1)S(1)} %collective-permute-done.refs_2_), channel_id=1, source_target_pairs={{0,2},{8,14},{128,130},{136,142},{256,258},{264,270},{384,386},{39... | collective-permute-start | bytes 1572872 | tf_op jit(solution)/shard_map/ppermute | solution.py:40
  93.5 17.9 %collective-permute-start.5 = (bf16[512,512]{1,0:T(8,128)(2,1)S(1)}, bf16[512,512]{1,0:T(8,128)(2,1)}, u32[]{:S(2)}, u32[]{:S(2)}) collective-permute-start(bf16[512,512]{1,0:T(8,128)(2,1)S(1)} %collective-permute-done.4.refs_6_), channel_id=1, source_target_pairs={{0,2},{8,14},{128,130},{136,142},{256,258},{264,270},{384,386},{39... | collective-permute-start | bytes 1572872 | tf_op jit(solution)/shard_map/ppermute | solution.py:40
  96.6 9.5 %collective-permute-start.15 = (bf16[2,128,512]{2,1,0:T(8,128)(2,1)S(1)}, bf16[2,128,512]{2,1,0:T(8,128)(2,1)S(1)}, u32[]{:S(2)}, u32[]{:S(2)}) collective-permute-start(bf16[2,128,512]{2,1,0:T(8,128)(2,1)S(1)} %constant_dynamic-slice_fusion), channel_id=1, source_target_pairs={{0,16},{8,120},{128,144},{136,248},{256,272},{264,376},{384,400},{... | collective-permute-start | bytes 786440 | tf_op jit(solution)/shard_map/ppermute | solution.py:40
  101.0 26.2 %collective-permute-start.16 = (bf16[8,128,512]{2,1,0:T(8,128)(2,1)}, bf16[8,128,512]{2,1,0:T(8,128)(2,1)}, u32[]{:S(2)}, u32[]{:S(2)}) collective-permute-start(bf16[8,128,512]{2,1,0:T(8,128)(2,1)} %pad_maximum_fusion.1), channel_id=1, source_target_pairs={{0,8},{8,0},{128,136},{136,128},{256,264},{264,256},{384,392},{392... | collective-permute-start | bytes 3145736 | tf_op jit(solution)/shard_map/ppermute | solution.py:40
  107.1 20.2 %collective-permute-start.17 = (bf16[6,128,512]{2,1,0:T(8,128)(2,1)}, bf16[6,128,512]{2,1,0:T(8,128)(2,1)}, u32[]{:S(2)}, u32[]{:S(2)}) collective-permute-start(bf16[6,128,512]{2,1,0:T(8,128)(2,1)} %pad_maximum_fusion.2), channel_id=1, source_target_pairs={{0,8},{8,0},{128,136},{136,128},{256,264},{264,256},{384,392},{392... | collective-permute-start | bytes 2359304 | tf_op jit(solution)/shard_map/ppermute | solution.py:40
  109.0 12.6 %collective-permute-start.2 = (bf16[512,512]{1,0:T(8,128)(2,1)}, bf16[512,512]{1,0:T(8,128)(2,1)}, u32[]{:S(2)}, u32[]{:S(2)}) collective-permute-start(bf16[512,512]{1,0:T(8,128)(2,1)} %collective-permute-done.1.refs_3_), channel_id=1, source_target_pairs={{0,2},{8,14},{128,130},{136,142},{256,258},{264,270},{384,386},{39... | collective-permute-start | bytes 1572872 | tf_op jit(solution)/shard_map/ppermute | solution.py:40
  111.4 15.8 %collective-permute-start.6 = (bf16[512,512]{1,0:T(8,128)(2,1)}, bf16[512,512]{1,0:T(8,128)(2,1)}, u32[]{:S(2)}, u32[]{:S(2)}) collective-permute-start(bf16[512,512]{1,0:T(8,128)(2,1)} %collective-permute-done.5.refs_7_), channel_id=1, source_target_pairs={{0,2},{8,14},{128,130},{136,142},{256,258},{264,270},{384,386},{39... | collective-permute-start | bytes 1572872 | tf_op jit(solution)/shard_map/ppermute | solution.py:40
  135.0 16.0 %collective-permute-start.18 = (bf16[512,512]{1,0:T(8,128)(2,1)}, bf16[512,512]{1,0:T(8,128)(2,1)}, u32[]{:S(2)}, u32[]{:S(2)}) collective-permute-start(bf16[512,512]{1,0:T(8,128)(2,1)} %project.3.own), channel_id=1, source_target_pairs={{0,8},{8,16},{16,24},{24,32},{32,40},{40,48},{48,56},{56,64},{64,7... | collective-permute-start | bytes 1572872 | tf_op jit(solution)/shard_map/ppermute | solution.py:46
  136.9 19.1 %collective-permute-start.19 = (bf16[512,512]{1,0:T(8,128)(2,1)}, bf16[512,512]{1,0:T(8,128)(2,1)}, u32[]{:S(2)}, u32[]{:S(2)}) collective-permute-start(bf16[512,512]{1,0:T(8,128)(2,1)} %project.3.own), channel_id=1, source_target_pairs={{0,16},{8,24},{16,32},{24,40},{32,48},{40,56},{48,64},{56,72},{64,... | collective-permute-start | bytes 1572872 | tf_op jit(solution)/shard_map/ppermute | solution.py:46
  164.4 11.0 %collective-permute-start.21 = (bf16[512,256]{1,0:T(8,128)(2,1)S(1)}, bf16[512,256]{1,0:T(8,128)(2,1)S(1)}, u32[]{:S(2)}, u32[]{:S(2)}) collective-permute-start(bf16[512,256]{1,0:T(8,128)(2,1)S(1)} %get-tuple-element.9), channel_id=1, source_target_pairs={{8,0},{16,8},{24,16},{32,24},{40,32},{48,40},{56,48},{64,56},{72,6... | collective-permute-start | bytes 786440 | tf_op jit(solution)/shard_map/ppermute | solution.py:46
  168.7 12.1 %collective-permute-start.20 = (bf16[512,256]{1,0:T(8,128)(2,1)S(1)}, bf16[512,256]{1,0:T(8,128)(2,1)S(1)}, u32[]{:S(2)}, u32[]{:S(2)}) collective-permute-start(bf16[512,256]{1,0:T(8,128)(2,1)S(1)} %get-tuple-element.8), channel_id=1, source_target_pairs={{16,0},{24,8},{32,16},{40,24},{48,32},{56,40},{64,48},{72,56},{80,... | collective-permute-start | bytes 786440 | tf_op jit(solution)/shard_map/ppermute | solution.py:46
  (9 other events, 79.5 us)
where the time goes:
time: 183 us; the launch traced here: 182 us
  starting transfers between devices  69 us (38%)
  waiting for transfers between devices  56.3 us (31%)
  Pallas kernels  22.1 us (12%)
  blocking collectives  18.9 us (10%)
  other arithmetic  7.65 us (4%)
  local copies, waits for them, and re-layouts  6 us (3%)
    ppermute x18, starting transfers between devices, hop(): return lax.ppermute(block, BOTH, route)  59 us
    ppermute x18, waiting for transfers between devices, hop(): return lax.ppermute(block, BOTH, route)  39.6 us
    all_gather x1, blocking collectives, gather_zcore(): lax.all_gather(w, 'ctx', axis=0, tiled=False, axis_index_groups=groups)  18.9 us
    ppermute x4, waiting for transfers between devices, along_ctx(): return lax.ppermute(block, 'ctx', route)  16.7 us
    pallas_call x2, Pallas kernels, project(): pl.pallas_call(lambda *refs: project_body(*refs, scale=scale, swaps=swaps...  10.6 us
    ppermute x4, starting transfers between devices, along_ctx(): return lax.ppermute(block, 'ctx', route)  10 us
    pallas_call x1, Pallas kernels, attend(): pl.pallas_call(scores_body, out_shape=(shape((4, REACH, TILE), BF), shape...  8.41 us
    unnamed x22, local copies, waits for them, and re-layouts  4.8 us
  transfers between devices with their start and end apart: 22, of which 9 were waited for; matrix products, arithmetic and copies ran while one was open for 4% of the time, Pallas kernels for 8%

commit v1 on v0

--- a/solution.py
+++ b/solution.py
@@ -16,6 +16,7 @@
 BOTH = ("ctx", "head")
 BF = jnp.bfloat16
 F32 = jnp.float32
+MIB = 1024 * 1024
 
 
 def place(x, y, z, core):
@@ -46,20 +47,12 @@
     return lax.ppermute(block, "ctx", route)
 
 
-def project_body(pos, t0, t1, t2, t3, p0, p1, p2, p3, *refs, scale, swaps):
-    *blocks, o_ref = refs
-    own_ref, r1, r2, r3, r4 = blocks[:5]
-    swapped = blocks[5:]
-    x, y, zh, sign, core = pos[0], pos[1], pos[2], pos[3], pos[4]
+def project_body(pos, t0, t1, t2, t3, p0, p1, p2, p3, own_ref, r1, r2, r3, r4, swapped, o_ref, *, scale):
+    x, y, zh, sign = pos[0], pos[1], pos[2], pos[3]
     total = jnp.zeros(o_ref.shape, F32)
-
-    def back(step, z):
-        ref, at = swaps[step - 1]
-        return swapped[ref][at + z]
 
     for slot, (near, far) in enumerate(((t0, p0), (t1, p1), (t2, p2), (t3, p3))):
         z = lax.rem(x - sign * slot + NX, NX)
-        half = lax.rem(z, 2)
 
         def columns(distance):
             chip = lax.rem(y + sign * distance + NY, NY)
@@ -67,9 +60,9 @@
             return jnp.where(lax.div(chip, 4) == zh, near[:, pl.ds(at, PAIR)], far[:, pl.ds(at, PAIR)])
 
         left = [columns(d) for d in (0, 4, -1, 1, -2, 2, -3, 3)]
-        right = [own_ref[z], jnp.where(lax.div(z, 2) == core, r4[half], back(4, half))]
-        for step, ref in ((1, r1), (2, r2), (3, r3)):
-            right += [ref[z], back(step, z)]
+        right = [own_ref[z], r4[z]]
+        for step, ref in enumerate((r1, r2, r3)):
+            right += [ref[z], swapped[NZL * step + z]]
         total += jnp.dot(
             jnp.concatenate(left, axis=1),
             jnp.concatenate(right, axis=0),
@@ -78,13 +71,13 @@
     o_ref[...] = (total * scale).astype(BF)
 
 
-def project(pos, near, far, ring, swapped, swaps, scale):
+def project(pos, near, far, ring, swapped, scale):
     rows = near[0].shape[0]
     cols = ring[0].shape[-1]
     full = pl.BlockSpec(memory_space=pltpu.VMEM)
-    operands = [*near, *far, *ring, *swapped]
+    operands = [*near, *far, *ring, swapped]
     return pl.pallas_call(
-        lambda *refs: project_body(*refs, scale=scale, swaps=swaps),
+        lambda *refs: project_body(*refs, scale=scale),
         out_shape=jax.ShapeDtypeStruct((rows, cols), BF),
         in_specs=[pl.BlockSpec(memory_space=pltpu.SMEM)] + [full] * len(operands),
         out_specs=full,
@@ -93,17 +86,15 @@
             bytes_accessed=2 * (rows * 4096 + cols * 4096 + rows * cols),
             transcendentals=0,
         ),
-        compiler_params=pltpu.CompilerParams(vmem_limit_bytes=48 * 1024 * 1024),
+        compiler_params=pltpu.CompilerParams(vmem_limit_bytes=26 * MIB),
         name="project",
     )(pos, *operands)
 
 
-def ring_y(block, core):
+def ring_y(block):
     out = [block]
-    for _ in range(3):
+    for _ in range(4):
         out.append(hop(out[-1], dy=1, by_core=True))
-    half = lax.dynamic_slice_in_dim(out[-1], 2 * core, 2, 0)
-    out.append(hop(half, dy=1, by_core=True))
     return out
 
 
@@ -112,6 +103,10 @@
     for _ in range(3):
         out.append(hop(out[-1], dx=1, by_core=True))
     return out
+
+
+def joined_blocks(blocks):
+    return jnp.concatenate(blocks, axis=0)
 
 
 def gather_zcore(w):
@@ -221,7 +216,7 @@
         cost_estimate=pl.CostEstimate(
             flops=6 * pairs * HEAD_SIZE, bytes_accessed=5 * rows * 1024 + 2 * pairs, transcendentals=pairs
         ),
-        compiler_params=pltpu.CompilerParams(vmem_limit_bytes=48 * 1024 * 1024),
+        compiler_params=pltpu.CompilerParams(vmem_limit_bytes=16 * MIB),
         name="scores",
     )(lead, lens, query, own, e1, e2, grad)
     out = pl.pallas_call(
@@ -232,7 +227,7 @@
         cost_estimate=pl.CostEstimate(
             flops=2 * pairs * HEAD_SIZE, bytes_accessed=4 * rows * 1024 + 2 * pairs, transcendentals=0
         ),
-        compiler_params=pltpu.CompilerParams(vmem_limit_bytes=48 * 1024 * 1024),
+        compiler_params=pltpu.CompilerParams(vmem_limit_bytes=14 * MIB),
         name="values",
     )(p, own, e1, e2)
     return out, dk0, dk1, dk2
@@ -244,7 +239,7 @@
     head = lax.axis_index("head").astype(jnp.int32)
     core, y = ctx % 2, (ctx // 2) % NY
     x, zh = head // NZH, head % NZH
-    pos = jnp.stack([x, y, zh, 1 - 2 * core, core])
+    pos = jnp.stack([x, y, zh, 1 - 2 * core])
 
     feature = jnp.arange(tokens.shape[1], dtype=jnp.int32)
     target = feature // ROWS * PAD + feature % ROWS
@@ -253,19 +248,18 @@
 
     partner = hop(own, dz=NZL)
     near = ring_x(own)
-    far = ring_x(partner)
+    far = [partner] + [hop(partner, dx=d, by_core=True) for d in (1, 2, 3)]
 
     w = gather_zcore(jnp.concatenate([key_matrix, value_matrix, w_query], axis=1))
     w = jnp.pad(w, ((0, 0), (0, PAD - ROWS), (0, 0)))
     kv_cols = 2 * HEAD_SIZE
-    kv = ring_y(w[:, :, :kv_cols].reshape(NZL, PAIR, kv_cols), core)
-    kv_a = hop(jnp.concatenate(kv[1:3], axis=0), swap=1)
-    kv_b = hop(jnp.concatenate(kv[3:], axis=0), swap=1)
-    qs = ring_y(w[:, :, kv_cols:].reshape(NZL, PAIR, -1), core)
-    q_a = hop(jnp.concatenate(qs[1:], axis=0), swap=1)
-
-    joined = project(pos, near, far, kv, [kv_a, kv_b], ((0, 0), (0, 4), (1, 0), (1, 4)), 1.0)
-    query = project(pos, near, far, qs, [q_a], ((0, 0), (0, 4), (0, 8), (0, 12)), 0.0625)
+    kv = ring_y(w[:, :, :kv_cols].reshape(NZL, PAIR, kv_cols))
+    kv_a = hop(joined_blocks(kv[1:4]), swap=1)
+    qs = ring_y(w[:, :, kv_cols:].reshape(NZL, PAIR, -1))
+    q_a = hop(joined_blocks(qs[1:4]), swap=1)
+
+    joined = project(pos, near, far, kv, kv_a, 1.0)
+    query = project(pos, near, far, qs, q_a, 0.0625)
 
     e2 = along_ctx(joined, 2)
     e1 = along_ctx(joined, 1)

time: 183 us -> 183 us (level)
  waiting for transfers between devices: 56.3 us -> 66.6 us
  starting transfers between devices: 69 us -> 61.6 us
  other arithmetic: 7.65 us -> 5.53 us
    ppermute x18 -> x17, waiting for transfers between devices: 39.6 us -> 51 us  [hop(): return lax.ppermute(block, BOTH, route)]
    ppermute x18 -> x17, starting transfers between devices: 59 us -> 51.6 us  [hop(): return lax.ppermute(block, BOTH, route)]
    unnamed x22 -> x34, local copies, waits for them, and re-layouts: 4.8 us -> 7.33 us
    concatenate x3 -> x2, other arithmetic: 5.93 us -> 3.75 us  [joined_blocks(): return jnp.concatenate(blocks, axis=0)]
  transfers between devices with their start and end apart: 22 -> 21, of which waited for: 9 -> 10; matrix products, arithmetic and copies ran while one was open for 4% -> 2% of each run, Pallas kernels for 8% -> 7%
where the time goes in v1:
time: 183 us; the launch traced here: 182 us
  waiting for transfers between devices  66.6 us (36%)
  starting transfers between devices  61.6 us (34%)
  Pallas kernels  20.4 us (11%)
  blocking collectives  18.9 us (10%)
  local copies, waits for them, and re-layouts  7.45 us (4%)
  other arithmetic  5.53 us (3%)
    ppermute x17, starting transfers between devices, hop(): return lax.ppermute(block, BOTH, route)  51.6 us
    ppermute x17, waiting for transfers between devices, hop(): return lax.ppermute(block, BOTH, route)  51 us
    all_gather x1, blocking collectives, gather_zcore(): lax.all_gather(w, 'ctx', axis=0, tiled=False, axis_index_groups=groups)  18.9 us
    ppermute x4, waiting for transfers between devices, along_ctx(): return lax.ppermute(block, 'ctx', route)  15.6 us
    ppermute x4, starting transfers between devices, along_ctx(): return lax.ppermute(block, 'ctx', route)  10 us
    pallas_call x2, Pallas kernels, project(): pl.pallas_call(lambda *refs: project_body(*refs, scale=scale), out_shape=...  9.87 us
    pallas_call x1, Pallas kernels, attend(): pl.pallas_call(scores_body, out_shape=(shape((4, REACH, TILE), BF), shape...  7.52 us
    unnamed x34, local copies, waits for them, and re-layouts  7.33 us
  transfers between devices with their start and end apart: 21, of which 10 were waited for; matrix products, arithmetic and copies ran while one was open for 2% of the time, Pallas kernels for 7%

profile of v1, /device:TPU:64, one launch (start us, length us, event | category | flops | bytes accessed | tf_op | source)
XLA Modules:
  0.0 182.3 jit_solution(990040921642818957)
XLA Ops:
  1.6 18.9 %all-gather.1 = bf16[8,60,1024]{2,1,0:T(8,128)(2,1)S(1)} all-gather(bf16[1,60,1024]{2,1,0:T(8,128)(2,1)S(1)} %maximum_bitcast_fusion), channel_id=2, replica_groups={{0,8,128,136,256,264,384,392},{16,24,144,152,272,280,400,408},{32,40,16..., dimensions={0}, use_global_device_ids=true | all-gather | bytes 1105920 | tf_op jit(solution)/shard_map/all_gather | solution.py:116
  20.6 3.3 %collective-permute-start.12 = (bf16[4,128,512]{2,1,0:T(8,128)(2,1)S(1)}, bf16[4,128,512]{2,1,0:T(8,128)(2,1)S(1)}, u32[]{:S(2)}, u32[]{:S(2)}) collective-permute-start(bf16[4,128,512]{2,1,0:T(8,128)(2,1)S(1)} %bitcast.15), channel_id=1, source_target_pairs={{0,16},{8,120},{128,144},{136,248},{256,272},{264,376},{384,400},{... | collective-permute-start | bytes 1572872 | tf_op jit(solution)/shard_map/ppermute | solution.py:41
  23.9 3.5 %collective-permute-start.7 = (bf16[4,128,512]{2,1,0:T(8,128)(2,1)S(1)}, bf16[4,128,512]{2,1,0:T(8,128)(2,1)S(1)}, u32[]{:S(2)}, u32[]{:S(2)}) collective-permute-start(bf16[4,128,512]{2,1,0:T(8,128)(2,1)S(1)} %bitcast.13), channel_id=1, source_target_pairs={{0,16},{8,120},{128,144},{136,248},{256,272},{264,376},{384,400},{... | collective-permute-start | bytes 1572872 | tf_op jit(solution)/shard_map/ppermute | solution.py:41
  27.4 5.5 %collective-permute-done.12.refs_10_ = bf16[4,128,512]{2,1,0:T(8,128)(2,1)S(1)} collective-permute-done((bf16[4,128,512]{2,1,0:T(8,128)(2,1)S(1)}, bf16[4,128,512]{2,1,0:T(8,128)(2,1)S(1)}, u32[]{:S(2)}, u32[]{:S(2)}) %collective-permute-start.12) | collective-permute-done | bytes 524320 | tf_op jit(solution)/shard_map/ppermute | solution.py:41
  35.0 3.6 %collective-permute-done.7.refs_10_ = bf16[4,128,512]{2,1,0:T(8,128)(2,1)S(1)} collective-permute-done((bf16[4,128,512]{2,1,0:T(8,128)(2,1)S(1)}, bf16[4,128,512]{2,1,0:T(8,128)(2,1)S(1)}, u32[]{:S(2)}, u32[]{:S(2)}) %collective-permute-start.7) | collective-permute-done | bytes 524320 | tf_op jit(solution)/shard_map/ppermute | solution.py:41
  40.6 4.6 %collective-permute-done.13.refs_11_ = bf16[4,128,512]{2,1,0:T(8,128)(2,1)S(1)} collective-permute-done((bf16[4,128,512]{2,1,0:T(8,128)(2,1)S(1)}, bf16[4,128,512]{2,1,0:T(8,128)(2,1)S(1)}, u32[]{:S(2)}, u32[]{:S(2)}) %collective-permute-start.13) | collective-permute-done | bytes 524320 | tf_op jit(solution)/shard_map/ppermute | solution.py:41
  47.7 8.2 %collective-permute-start.3 = (bf16[512,512]{1,0:T(8,128)(2,1)S(1)}, bf16[512,512]{1,0:T(8,128)(2,1)S(1)}, u32[]{:S(2)}, u32[]{:S(2)}) collective-permute-start(bf16[512,512]{1,0:T(8,128)(2,1)S(1)} %fusion.refs_1_), channel_id=1, source_target_pairs={{0,1},{8,9},{128,129},{136,137},{256,257},{264,265},{384,385},{392... | collective-permute-start | bytes 1572872 | tf_op jit(solution)/shard_map/ppermute | solution.py:41
  56.0 3.4 %collective-permute-start = (bf16[512,512]{1,0:T(8,128)(2,1)S(1)}, bf16[512,512]{1,0:T(8,128)(2,1)S(1)}, u32[]{:S(2)}, u32[]{:S(2)}) collective-permute-start(bf16[512,512]{1,0:T(8,128)(2,1)S(1)} %fusion.refs_1_), channel_id=1, source_target_pairs={{0,2},{8,14},{128,130},{136,142},{256,258},{264,270},{384,386},{39... | collective-permute-start | bytes 1572872 | tf_op jit(solution)/shard_map/ppermute | solution.py:41
  64.4 3.2 %collective-permute-start.16 = (bf16[12,128,512]{2,1,0:T(8,128)(2,1)}, bf16[12,128,512]{2,1,0:T(8,128)(2,1)}, u32[]{:S(2)}, u32[]{:S(2)}) collective-permute-start(bf16[12,128,512]{2,1,0:T(8,128)(2,1)} %pad_maximum_fusion.1), channel_id=1, source_target_pairs={{0,8},{8,0},{128,136},{136,128},{256,264},{264,256},{384,392},{392... | collective-permute-start | bytes 4718600 | tf_op jit(solution)/shard_map/ppermute | solution.py:41
  67.6 12.2 %collective-permute-done.3.refs_5_ = bf16[512,512]{1,0:T(8,128)(2,1)S(1)} collective-permute-done((bf16[512,512]{1,0:T(8,128)(2,1)S(1)}, bf16[512,512]{1,0:T(8,128)(2,1)S(1)}, u32[]{:S(2)}, u32[]{:S(2)}) %collective-permute-start.3) | collective-permute-done | bytes 524320 | tf_op jit(solution)/shard_map/ppermute | solution.py:41
  79.9 3.4 %collective-permute-start.4 = (bf16[512,512]{1,0:T(8,128)(2,1)S(1)}, bf16[512,512]{1,0:T(8,128)(2,1)S(1)}, u32[]{:S(2)}, u32[]{:S(2)}) collective-permute-start(bf16[512,512]{1,0:T(8,128)(2,1)S(1)} %collective-permute-done.3.refs_5_), channel_id=1, source_target_pairs={{0,2},{8,14},{128,130},{136,142},{256,258},{264,270},{384,386},{39... | collective-permute-start | bytes 1572872 | tf_op jit(solution)/shard_map/ppermute | solution.py:41
  83.3 4.6 %collective-permute-start.5 = (bf16[512,512]{1,0:T(8,128)(2,1)S(1)}, bf16[512,512]{1,0:T(8,128)(2,1)S(1)}, u32[]{:S(2)}, u32[]{:S(2)}) collective-permute-start(bf16[512,512]{1,0:T(8,128)(2,1)S(1)} %collective-permute-done.3.refs_5_), channel_id=1, source_target_pairs={{0,4},{8,12},{128,132},{136,140},{256,260},{264,268},{384,388},{39... | collective-permute-start | bytes 1572872 | tf_op jit(solution)/shard_map/ppermute | solution.py:41
  93.1 16.4 %collective-permute-done.1.refs_3_ = bf16[512,512]{1,0:T(8,128)(2,1)} collective-permute-done((bf16[512,512]{1,0:T(8,128)(2,1)S(1)}, bf16[512,512]{1,0:T(8,128)(2,1)}, u32[]{:S(2)}, u32[]{:S(2)}) %collective-permute-start.1) | collective-permute-done | bytes 524320 | tf_op jit(solution)/shard_map/ppermute | solution.py:41
  109.5 3.1 %collective-permute-start.6 = (bf16[512,512]{1,0:T(8,128)(2,1)S(1)}, bf16[512,512]{1,0:T(8,128)(2,1)}, u32[]{:S(2)}, u32[]{:S(2)}) collective-permute-start(bf16[512,512]{1,0:T(8,128)(2,1)S(1)} %collective-permute-done.3.refs_5_), channel_id=1, source_target_pairs={{0,6},{8,10},{128,134},{136,138},{256,262},{264,266},{384,390},{39... | collective-permute-start | bytes 1572872 | tf_op jit(solution)/shard_map/ppermute | solution.py:41
  112.6 2.7 %collective-permute-start.2 = (bf16[512,512]{1,0:T(8,128)(2,1)}, bf16[512,512]{1,0:T(8,128)(2,1)}, u32[]{:S(2)}, u32[]{:S(2)}) collective-permute-start(bf16[512,512]{1,0:T(8,128)(2,1)} %collective-permute-done.1.refs_3_), channel_id=1, source_target_pairs={{0,2},{8,14},{128,130},{136,142},{256,258},{264,270},{384,386},{39... | collective-permute-start | bytes 1572872 | tf_op jit(solution)/shard_map/ppermute | solution.py:41
  117.4 8.3 %collective-permute-done.6.refs_8_ = bf16[512,512]{1,0:T(8,128)(2,1)} collective-permute-done((bf16[512,512]{1,0:T(8,128)(2,1)S(1)}, bf16[512,512]{1,0:T(8,128)(2,1)}, u32[]{:S(2)}, u32[]{:S(2)}) %collective-permute-start.6) | collective-permute-done | bytes 524320 | tf_op jit(solution)/shard_map/ppermute | solution.py:41
  131.1 5.4 %project.3.own = bf16[512,512]{1,0:T(8,128)(2,1)} custom-call(s32[4]{0:T(128)S(1)} %pad_add_fusion.refs_0_, bf16[512,512]{1,0:T(8,128)(2,1)S(1)} %fusion.refs_1_, bf16[512,512]{1,0:T(8,128)(2,1)S(1)} %collective-permute-done.refs_2_, bf16[512,512]{1,0:T(8,128)(2,1)} %collective-permute-done.1.refs_3_, bf16[512,512]{1,0:T(8,128)(2,1)} %collective-permute-done.2.refs_4_, ...), custom_call_target="tpu_custom_call" | custom-call | flops 2147483648 | bytes 8912896 | tf_op jit(solution)/shard_map/project/pallas_call | solution.py:79
  144.5 4.5 %project.2.q_ref = bf16[512,512]{1,0:T(8,128)(2,1)S(1)} custom-call(s32[4]{0:T(128)S(1)} %pad_add_fusion.refs_0_, bf16[512,512]{1,0:T(8,128)(2,1)S(1)} %fusion.refs_1_, bf16[512,512]{1,0:T(8,128)(2,1)S(1)} %collective-permute-done.refs_2_, bf16[512,512]{1,0:T(8,128)(2,1)} %collective-permute-done.1.refs_3_, bf16[512,512]{1,0:T(8,128)(2,1)} %collective-permute-done.2.refs_4_, ...), custom_call_target="tpu_custom_call" | custom-call | flops 2147483648 | bytes 8912896 | tf_op jit(solution)/shard_map/project/pallas_call | solution.py:79
  149.0 3.5 %collective-permute-done.17.e1 = bf16[512,512]{1,0:T(8,128)(2,1)} collective-permute-done((bf16[512,512]{1,0:T(8,128)(2,1)}, bf16[512,512]{1,0:T(8,128)(2,1)}, u32[]{:S(2)}, u32[]{:S(2)}) %collective-permute-start.17) | collective-permute-done | bytes 524320 | tf_op jit(solution)/shard_map/ppermute | solution.py:47
  152.5 5.0 %collective-permute-done.18.e2 = bf16[512,512]{1,0:T(8,128)(2,1)} collective-permute-done((bf16[512,512]{1,0:T(8,128)(2,1)}, bf16[512,512]{1,0:T(8,128)(2,1)}, u32[]{:S(2)}, u32[]{:S(2)}) %collective-permute-start.18) | collective-permute-done | bytes 524320 | tf_op jit(solution)/shard_map/ppermute | solution.py:47
  157.5 7.5 %scores.1 = (bf16[4,1280,256]{2,1,0:T(8,128)(2,1)S(1)}, f32[512,256]{1,0:T(8,128)S(1)}, bf16[512,256]{1,0:T(8,128)(2,1)S(1)}, bf16[512,256]{1,0:T(8,128)(2,1)S(1)}) custom-call(s32[1]{0:T(128)} %bitcast.lead, s32[1,32]{1,0:T(1,128)S(1)} %bitcast.17, bf16[512,512]{1,0:T(8,128)(2,1)S(1)} %project.2.q_ref, bf16[512,512]{1,0:T(8,128)(2,1)} %project.3.own, ...), custom_call_target="tpu_custom_call" | custom-call | flops 2013265920 | bytes 5242880 | tf_op jit(solution)/shard_map/scores/pallas_call | solution.py:200
  165.0 4.3 %collective-permute-start.20 = (bf16[512,256]{1,0:T(8,128)(2,1)S(1)}, bf16[512,256]{1,0:T(8,128)(2,1)S(1)}, u32[]{:S(2)}, u32[]{:S(2)}) collective-permute-start(bf16[512,256]{1,0:T(8,128)(2,1)S(1)} %get-tuple-element.9), channel_id=1, source_target_pairs={{8,0},{16,8},{24,16},{32,24},{40,32},{48,40},{56,48},{64,56},{72,6... | collective-permute-start | bytes 786440 | tf_op jit(solution)/shard_map/ppermute | solution.py:47
  171.3 3.0 %values.1 = bf16[512,512]{1,0:T(8,128)(2,1)} custom-call(bf16[4,1280,256]{2,1,0:T(8,128)(2,1)S(1)} %get-tuple-element.6.p_ref, bf16[512,512]{1,0:T(8,128)(2,1)} %project.3.own, bf16[512,512]{1,0:T(8,128)(2,1)} %collective-permute-done.17.e1, bf16[512,512]{1,0:T(8,128)(2,1)} %collective-permute-done.18.e2), custom_call_target="tpu_custom_call" | custom-call | flops 671088640 | bytes 4718592 | tf_op jit(solution)/shard_map/values/pallas_call | solution.py:222
  174.3 7.1 %collective-permute-done.19 = bf16[512,256]{1,0:T(8,128)(2,1)S(1)} collective-permute-done((bf16[512,256]{1,0:T(8,128)(2,1)S(1)}, bf16[512,256]{1,0:T(8,128)(2,1)S(1)}, u32[]{:S(2)}, u32[]{:S(2)}) %collective-permute-start.19) | collective-permute-done | bytes 262176 | tf_op jit(solution)/shard_map/ppermute | solution.py:47
  (65 shorter events, 35.8 us)
Async XLA Ops:
  0.6 46.5 %copy-start = (bf16[512,480]{0,1:T(8,128)(2,1)S(1)}, bf16[512,480]{0,1:T(8,128)(2,1)}, u32[]{:S(2)}) copy-start(bf16[512,480]{0,1:T(8,128)(2,1)} %param.6) | copy-start | bytes 1474564
  20.6 38.8 %copy-start.7 = (bf16[8,64,512]{2,1,0:T(8,128)(2,1)}, bf16[8,64,512]{2,1,0:T(8,128)(2,1)S(1)}, u32[]{:S(2)}) copy-start(bf16[8,64,512]{2,1,0:T(8,128)(2,1)S(1)} %get-tuple-element.10) | copy-start | bytes 1572868
  20.6 12.3 %collective-permute-start.12 = (bf16[4,128,512]{2,1,0:T(8,128)(2,1)S(1)}, bf16[4,128,512]{2,1,0:T(8,128)(2,1)S(1)}, u32[]{:S(2)}, u32[]{:S(2)}) collective-permute-start(bf16[4,128,512]{2,1,0:T(8,128)(2,1)S(1)} %bitcast.15), channel_id=1, source_target_pairs={{0,16},{8,120},{128,144},{136,248},{256,272},{264,376},{384,400},{... | collective-permute-start | bytes 1572872 | tf_op jit(solution)/shard_map/ppermute | solution.py:41
  23.9 14.7 %collective-permute-start.7 = (bf16[4,128,512]{2,1,0:T(8,128)(2,1)S(1)}, bf16[4,128,512]{2,1,0:T(8,128)(2,1)S(1)}, u32[]{:S(2)}, u32[]{:S(2)}) collective-permute-start(bf16[4,128,512]{2,1,0:T(8,128)(2,1)S(1)} %bitcast.13), channel_id=1, source_target_pairs={{0,16},{8,120},{128,144},{136,248},{256,272},{264,376},{384,400},{... | collective-permute-start | bytes 1572872 | tf_op jit(solution)/shard_map/ppermute | solution.py:41
  32.9 12.3 %collective-permute-start.13 = (bf16[4,128,512]{2,1,0:T(8,128)(2,1)S(1)}, bf16[4,128,512]{2,1,0:T(8,128)(2,1)S(1)}, u32[]{:S(2)}, u32[]{:S(2)}) collective-permute-start(bf16[4,128,512]{2,1,0:T(8,128)(2,1)S(1)} %collective-permute-done.12.refs_10_), channel_id=1, source_target_pairs={{0,16},{8,120},{128,144},{136,248},{256,272},{264,376},{384,400},{... | collective-permute-start | bytes 1572872 | tf_op jit(solution)/shard_map/ppermute | solution.py:41
  38.6 51.3 %copy-start.3 = (bf16[4,128,512]{2,1,0:T(8,128)(2,1)}, bf16[4,128,512]{2,1,0:T(8,128)(2,1)S(1)}, u32[]{:S(2)}) copy-start(bf16[4,128,512]{2,1,0:T(8,128)(2,1)S(1)} %collective-permute-done.7.refs_10_) | copy-start | bytes 1572868
  38.6 20.8 %collective-permute-start.8 = (bf16[4,128,512]{2,1,0:T(8,128)(2,1)S(1)}, bf16[4,128,512]{2,1,0:T(8,128)(2,1)S(1)}, u32[]{:S(2)}, u32[]{:S(2)}) collective-permute-start(bf16[4,128,512]{2,1,0:T(8,128)(2,1)S(1)} %collective-permute-done.7.refs_10_), channel_id=1, source_target_pairs={{0,16},{8,120},{128,144},{136,248},{256,272},{264,376},{384,400},{... | collective-permute-start | bytes 1572872 | tf_op jit(solution)/shard_map/ppermute | solution.py:41
  45.2 16.8 %collective-permute-start.14 = (bf16[4,128,512]{2,1,0:T(8,128)(2,1)S(1)}, bf16[4,128,512]{2,1,0:T(8,128)(2,1)}, u32[]{:S(2)}, u32[]{:S(2)}) collective-permute-start(bf16[4,128,512]{2,1,0:T(8,128)(2,1)S(1)} %collective-permute-done.13.refs_11_), channel_id=1, source_target_pairs={{0,16},{8,120},{128,144},{136,248},{256,272},{264,376},{384,400},{... | collective-permute-start | bytes 1572872 | tf_op jit(solution)/shard_map/ppermute | solution.py:41
  47.7 32.1 %collective-permute-start.3 = (bf16[512,512]{1,0:T(8,128)(2,1)S(1)}, bf16[512,512]{1,0:T(8,128)(2,1)S(1)}, u32[]{:S(2)}, u32[]{:S(2)}) collective-permute-start(bf16[512,512]{1,0:T(8,128)(2,1)S(1)} %fusion.refs_1_), channel_id=1, source_target_pairs={{0,1},{8,9},{128,129},{136,137},{256,257},{264,265},{384,385},{392... | collective-permute-start | bytes 1572872 | tf_op jit(solution)/shard_map/ppermute | solution.py:41
  56.0 31.9 %collective-permute-start = (bf16[512,512]{1,0:T(8,128)(2,1)S(1)}, bf16[512,512]{1,0:T(8,128)(2,1)S(1)}, u32[]{:S(2)}, u32[]{:S(2)}) collective-permute-start(bf16[512,512]{1,0:T(8,128)(2,1)S(1)} %fusion.refs_1_), channel_id=1, source_target_pairs={{0,2},{8,14},{128,130},{136,142},{256,258},{264,270},{384,386},{39... | collective-permute-start | bytes 1572872 | tf_op jit(solution)/shard_map/ppermute | solution.py:41
  59.4 30.4 %collective-permute-start.9 = (bf16[4,128,512]{2,1,0:T(8,128)(2,1)S(1)}, bf16[4,128,512]{2,1,0:T(8,128)(2,1)S(1)}, u32[]{:S(2)}, u32[]{:S(2)}) collective-permute-start(bf16[4,128,512]{2,1,0:T(8,128)(2,1)S(1)} %collective-permute-done.8.refs_11_), channel_id=1, source_target_pairs={{0,16},{8,120},{128,144},{136,248},{256,272},{264,376},{384,400},{... | collective-permute-start | bytes 1572872 | tf_op jit(solution)/shard_map/ppermute | solution.py:41
  64.4 63.6 %collective-permute-start.16 = (bf16[12,128,512]{2,1,0:T(8,128)(2,1)}, bf16[12,128,512]{2,1,0:T(8,128)(2,1)}, u32[]{:S(2)}, u32[]{:S(2)}) collective-permute-start(bf16[12,128,512]{2,1,0:T(8,128)(2,1)} %pad_maximum_fusion.1), channel_id=1, source_target_pairs={{0,8},{8,0},{128,136},{136,128},{256,264},{264,256},{384,392},{392... | collective-permute-start | bytes 4718600 | tf_op jit(solution)/shard_map/ppermute | solution.py:41
  79.9 32.7 %collective-permute-start.4 = (bf16[512,512]{1,0:T(8,128)(2,1)S(1)}, bf16[512,512]{1,0:T(8,128)(2,1)S(1)}, u32[]{:S(2)}, u32[]{:S(2)}) collective-permute-start(bf16[512,512]{1,0:T(8,128)(2,1)S(1)} %collective-permute-done.3.refs_5_), channel_id=1, source_target_pairs={{0,2},{8,14},{128,130},{136,142},{256,258},{264,270},{384,386},{39... | collective-permute-start | bytes 1572872 | tf_op jit(solution)/shard_map/ppermute | solution.py:41
  83.3 32.1 %collective-permute-start.5 = (bf16[512,512]{1,0:T(8,128)(2,1)S(1)}, bf16[512,512]{1,0:T(8,128)(2,1)S(1)}, u32[]{:S(2)}, u32[]{:S(2)}) collective-permute-start(bf16[512,512]{1,0:T(8,128)(2,1)S(1)} %collective-permute-done.3.refs_5_), channel_id=1, source_target_pairs={{0,4},{8,12},{128,132},{136,140},{256,260},{264,268},{384,388},{39... | collective-permute-start | bytes 1572872 | tf_op jit(solution)/shard_map/ppermute | solution.py:41
  87.9 21.6 %collective-permute-start.1 = (bf16[512,512]{1,0:T(8,128)(2,1)S(1)}, bf16[512,512]{1,0:T(8,128)(2,1)}, u32[]{:S(2)}, u32[]{:S(2)}) collective-permute-start(bf16[512,512]{1,0:T(8,128)(2,1)S(1)} %collective-permute-done.refs_2_), channel_id=1, source_target_pairs={{0,2},{8,14},{128,130},{136,142},{256,258},{264,270},{384,386},{39... | collective-permute-start | bytes 1572872 | tf_op jit(solution)/shard_map/ppermute | solution.py:41
  91.2 49.2 %collective-permute-start.11 = (bf16[12,128,512]{2,1,0:T(8,128)(2,1)}, bf16[12,128,512]{2,1,0:T(8,128)(2,1)}, u32[]{:S(2)}, u32[]{:S(2)}) collective-permute-start(bf16[12,128,512]{2,1,0:T(8,128)(2,1)} %pad_maximum_fusion), channel_id=1, source_target_pairs={{0,8},{8,0},{128,136},{136,128},{256,264},{264,256},{384,392},{392... | collective-permute-start | bytes 4718600 | tf_op jit(solution)/shard_map/ppermute | solution.py:41
  109.5 16.3 %collective-permute-start.6 = (bf16[512,512]{1,0:T(8,128)(2,1)S(1)}, bf16[512,512]{1,0:T(8,128)(2,1)}, u32[]{:S(2)}, u32[]{:S(2)}) collective-permute-start(bf16[512,512]{1,0:T(8,128)(2,1)S(1)} %collective-permute-done.3.refs_5_), channel_id=1, source_target_pairs={{0,6},{8,10},{128,134},{136,138},{256,262},{264,266},{384,390},{39... | collective-permute-start | bytes 1572872 | tf_op jit(solution)/shard_map/ppermute | solution.py:41
  112.6 15.1 %collective-permute-start.2 = (bf16[512,512]{1,0:T(8,128)(2,1)}, bf16[512,512]{1,0:T(8,128)(2,1)}, u32[]{:S(2)}, u32[]{:S(2)}) collective-permute-start(bf16[512,512]{1,0:T(8,128)(2,1)} %collective-permute-done.1.refs_3_), channel_id=1, source_target_pairs={{0,2},{8,14},{128,130},{136,142},{256,258},{264,270},{384,386},{39... | collective-permute-start | bytes 1572872 | tf_op jit(solution)/shard_map/ppermute | solution.py:41
  115.4 12.6 %collective-permute-start.15 = (bf16[4,128,512]{2,1,0:T(8,128)(2,1)}, bf16[4,128,512]{2,1,0:T(8,128)(2,1)}, u32[]{:S(2)}, u32[]{:S(2)}) collective-permute-start(bf16[4,128,512]{2,1,0:T(8,128)(2,1)} %collective-permute-done.14.refs_12_), channel_id=1, source_target_pairs={{0,16},{8,120},{128,144},{136,248},{256,272},{264,376},{384,400},{... | collective-permute-start | bytes 1572872 | tf_op jit(solution)/shard_map/ppermute | solution.py:41
  125.8 14.6 %collective-permute-start.10 = (bf16[4,128,512]{2,1,0:T(8,128)(2,1)}, bf16[4,128,512]{2,1,0:T(8,128)(2,1)}, u32[]{:S(2)}, u32[]{:S(2)}) collective-permute-start(bf16[4,128,512]{2,1,0:T(8,128)(2,1)} %copy-done.13), channel_id=1, source_target_pairs={{0,16},{8,120},{128,144},{136,248},{256,272},{264,376},{384,400},{... | collective-permute-start | bytes 1572872 | tf_op jit(solution)/shard_map/ppermute | solution.py:41
  136.5 16.0 %collective-permute-start.17 = (bf16[512,512]{1,0:T(8,128)(2,1)}, bf16[512,512]{1,0:T(8,128)(2,1)}, u32[]{:S(2)}, u32[]{:S(2)}) collective-permute-start(bf16[512,512]{1,0:T(8,128)(2,1)} %project.3.own), channel_id=1, source_target_pairs={{0,8},{8,16},{16,24},{24,32},{32,40},{40,48},{48,56},{56,64},{64,7... | collective-permute-start | bytes 1572872 | tf_op jit(solution)/shard_map/ppermute | solution.py:47
  138.4 19.1 %collective-permute-start.18 = (bf16[512,512]{1,0:T(8,128)(2,1)}, bf16[512,512]{1,0:T(8,128)(2,1)}, u32[]{:S(2)}, u32[]{:S(2)}) collective-permute-start(bf16[512,512]{1,0:T(8,128)(2,1)} %project.3.own), channel_id=1, source_target_pairs={{0,16},{8,24},{16,32},{24,40},{32,48},{40,56},{48,64},{56,72},{64,... | collective-permute-start | bytes 1572872 | tf_op jit(solution)/shard_map/ppermute | solution.py:47
  165.0 9.3 %collective-permute-start.20 = (bf16[512,256]{1,0:T(8,128)(2,1)S(1)}, bf16[512,256]{1,0:T(8,128)(2,1)S(1)}, u32[]{:S(2)}, u32[]{:S(2)}) collective-permute-start(bf16[512,256]{1,0:T(8,128)(2,1)S(1)} %get-tuple-element.9), channel_id=1, source_target_pairs={{8,0},{16,8},{24,16},{32,24},{40,32},{48,40},{56,48},{64,56},{72,6... | collective-permute-start | bytes 786440 | tf_op jit(solution)/shard_map/ppermute | solution.py:47
  169.3 12.1 %collective-permute-start.19 = (bf16[512,256]{1,0:T(8,128)(2,1)S(1)}, bf16[512,256]{1,0:T(8,128)(2,1)S(1)}, u32[]{:S(2)}, u32[]{:S(2)}) collective-permute-start(bf16[512,256]{1,0:T(8,128)(2,1)S(1)} %get-tuple-element.8), channel_id=1, source_target_pairs={{16,0},{24,8},{32,16},{40,24},{48,32},{56,40},{64,48},{72,56},{80,... | collective-permute-start | bytes 786440 | tf_op jit(solution)/shard_map/ppermute | solution.py:47
  (14 other events, 147.1 us)

commit v2 on v1

--- a/solution.py
+++ b/solution.py
@@ -47,8 +47,12 @@
     return lax.ppermute(block, "ctx", route)
 
 
-def project_body(pos, t0, t1, t2, t3, p0, p1, p2, p3, own_ref, r1, r2, r3, r4, swapped, o_ref, *, scale):
-    x, y, zh, sign = pos[0], pos[1], pos[2], pos[3]
+def project_body(t0, t1, t2, t3, p0, p1, p2, p3, own_ref, r1, r2, r3, r4, swapped, o_ref, *, scale):
+    ctx = lax.axis_index("ctx").astype(jnp.int32)
+    head = lax.axis_index("head").astype(jnp.int32)
+    y = lax.rem(lax.div(ctx, 2), NY)
+    sign = 1 - 2 * lax.rem(ctx, 2)
+    x, zh = lax.div(head, NZH), lax.rem(head, NZH)
     total = jnp.zeros(o_ref.shape, F32)
 
     for slot, (near, far) in enumerate(((t0, p0), (t1, p1), (t2, p2), (t3, p3))):
@@ -71,7 +75,7 @@
     o_ref[...] = (total * scale).astype(BF)
 
 
-def project(pos, near, far, ring, swapped, scale):
+def project(near, far, ring, swapped, scale):
     rows = near[0].shape[0]
     cols = ring[0].shape[-1]
     full = pl.BlockSpec(memory_space=pltpu.VMEM)
@@ -79,16 +83,16 @@
     return pl.pallas_call(
         lambda *refs: project_body(*refs, scale=scale),
         out_shape=jax.ShapeDtypeStruct((rows, cols), BF),
-        in_specs=[pl.BlockSpec(memory_space=pltpu.SMEM)] + [full] * len(operands),
+        in_specs=[full] * len(operands),
         out_specs=full,
         cost_estimate=pl.CostEstimate(
             flops=2 * rows * 4096 * cols,
             bytes_accessed=2 * (rows * 4096 + cols * 4096 + rows * cols),
             transcendentals=0,
         ),
-        compiler_params=pltpu.CompilerParams(vmem_limit_bytes=26 * MIB),
+        compiler_params=pltpu.CompilerParams(vmem_limit_bytes=20 * MIB),
         name="project",
-    )(pos, *operands)
+    )(*operands)
 
 
 def ring_y(block):
@@ -105,8 +109,24 @@
     return out
 
 
+def join_body(*refs):
+    *parts, o_ref = refs
+    for i, part in enumerate(parts):
+        o_ref[i * NZL : (i + 1) * NZL] = part[...]
+
+
 def joined_blocks(blocks):
-    return jnp.concatenate(blocks, axis=0)
+    full = pl.BlockSpec(memory_space=pltpu.VMEM)
+    shape = (len(blocks) * NZL,) + blocks[0].shape[1:]
+    return pl.pallas_call(
+        join_body,
+        out_shape=jax.ShapeDtypeStruct(shape, BF),
+        in_specs=[full] * len(blocks),
+        out_specs=full,
+        cost_estimate=pl.CostEstimate(flops=0, bytes_accessed=4 * 2**20, transcendentals=0),
+        compiler_params=pltpu.CompilerParams(vmem_limit_bytes=8 * MIB),
+        name="join",
+    )(*blocks)
 
 
 def gather_zcore(w):
@@ -120,13 +140,14 @@
 REACH = 5 * TILE
 
 
-def scores_body(lead, len_ref, q_ref, own, e1, e2, g_ref, p_ref, dk0, dk1, dk2, ext, s_ref, d_ref, acc):
+def scores_body(len_ref, q_ref, own, e1, e2, g_ref, p_ref, dk0, dk1, dk2, ext, s_ref, d_ref, acc):
     rows = q_ref.shape[0]
     ext[0:rows] = e2[...]
     ext[rows : 2 * rows] = e1[...]
     ext[2 * rows : 3 * rows] = own[...]
     acc[...] = jnp.zeros_like(acc)
     docs = len_ref.shape[1]
+    lead = lax.axis_index("ctx").astype(jnp.int32) * rows
     i0 = lax.broadcasted_iota(jnp.int32, (docs, docs), 0)
     i1 = lax.broadcasted_iota(jnp.int32, (docs, docs), 1)
     starts = jnp.sum(jnp.where(i1 < i0, len_ref[...], 0), axis=1, keepdims=True)
@@ -139,9 +160,9 @@
         q = q_ref[pl.ds(row0, TILE), pl.ds(col0, HEAD_SIZE)]
         g = g_ref[pl.ds(row0, TILE), pl.ds(col0, HEAD_SIZE)]
         row = row0 + lax.broadcasted_iota(jnp.int32, (1, TILE), 1)
-        at = lead[0] + row
+        at = lead + row
         begin = jnp.max(jnp.where(starts <= at, starts, 0), axis=0, keepdims=True)
-        low = jnp.maximum(begin - lead[0] + WINDOW, row + 1)
+        low = jnp.maximum(begin - lead + WINDOW, row + 1)
         nt = (((1,), (1,)), ((), ()))
         peak = jnp.full((1, TILE), -1e30, F32)
         for j in range(5):
@@ -191,10 +212,9 @@
             o_ref[i * TILE : (i + 1) * TILE, h * HEAD_SIZE : (h + 1) * HEAD_SIZE] = a.astype(BF)
 
 
-def attend(lead, lens, query, own, e1, e2, grad):
+def attend(lens, query, own, e1, e2, grad):
     rows = query.shape[0]
     full = pl.BlockSpec(memory_space=pltpu.VMEM)
-    smem = pl.BlockSpec(memory_space=pltpu.SMEM)
     shape = jax.ShapeDtypeStruct
     pairs = 4 * TILE * REACH
     p, dk0, dk1, dk2 = pl.pallas_call(
@@ -205,7 +225,7 @@
             shape((rows, HEAD_SIZE), BF),
             shape((rows, HEAD_SIZE), BF),
         ),
-        in_specs=[smem] + [full] * 6,
+        in_specs=[full] * 6,
         out_specs=(full,) * 4,
         scratch_shapes=[
             pltpu.VMEM((3 * rows, 2 * HEAD_SIZE), BF),
@@ -218,7 +238,7 @@
         ),
         compiler_params=pltpu.CompilerParams(vmem_limit_bytes=16 * MIB),
         name="scores",
-    )(lead, lens, query, own, e1, e2, grad)
+    )(lens, query, own, e1, e2, grad)
     out = pl.pallas_call(
         values_body,
         out_shape=shape((rows, 2 * HEAD_SIZE), BF),
@@ -234,13 +254,6 @@
 
 
 def local(tokens, w_query, key_matrix, value_matrix, d_attended, doc_lengths):
-    rows = tokens.shape[0]
-    ctx = lax.axis_index("ctx").astype(jnp.int32)
-    head = lax.axis_index("head").astype(jnp.int32)
-    core, y = ctx % 2, (ctx // 2) % NY
-    x, zh = head // NZH, head % NZH
-    pos = jnp.stack([x, y, zh, 1 - 2 * core])
-
     feature = jnp.arange(tokens.shape[1], dtype=jnp.int32)
     target = feature // ROWS * PAD + feature % ROWS
     spread = (target[:, None] == jnp.arange(8 * PAD, dtype=jnp.int32)[None, :]).astype(BF)
@@ -258,14 +271,13 @@
     qs = ring_y(w[:, :, kv_cols:].reshape(NZL, PAIR, -1))
     q_a = hop(joined_blocks(qs[1:4]), swap=1)
 
-    joined = project(pos, near, far, kv, kv_a, 1.0)
-    query = project(pos, near, far, qs, q_a, 0.0625)
+    joined = project(near, far, kv, kv_a, 1.0)
+    query = project(near, far, qs, q_a, 0.0625)
 
     e2 = along_ctx(joined, 2)
     e1 = along_ctx(joined, 1)
-    lead = (ctx * rows).reshape(1)
     attended, dk0, dk1, dk2 = attend(
-        lead, doc_lengths.reshape(1, -1), query, joined, e1, e2, d_attended
+        doc_lengths.reshape(1, -1), query, joined, e1, e2, d_attended
     )
     key_total = dk0 + along_ctx(dk2, -2).astype(F32) + along_ctx(dk1, -1).astype(F32)
     return (attended, key_total.astype(BF))

time: 183 us -> 170 us (0.929)
  starting transfers between devices: 61.6 us -> 71.3 us
  Pallas kernels: 20.4 us -> 12.9 us
  local copies, waits for them, and re-layouts: 7.45 us -> 0.14 us
  waiting for transfers between devices: 66.6 us -> 62.4 us
  other arithmetic: 5.53 us -> 1.71 us
    ppermute x17, waiting for transfers between devices: 51 us -> 39.5 us  [hop(): return lax.ppermute(block, BOTH, route)]
    ppermute x17, starting transfers between devices: 51.6 us -> 61.1 us  [hop(): return lax.ppermute(block, BOTH, route)]
    unnamed x34 -> x6, local copies, waits for them, and re-layouts: 7.33 us -> 0.02 us
    ppermute x4, waiting for transfers between devices: 15.6 us -> 22.9 us  [along_ctx(): return lax.ppermute(block, 'ctx', route)]
    pallas_call x2, Pallas kernels: 9.87 us -> 4.8 us  [project(): pl.pallas_call(lambda *refs: project_body(*refs, scale=scale), out_shape=...]
    concatenate x2 -> x0, other arithmetic: 3.75 us -> none  [joined_blocks(): return jnp.concatenate(blocks, axis=0)]
  transfers between devices with their start and end apart: 21 -> 21, of which waited for: 10 -> 13; matrix products, arithmetic and copies ran while one was open for 2% -> 0% of each run, Pallas kernels for 7% -> 4%
where the time goes in v2:
time: 170 us; the launch traced here: 169 us
  starting transfers between devices  71.3 us (42%)
  waiting for transfers between devices  62.4 us (37%)
  blocking collectives  18.9 us (11%)
  Pallas kernels  12.9 us (8%)
  other arithmetic  1.71 us (1%)
    ppermute x17, starting transfers between devices, hop(): return lax.ppermute(block, BOTH, route)  61.1 us
    ppermute x17, waiting for transfers between devices, hop(): return lax.ppermute(block, BOTH, route)  39.5 us
    ppermute x4, waiting for transfers between devices, along_ctx(): return lax.ppermute(block, 'ctx', route)  22.9 us
    all_gather x1, blocking collectives, gather_zcore(): lax.all_gather(w, 'ctx', axis=0, tiled=False, axis_index_groups=groups)  18.9 us
    ppermute x4, starting transfers between devices, along_ctx(): return lax.ppermute(block, 'ctx', route)  10.2 us
    pallas_call x1, Pallas kernels, attend(): pl.pallas_call(scores_body, out_shape=(shape((4, REACH, TILE), BF), shape...  6.17 us
    pallas_call x2, Pallas kernels, project(): pl.pallas_call(lambda *refs: project_body(*refs, scale=scale), out_shape=...  4.8 us
  transfers between devices with their start and end apart: 21, of which 13 were waited for; matrix products, arithmetic and copies ran while one was open for 0% of the time, Pallas kernels for 4%

profile of v2, /device:TPU:64, one launch (start us, length us, event | category | flops | bytes accessed | tf_op | source)
XLA Modules:
  0.0 168.9 jit_solution(12210183117937091016)
XLA Ops:
  1.6 18.9 %all-gather.1 = bf16[8,60,1024]{2,1,0:T(8,128)(2,1)S(1)} all-gather(bf16[1,60,1024]{2,1,0:T(8,128)(2,1)S(1)} %maximum_bitcast_fusion), channel_id=2, replica_groups={{0,8,128,136,256,264,384,392},{16,24,144,152,272,280,400,408},{32,40,16..., dimensions={0}, use_global_device_ids=true | all-gather | bytes 1105920 | tf_op jit(solution)/shard_map/all_gather | solution.py:136
  20.6 3.3 %collective-permute-start.12 = (bf16[4,128,512]{2,1,0:T(8,128)(2,1)S(1)}, bf16[4,128,512]{2,1,0:T(8,128)(2,1)S(1)}, u32[]{:S(2)}, u32[]{:S(2)}) collective-permute-start(bf16[4,128,512]{2,1,0:T(8,128)(2,1)S(1)} %bitcast.10), channel_id=1, source_target_pairs={{0,16},{8,120},{128,144},{136,248},{256,272},{264,376},{384,400},{... | collective-permute-start | bytes 1572872 | tf_op jit(solution)/shard_map/ppermute | solution.py:41
  23.9 3.5 %collective-permute-start.7 = (bf16[4,128,512]{2,1,0:T(8,128)(2,1)S(1)}, bf16[4,128,512]{2,1,0:T(8,128)(2,1)S(1)}, u32[]{:S(2)}, u32[]{:S(2)}) collective-permute-start(bf16[4,128,512]{2,1,0:T(8,128)(2,1)S(1)} %bitcast.8), channel_id=1, source_target_pairs={{0,16},{8,120},{128,144},{136,248},{256,272},{264,376},{384,400},{... | collective-permute-start | bytes 1572872 | tf_op jit(solution)/shard_map/ppermute | solution.py:41
  27.4 5.5 %collective-permute-done.12.refs_0_.refs_9_ = bf16[4,128,512]{2,1,0:T(8,128)(2,1)S(1)} collective-permute-done((bf16[4,128,512]{2,1,0:T(8,128)(2,1)S(1)}, bf16[4,128,512]{2,1,0:T(8,128)(2,1)S(1)}, u32[]{:S(2)}, u32[]{:S(2)}) %collective-permute-start.12) | collective-permute-done | bytes 524320 | tf_op jit(solution)/shard_map/ppermute | solution.py:41
  34.9 3.6 %collective-permute-done.7.refs_0_.refs_9_ = bf16[4,128,512]{2,1,0:T(8,128)(2,1)S(1)} collective-permute-done((bf16[4,128,512]{2,1,0:T(8,128)(2,1)S(1)}, bf16[4,128,512]{2,1,0:T(8,128)(2,1)S(1)}, u32[]{:S(2)}, u32[]{:S(2)}) %collective-permute-start.7) | collective-permute-done | bytes 524320 | tf_op jit(solution)/shard_map/ppermute | solution.py:41
  40.6 4.6 %collective-permute-done.13.refs_1_.refs_10_ = bf16[4,128,512]{2,1,0:T(8,128)(2,1)S(1)} collective-permute-done((bf16[4,128,512]{2,1,0:T(8,128)(2,1)S(1)}, bf16[4,128,512]{2,1,0:T(8,128)(2,1)S(1)}, u32[]{:S(2)}, u32[]{:S(2)}) %collective-permute-start.13) | collective-permute-done | bytes 524320 | tf_op jit(solution)/shard_map/ppermute | solution.py:41
  47.7 3.4 %collective-permute-start = (bf16[512,512]{1,0:T(8,128)(2,1)S(1)}, bf16[512,512]{1,0:T(8,128)(2,1)S(1)}, u32[]{:S(2)}, u32[]{:S(2)}) collective-permute-start(bf16[512,512]{1,0:T(8,128)(2,1)S(1)} %fusion.refs_0_), channel_id=1, source_target_pairs={{0,2},{8,14},{128,130},{136,142},{256,258},{264,270},{384,386},{39... | collective-permute-start | bytes 1572872 | tf_op jit(solution)/shard_map/ppermute | solution.py:41
  51.1 8.2 %collective-permute-start.3 = (bf16[512,512]{1,0:T(8,128)(2,1)S(1)}, bf16[512,512]{1,0:T(8,128)(2,1)S(1)}, u32[]{:S(2)}, u32[]{:S(2)}) collective-permute-start(bf16[512,512]{1,0:T(8,128)(2,1)S(1)} %fusion.refs_0_), channel_id=1, source_target_pairs={{0,1},{8,9},{128,129},{136,137},{256,257},{264,265},{384,385},{392... | collective-permute-start | bytes 1572872 | tf_op jit(solution)/shard_map/ppermute | solution.py:41
  59.3 2.6 %collective-permute-start.9 = (bf16[4,128,512]{2,1,0:T(8,128)(2,1)S(1)}, bf16[4,128,512]{2,1,0:T(8,128)(2,1)S(1)}, u32[]{:S(2)}, u32[]{:S(2)}) collective-permute-start(bf16[4,128,512]{2,1,0:T(8,128)(2,1)S(1)} %collective-permute-done.8.refs_1_.refs_10_), channel_id=1, source_target_pairs={{0,16},{8,120},{128,144},{136,248},{256,272},{264,376},{384,400},{... | collective-permute-start | bytes 1572872 | tf_op jit(solution)/shard_map/ppermute | solution.py:41
  62.0 3.2 %collective-permute-start.16 = (bf16[12,128,512]{2,1,0:T(8,128)(2,1)S(1)}, bf16[12,128,512]{2,1,0:T(8,128)(2,1)S(1)}, u32[]{:S(2)}, u32[]{:S(2)}) collective-permute-start(bf16[12,128,512]{2,1,0:T(8,128)(2,1)S(1)} %join.3), channel_id=1, source_target_pairs={{0,8},{8,0},{128,136},{136,128},{256,264},{264,256},{384,392},{392... | collective-permute-start | bytes 4718600 | tf_op jit(solution)/shard_map/ppermute | solution.py:41
  67.4 14.8 %collective-permute-done.3.refs_4_ = bf16[512,512]{1,0:T(8,128)(2,1)S(1)} collective-permute-done((bf16[512,512]{1,0:T(8,128)(2,1)S(1)}, bf16[512,512]{1,0:T(8,128)(2,1)S(1)}, u32[]{:S(2)}, u32[]{:S(2)}) %collective-permute-start.3) | collective-permute-done | bytes 524320 | tf_op jit(solution)/shard_map/ppermute | solution.py:41
  82.2 4.0 %collective-permute-start.4 = (bf16[512,512]{1,0:T(8,128)(2,1)S(1)}, bf16[512,512]{1,0:T(8,128)(2,1)S(1)}, u32[]{:S(2)}, u32[]{:S(2)}) collective-permute-start(bf16[512,512]{1,0:T(8,128)(2,1)S(1)} %collective-permute-done.3.refs_4_), channel_id=1, source_target_pairs={{0,2},{8,14},{128,130},{136,142},{256,258},{264,270},{384,386},{39... | collective-permute-start | bytes 1572872 | tf_op jit(solution)/shard_map/ppermute | solution.py:41
  86.2 3.9 %collective-permute-start.5 = (bf16[512,512]{1,0:T(8,128)(2,1)S(1)}, bf16[512,512]{1,0:T(8,128)(2,1)S(1)}, u32[]{:S(2)}, u32[]{:S(2)}) collective-permute-start(bf16[512,512]{1,0:T(8,128)(2,1)S(1)} %collective-permute-done.3.refs_4_), channel_id=1, source_target_pairs={{0,4},{8,12},{128,132},{136,140},{256,260},{264,268},{384,388},{39... | collective-permute-start | bytes 1572872 | tf_op jit(solution)/shard_map/ppermute | solution.py:41
  92.2 4.0 %collective-permute-start.6 = (bf16[512,512]{1,0:T(8,128)(2,1)S(1)}, bf16[512,512]{1,0:T(8,128)(2,1)S(1)}, u32[]{:S(2)}, u32[]{:S(2)}) collective-permute-start(bf16[512,512]{1,0:T(8,128)(2,1)S(1)} %collective-permute-done.3.refs_4_), channel_id=1, source_target_pairs={{0,6},{8,10},{128,134},{136,138},{256,262},{264,266},{384,390},{39... | collective-permute-start | bytes 1572872 | tf_op jit(solution)/shard_map/ppermute | solution.py:41
  96.7 8.6 %collective-permute-start.2 = (bf16[512,512]{1,0:T(8,128)(2,1)S(1)}, bf16[512,512]{1,0:T(8,128)(2,1)S(1)}, u32[]{:S(2)}, u32[]{:S(2)}) collective-permute-start(bf16[512,512]{1,0:T(8,128)(2,1)S(1)} %collective-permute-done.1.refs_2_), channel_id=1, source_target_pairs={{0,2},{8,14},{128,130},{136,142},{256,258},{264,270},{384,386},{39... | collective-permute-start | bytes 1572872 | tf_op jit(solution)/shard_map/ppermute | solution.py:41
  105.2 4.0 %collective-permute-done.5.refs_6_ = bf16[512,512]{1,0:T(8,128)(2,1)S(1)} collective-permute-done((bf16[512,512]{1,0:T(8,128)(2,1)S(1)}, bf16[512,512]{1,0:T(8,128)(2,1)S(1)}, u32[]{:S(2)}, u32[]{:S(2)}) %collective-permute-start.5) | collective-permute-done | bytes 524320 | tf_op jit(solution)/shard_map/ppermute | solution.py:41
  109.2 3.3 %collective-permute-start.15 = (bf16[4,128,512]{2,1,0:T(8,128)(2,1)S(1)}, bf16[4,128,512]{2,1,0:T(8,128)(2,1)S(1)}, u32[]{:S(2)}, u32[]{:S(2)}) collective-permute-start(bf16[4,128,512]{2,1,0:T(8,128)(2,1)S(1)} %collective-permute-done.14.refs_2_.refs_11_), channel_id=1, source_target_pairs={{0,16},{8,120},{128,144},{136,248},{256,272},{264,376},{384,400},{... | collective-permute-start | bytes 1572872 | tf_op jit(solution)/shard_map/ppermute | solution.py:41
  114.2 3.2 %collective-permute-start.10 = (bf16[4,128,512]{2,1,0:T(8,128)(2,1)S(1)}, bf16[4,128,512]{2,1,0:T(8,128)(2,1)S(1)}, u32[]{:S(2)}, u32[]{:S(2)}) collective-permute-start(bf16[4,128,512]{2,1,0:T(8,128)(2,1)S(1)} %collective-permute-done.9.refs_2_.refs_11_), channel_id=1, source_target_pairs={{0,16},{8,120},{128,144},{136,248},{256,272},{264,376},{384,400},{... | collective-permute-start | bytes 1572872 | tf_op jit(solution)/shard_map/ppermute | solution.py:41
  117.9 4.3 %collective-permute-done.15.refs_12_ = bf16[4,128,512]{2,1,0:T(8,128)(2,1)S(1)} collective-permute-done((bf16[4,128,512]{2,1,0:T(8,128)(2,1)S(1)}, bf16[4,128,512]{2,1,0:T(8,128)(2,1)S(1)}, u32[]{:S(2)}, u32[]{:S(2)}) %collective-permute-start.15) | collective-permute-done | bytes 524320 | tf_op jit(solution)/shard_map/ppermute | solution.py:41
  131.1 9.4 %collective-permute-done.17.e1 = bf16[512,512]{1,0:T(8,128)(2,1)S(1)} collective-permute-done((bf16[512,512]{1,0:T(8,128)(2,1)S(1)}, bf16[512,512]{1,0:T(8,128)(2,1)S(1)}, u32[]{:S(2)}, u32[]{:S(2)}) %collective-permute-start.17) | collective-permute-done | bytes 524320 | tf_op jit(solution)/shard_map/ppermute | solution.py:47
  140.5 5.0 %collective-permute-done.18.e2 = bf16[512,512]{1,0:T(8,128)(2,1)S(1)} collective-permute-done((bf16[512,512]{1,0:T(8,128)(2,1)S(1)}, bf16[512,512]{1,0:T(8,128)(2,1)S(1)}, u32[]{:S(2)}, u32[]{:S(2)}) %collective-permute-start.18) | collective-permute-done | bytes 524320 | tf_op jit(solution)/shard_map/ppermute | solution.py:47
  145.5 6.2 %scores.1 = (bf16[4,1280,256]{2,1,0:T(8,128)(2,1)S(1)}, f32[512,256]{1,0:T(8,128)S(1)}, bf16[512,256]{1,0:T(8,128)(2,1)S(1)}, bf16[512,256]{1,0:T(8,128)(2,1)S(1)}) custom-call(s32[1,32]{1,0:T(1,128)S(1)} %bitcast.12, bf16[512,512]{1,0:T(8,128)(2,1)S(1)} %project.2.q_ref, bf16[512,512]{1,0:T(8,128)(2,1)S(1)} %project.3.own, ...), custom_call_target="tpu_custom_call" | custom-call | flops 2013265920 | bytes 5242880 | tf_op jit(solution)/shard_map/scores/pallas_call | solution.py:220
  151.7 4.3 %collective-permute-start.20 = (bf16[512,256]{1,0:T(8,128)(2,1)S(1)}, bf16[512,256]{1,0:T(8,128)(2,1)S(1)}, u32[]{:S(2)}, u32[]{:S(2)}) collective-permute-start(bf16[512,256]{1,0:T(8,128)(2,1)S(1)} %get-tuple-element.9), channel_id=1, source_target_pairs={{8,0},{16,8},{24,16},{32,24},{40,32},{48,40},{56,48},{64,56},{72,6... | collective-permute-start | bytes 786440 | tf_op jit(solution)/shard_map/ppermute | solution.py:47
  160.8 7.2 %collective-permute-done.19 = bf16[512,256]{1,0:T(8,128)(2,1)S(1)} collective-permute-done((bf16[512,256]{1,0:T(8,128)(2,1)S(1)}, bf16[512,256]{1,0:T(8,128)(2,1)S(1)}, u32[]{:S(2)}, u32[]{:S(2)}) %collective-permute-start.19) | collective-permute-done | bytes 262176 | tf_op jit(solution)/shard_map/ppermute | solution.py:47
  (36 shorter events, 28.8 us)
Async XLA Ops:
  0.6 46.5 %copy-start = (bf16[512,480]{0,1:T(8,128)(2,1)S(1)}, bf16[512,480]{0,1:T(8,128)(2,1)}, u32[]{:S(2)}) copy-start(bf16[512,480]{0,1:T(8,128)(2,1)} %param.6) | copy-start | bytes 1474564
  20.6 12.3 %collective-permute-start.12 = (bf16[4,128,512]{2,1,0:T(8,128)(2,1)S(1)}, bf16[4,128,512]{2,1,0:T(8,128)(2,1)S(1)}, u32[]{:S(2)}, u32[]{:S(2)}) collective-permute-start(bf16[4,128,512]{2,1,0:T(8,128)(2,1)S(1)} %bitcast.10), channel_id=1, source_target_pairs={{0,16},{8,120},{128,144},{136,248},{256,272},{264,376},{384,400},{... | collective-permute-start | bytes 1572872 | tf_op jit(solution)/shard_map/ppermute | solution.py:41
  23.9 14.7 %collective-permute-start.7 = (bf16[4,128,512]{2,1,0:T(8,128)(2,1)S(1)}, bf16[4,128,512]{2,1,0:T(8,128)(2,1)S(1)}, u32[]{:S(2)}, u32[]{:S(2)}) collective-permute-start(bf16[4,128,512]{2,1,0:T(8,128)(2,1)S(1)} %bitcast.8), channel_id=1, source_target_pairs={{0,16},{8,120},{128,144},{136,248},{256,272},{264,376},{384,400},{... | collective-permute-start | bytes 1572872 | tf_op jit(solution)/shard_map/ppermute | solution.py:41
  32.9 12.3 %collective-permute-start.13 = (bf16[4,128,512]{2,1,0:T(8,128)(2,1)S(1)}, bf16[4,128,512]{2,1,0:T(8,128)(2,1)S(1)}, u32[]{:S(2)}, u32[]{:S(2)}) collective-permute-start(bf16[4,128,512]{2,1,0:T(8,128)(2,1)S(1)} %collective-permute-done.12.refs_0_.refs_9_), channel_id=1, source_target_pairs={{0,16},{8,120},{128,144},{136,248},{256,272},{264,376},{384,400},{... | collective-permute-start | bytes 1572872 | tf_op jit(solution)/shard_map/ppermute | solution.py:41
  38.5 20.8 %collective-permute-start.8 = (bf16[4,128,512]{2,1,0:T(8,128)(2,1)S(1)}, bf16[4,128,512]{2,1,0:T(8,128)(2,1)S(1)}, u32[]{:S(2)}, u32[]{:S(2)}) collective-permute-start(bf16[4,128,512]{2,1,0:T(8,128)(2,1)S(1)} %collective-permute-done.7.refs_0_.refs_9_), channel_id=1, source_target_pairs={{0,16},{8,120},{128,144},{136,248},{256,272},{264,376},{384,400},{... | collective-permute-start | bytes 1572872 | tf_op jit(solution)/shard_map/ppermute | solution.py:41
  45.2 16.7 %collective-permute-start.14 = (bf16[4,128,512]{2,1,0:T(8,128)(2,1)S(1)}, bf16[4,128,512]{2,1,0:T(8,128)(2,1)S(1)}, u32[]{:S(2)}, u32[]{:S(2)}) collective-permute-start(bf16[4,128,512]{2,1,0:T(8,128)(2,1)S(1)} %collective-permute-done.13.refs_1_.refs_10_), channel_id=1, source_target_pairs={{0,16},{8,120},{128,144},{136,248},{256,272},{264,376},{384,400},{... | collective-permute-start | bytes 1572872 | tf_op jit(solution)/shard_map/ppermute | solution.py:41
  47.7 17.5 %collective-permute-start = (bf16[512,512]{1,0:T(8,128)(2,1)S(1)}, bf16[512,512]{1,0:T(8,128)(2,1)S(1)}, u32[]{:S(2)}, u32[]{:S(2)}) collective-permute-start(bf16[512,512]{1,0:T(8,128)(2,1)S(1)} %fusion.refs_0_), channel_id=1, source_target_pairs={{0,2},{8,14},{128,130},{136,142},{256,258},{264,270},{384,386},{39... | collective-permute-start | bytes 1572872 | tf_op jit(solution)/shard_map/ppermute | solution.py:41
  51.1 31.1 %collective-permute-start.3 = (bf16[512,512]{1,0:T(8,128)(2,1)S(1)}, bf16[512,512]{1,0:T(8,128)(2,1)S(1)}, u32[]{:S(2)}, u32[]{:S(2)}) collective-permute-start(bf16[512,512]{1,0:T(8,128)(2,1)S(1)} %fusion.refs_0_), channel_id=1, source_target_pairs={{0,1},{8,9},{128,129},{136,137},{256,257},{264,265},{384,385},{392... | collective-permute-start | bytes 1572872 | tf_op jit(solution)/shard_map/ppermute | solution.py:41
  59.3 30.8 %collective-permute-start.9 = (bf16[4,128,512]{2,1,0:T(8,128)(2,1)S(1)}, bf16[4,128,512]{2,1,0:T(8,128)(2,1)S(1)}, u32[]{:S(2)}, u32[]{:S(2)}) collective-permute-start(bf16[4,128,512]{2,1,0:T(8,128)(2,1)S(1)} %collective-permute-done.8.refs_1_.refs_10_), channel_id=1, source_target_pairs={{0,16},{8,120},{128,144},{136,248},{256,272},{264,376},{384,400},{... | collective-permute-start | bytes 1572872 | tf_op jit(solution)/shard_map/ppermute | solution.py:41
  62.0 60.2 %collective-permute-start.16 = (bf16[12,128,512]{2,1,0:T(8,128)(2,1)S(1)}, bf16[12,128,512]{2,1,0:T(8,128)(2,1)S(1)}, u32[]{:S(2)}, u32[]{:S(2)}) collective-permute-start(bf16[12,128,512]{2,1,0:T(8,128)(2,1)S(1)} %join.3), channel_id=1, source_target_pairs={{0,8},{8,0},{128,136},{136,128},{256,264},{264,256},{384,392},{392... | collective-permute-start | bytes 4718600 | tf_op jit(solution)/shard_map/ppermute | solution.py:41
  65.3 27.0 %collective-permute-start.1 = (bf16[512,512]{1,0:T(8,128)(2,1)S(1)}, bf16[512,512]{1,0:T(8,128)(2,1)S(1)}, u32[]{:S(2)}, u32[]{:S(2)}) collective-permute-start(bf16[512,512]{1,0:T(8,128)(2,1)S(1)} %collective-permute-done.refs_1_), channel_id=1, source_target_pairs={{0,2},{8,14},{128,130},{136,142},{256,258},{264,270},{384,386},{39... | collective-permute-start | bytes 1572872 | tf_op jit(solution)/shard_map/ppermute | solution.py:41
  82.2 14.4 %collective-permute-start.4 = (bf16[512,512]{1,0:T(8,128)(2,1)S(1)}, bf16[512,512]{1,0:T(8,128)(2,1)S(1)}, u32[]{:S(2)}, u32[]{:S(2)}) collective-permute-start(bf16[512,512]{1,0:T(8,128)(2,1)S(1)} %collective-permute-done.3.refs_4_), channel_id=1, source_target_pairs={{0,2},{8,14},{128,130},{136,142},{256,258},{264,270},{384,386},{39... | collective-permute-start | bytes 1572872 | tf_op jit(solution)/shard_map/ppermute | solution.py:41
  86.2 23.0 %collective-permute-start.5 = (bf16[512,512]{1,0:T(8,128)(2,1)S(1)}, bf16[512,512]{1,0:T(8,128)(2,1)S(1)}, u32[]{:S(2)}, u32[]{:S(2)}) collective-permute-start(bf16[512,512]{1,0:T(8,128)(2,1)S(1)} %collective-permute-done.3.refs_4_), channel_id=1, source_target_pairs={{0,4},{8,12},{128,132},{136,140},{256,260},{264,268},{384,388},{39... | collective-permute-start | bytes 1572872 | tf_op jit(solution)/shard_map/ppermute | solution.py:41
  90.3 38.3 %collective-permute-start.11 = (bf16[12,128,512]{2,1,0:T(8,128)(2,1)S(1)}, bf16[12,128,512]{2,1,0:T(8,128)(2,1)S(1)}, u32[]{:S(2)}, u32[]{:S(2)}) collective-permute-start(bf16[12,128,512]{2,1,0:T(8,128)(2,1)S(1)} %join.2), channel_id=1, source_target_pairs={{0,8},{8,0},{128,136},{136,128},{256,264},{264,256},{384,392},{392... | collective-permute-start | bytes 4718600 | tf_op jit(solution)/shard_map/ppermute | solution.py:41
  92.2 21.9 %collective-permute-start.6 = (bf16[512,512]{1,0:T(8,128)(2,1)S(1)}, bf16[512,512]{1,0:T(8,128)(2,1)S(1)}, u32[]{:S(2)}, u32[]{:S(2)}) collective-permute-start(bf16[512,512]{1,0:T(8,128)(2,1)S(1)} %collective-permute-done.3.refs_4_), channel_id=1, source_target_pairs={{0,6},{8,10},{128,134},{136,138},{256,262},{264,266},{384,390},{39... | collective-permute-start | bytes 1572872 | tf_op jit(solution)/shard_map/ppermute | solution.py:41
  96.7 21.2 %collective-permute-start.2 = (bf16[512,512]{1,0:T(8,128)(2,1)S(1)}, bf16[512,512]{1,0:T(8,128)(2,1)S(1)}, u32[]{:S(2)}, u32[]{:S(2)}) collective-permute-start(bf16[512,512]{1,0:T(8,128)(2,1)S(1)} %collective-permute-done.1.refs_2_), channel_id=1, source_target_pairs={{0,2},{8,14},{128,130},{136,142},{256,258},{264,270},{384,386},{39... | collective-permute-start | bytes 1572872 | tf_op jit(solution)/shard_map/ppermute | solution.py:41
  109.2 13.0 %collective-permute-start.15 = (bf16[4,128,512]{2,1,0:T(8,128)(2,1)S(1)}, bf16[4,128,512]{2,1,0:T(8,128)(2,1)S(1)}, u32[]{:S(2)}, u32[]{:S(2)}) collective-permute-start(bf16[4,128,512]{2,1,0:T(8,128)(2,1)S(1)} %collective-permute-done.14.refs_2_.refs_11_), channel_id=1, source_target_pairs={{0,16},{8,120},{128,144},{136,248},{256,272},{264,376},{384,400},{... | collective-permute-start | bytes 1572872 | tf_op jit(solution)/shard_map/ppermute | solution.py:41
  114.2 14.5 %collective-permute-start.10 = (bf16[4,128,512]{2,1,0:T(8,128)(2,1)S(1)}, bf16[4,128,512]{2,1,0:T(8,128)(2,1)S(1)}, u32[]{:S(2)}, u32[]{:S(2)}) collective-permute-start(bf16[4,128,512]{2,1,0:T(8,128)(2,1)S(1)} %collective-permute-done.9.refs_2_.refs_11_), channel_id=1, source_target_pairs={{0,16},{8,120},{128,144},{136,248},{256,272},{264,376},{384,400},{... | collective-permute-start | bytes 1572872 | tf_op jit(solution)/shard_map/ppermute | solution.py:41
  124.6 20.9 %copy-start.1 = (bf16[512,512]{1,0:T(8,128)(2,1)S(1)}, bf16[512,512]{1,0:T(8,128)(2,1)}, u32[]{:S(2)}) copy-start(bf16[512,512]{1,0:T(8,128)(2,1)} %g_ref.1) | copy-start | bytes 1572868
  124.6 20.9 %copy-start.2 = (s32[32]{0:T(128)S(1)}, s32[32]{0:T(128)}, u32[]{:S(2)}) copy-start(s32[32]{0:T(128)} %param.11) | copy-start | bytes 388
  124.6 15.9 %collective-permute-start.17 = (bf16[512,512]{1,0:T(8,128)(2,1)S(1)}, bf16[512,512]{1,0:T(8,128)(2,1)S(1)}, u32[]{:S(2)}, u32[]{:S(2)}) collective-permute-start(bf16[512,512]{1,0:T(8,128)(2,1)S(1)} %project.3.own), channel_id=1, source_target_pairs={{0,8},{8,16},{16,24},{24,32},{32,40},{40,48},{48,56},{56,64},{64,7... | collective-permute-start | bytes 1572872 | tf_op jit(solution)/shard_map/ppermute | solution.py:47
  126.7 18.8 %collective-permute-start.18 = (bf16[512,512]{1,0:T(8,128)(2,1)S(1)}, bf16[512,512]{1,0:T(8,128)(2,1)S(1)}, u32[]{:S(2)}, u32[]{:S(2)}) collective-permute-start(bf16[512,512]{1,0:T(8,128)(2,1)S(1)} %project.3.own), channel_id=1, source_target_pairs={{0,16},{8,24},{16,32},{24,40},{32,48},{40,56},{48,64},{56,72},{64,... | collective-permute-start | bytes 1572872 | tf_op jit(solution)/shard_map/ppermute | solution.py:47
  151.7 9.2 %collective-permute-start.20 = (bf16[512,256]{1,0:T(8,128)(2,1)S(1)}, bf16[512,256]{1,0:T(8,128)(2,1)S(1)}, u32[]{:S(2)}, u32[]{:S(2)}) collective-permute-start(bf16[512,256]{1,0:T(8,128)(2,1)S(1)} %get-tuple-element.9), channel_id=1, source_target_pairs={{8,0},{16,8},{24,16},{32,24},{40,32},{48,40},{56,48},{64,56},{72,6... | collective-permute-start | bytes 786440 | tf_op jit(solution)/shard_map/ppermute | solution.py:47
  156.0 12.1 %collective-permute-start.19 = (bf16[512,256]{1,0:T(8,128)(2,1)S(1)}, bf16[512,256]{1,0:T(8,128)(2,1)S(1)}, u32[]{:S(2)}, u32[]{:S(2)}) collective-permute-start(bf16[512,256]{1,0:T(8,128)(2,1)S(1)} %get-tuple-element.8), channel_id=1, source_target_pairs={{16,0},{24,8},{32,16},{40,24},{48,32},{56,40},{64,48},{72,56},{80,... | collective-permute-start | bytes 786440 | tf_op jit(solution)/shard_map/ppermute | solution.py:47

commit v3 on v2

--- a/solution.py
+++ b/solution.py
@@ -103,10 +103,10 @@
 
 
 def ring_x(block):
-    out = [block]
-    for _ in range(3):
-        out.append(hop(out[-1], dx=1, by_core=True))
-    return out
+    one = hop(block, dx=1, by_core=True)
+    three = hop(block, dx=3, by_core=True)
+    two = hop(one, dx=1, by_core=True)
+    return [block, one, two, three]
 
 
 def join_body(*refs):
@@ -261,7 +261,7 @@
 
     partner = hop(own, dz=NZL)
     near = ring_x(own)
-    far = [partner] + [hop(partner, dx=d, by_core=True) for d in (1, 2, 3)]
+    far = ring_x(partner)
 
     w = gather_zcore(jnp.concatenate([key_matrix, value_matrix, w_query], axis=1))
     w = jnp.pad(w, ((0, 0), (0, PAD - ROWS), (0, 0)))

time: 170 us -> 160 us (0.941)
  the two profiles are of different devices: /device:TPU:64 before, /device:TPU:68 now
where the time goes in v3:
time: 160 us
  waiting for transfers between devices  65.3 us (41%)
  starting transfers between devices  59.4 us (37%)
  blocking collectives  18.7 us (12%)
  Pallas kernels  12.9 us (8%)
  other arithmetic  1.71 us (1%)
    ppermute x17, starting transfers between devices, hop(): return lax.ppermute(block, BOTH, route)  49.2 us
    ppermute x17, waiting for transfers between devices, hop(): return lax.ppermute(block, BOTH, route)  42.3 us
    ppermute x4, waiting for transfers between devices, along_ctx(): return lax.ppermute(block, 'ctx', route)  22.9 us
    all_gather x1, blocking collectives, gather_zcore(): lax.all_gather(w, 'ctx', axis=0, tiled=False, axis_index_groups=groups)  18.7 us
    ppermute x4, starting transfers between devices, along_ctx(): return lax.ppermute(block, 'ctx', route)  10.2 us
    pallas_call x1, Pallas kernels, attend(): pl.pallas_call(scores_body, out_shape=(shape((4, REACH, TILE), BF), shape...  6.16 us
    pallas_call x2, Pallas kernels, project(): pl.pallas_call(lambda *refs: project_body(*refs, scale=scale), out_shape=...  4.8 us
  transfers between devices with their start and end apart: 21, of which 12 were waited for; matrix products, arithmetic and copies ran while one was open for 0% of the time, Pallas kernels for 4%

profile of v3, /device:TPU:68, one launch (start us, length us, event | category | flops | bytes accessed | tf_op | source)
XLA Modules:
  0.0 159.6 jit_solution(8523139463093519676)
XLA Ops:
  1.6 18.7 %all-gather.1 = bf16[8,60,1024]{2,1,0:T(8,128)(2,1)S(1)} all-gather(bf16[1,60,1024]{2,1,0:T(8,128)(2,1)S(1)} %maximum_bitcast_fusion), channel_id=2, replica_groups={{0,8,128,136,256,264,384,392},{16,24,144,152,272,280,400,408},{32,40,16..., dimensions={0}, use_global_device_ids=true | all-gather | bytes 1105920 | tf_op jit(solution)/shard_map/all_gather | solution.py:136
  20.4 3.5 %collective-permute-start.12 = (bf16[4,128,512]{2,1,0:T(8,128)(2,1)S(1)}, bf16[4,128,512]{2,1,0:T(8,128)(2,1)S(1)}, u32[]{:S(2)}, u32[]{:S(2)}) collective-permute-start(bf16[4,128,512]{2,1,0:T(8,128)(2,1)S(1)} %bitcast.10), channel_id=1, source_target_pairs={{0,16},{8,120},{128,144},{136,248},{256,272},{264,376},{384,400},{... | collective-permute-start | bytes 1572872 | tf_op jit(solution)/shard_map/ppermute | solution.py:41
  23.9 3.5 %collective-permute-start.7 = (bf16[4,128,512]{2,1,0:T(8,128)(2,1)S(1)}, bf16[4,128,512]{2,1,0:T(8,128)(2,1)S(1)}, u32[]{:S(2)}, u32[]{:S(2)}) collective-permute-start(bf16[4,128,512]{2,1,0:T(8,128)(2,1)S(1)} %bitcast.8), channel_id=1, source_target_pairs={{0,16},{8,120},{128,144},{136,248},{256,272},{264,376},{384,400},{... | collective-permute-start | bytes 1572872 | tf_op jit(solution)/shard_map/ppermute | solution.py:41
  27.4 5.5 %collective-permute-done.12.refs_0_.refs_9_ = bf16[4,128,512]{2,1,0:T(8,128)(2,1)S(1)} collective-permute-done((bf16[4,128,512]{2,1,0:T(8,128)(2,1)S(1)}, bf16[4,128,512]{2,1,0:T(8,128)(2,1)S(1)}, u32[]{:S(2)}, u32[]{:S(2)}) %collective-permute-start.12) | collective-permute-done | bytes 524320 | tf_op jit(solution)/shard_map/ppermute | solution.py:41
  34.9 3.6 %collective-permute-done.7.refs_0_.refs_9_ = bf16[4,128,512]{2,1,0:T(8,128)(2,1)S(1)} collective-permute-done((bf16[4,128,512]{2,1,0:T(8,128)(2,1)S(1)}, bf16[4,128,512]{2,1,0:T(8,128)(2,1)S(1)}, u32[]{:S(2)}, u32[]{:S(2)}) %collective-permute-start.7) | collective-permute-done | bytes 524320 | tf_op jit(solution)/shard_map/ppermute | solution.py:41
  40.6 4.6 %collective-permute-done.13.refs_1_.refs_10_ = bf16[4,128,512]{2,1,0:T(8,128)(2,1)S(1)} collective-permute-done((bf16[4,128,512]{2,1,0:T(8,128)(2,1)S(1)}, bf16[4,128,512]{2,1,0:T(8,128)(2,1)S(1)}, u32[]{:S(2)}, u32[]{:S(2)}) %collective-permute-start.13) | collective-permute-done | bytes 524320 | tf_op jit(solution)/shard_map/ppermute | solution.py:41
  47.7 8.2 %collective-permute-start.3 = (bf16[512,512]{1,0:T(8,128)(2,1)S(1)}, bf16[512,512]{1,0:T(8,128)(2,1)S(1)}, u32[]{:S(2)}, u32[]{:S(2)}) collective-permute-start(bf16[512,512]{1,0:T(8,128)(2,1)S(1)} %fusion.refs_0_), channel_id=1, source_target_pairs={{0,1},{8,9},{128,129},{136,137},{256,257},{264,265},{384,385},{392... | collective-permute-start | bytes 1572872 | tf_op jit(solution)/shard_map/ppermute | solution.py:41
  55.9 3.1 %collective-permute-start = (bf16[512,512]{1,0:T(8,128)(2,1)S(1)}, bf16[512,512]{1,0:T(8,128)(2,1)S(1)}, u32[]{:S(2)}, u32[]{:S(2)}) collective-permute-start(bf16[512,512]{1,0:T(8,128)(2,1)S(1)} %fusion.refs_0_), channel_id=1, source_target_pairs={{0,2},{8,14},{128,130},{136,142},{256,258},{264,270},{384,386},{39... | collective-permute-start | bytes 1572872 | tf_op jit(solution)/shard_map/ppermute | solution.py:41
  59.1 2.5 %collective-permute-start.9 = (bf16[4,128,512]{2,1,0:T(8,128)(2,1)S(1)}, bf16[4,128,512]{2,1,0:T(8,128)(2,1)S(1)}, u32[]{:S(2)}, u32[]{:S(2)}) collective-permute-start(bf16[4,128,512]{2,1,0:T(8,128)(2,1)S(1)} %collective-permute-done.8.refs_1_.refs_10_), channel_id=1, source_target_pairs={{0,16},{8,120},{128,144},{136,248},{256,272},{264,376},{384,400},{... | collective-permute-start | bytes 1572872 | tf_op jit(solution)/shard_map/ppermute | solution.py:41
  63.7 2.7 %collective-permute-start.2 = (bf16[512,512]{1,0:T(8,128)(2,1)S(1)}, bf16[512,512]{1,0:T(8,128)(2,1)S(1)}, u32[]{:S(2)}, u32[]{:S(2)}) collective-permute-start(bf16[512,512]{1,0:T(8,128)(2,1)S(1)} %fusion.refs_0_), channel_id=1, source_target_pairs={{0,6},{8,10},{128,134},{136,138},{256,262},{264,266},{384,390},{39... | collective-permute-start | bytes 1572872 | tf_op jit(solution)/shard_map/ppermute | solution.py:41
  66.4 13.4 %collective-permute-done.3.refs_4_ = bf16[512,512]{1,0:T(8,128)(2,1)S(1)} collective-permute-done((bf16[512,512]{1,0:T(8,128)(2,1)S(1)}, bf16[512,512]{1,0:T(8,128)(2,1)S(1)}, u32[]{:S(2)}, u32[]{:S(2)}) %collective-permute-start.3) | collective-permute-done | bytes 524320 | tf_op jit(solution)/shard_map/ppermute | solution.py:41
  79.8 3.1 %collective-permute-start.4 = (bf16[512,512]{1,0:T(8,128)(2,1)S(1)}, bf16[512,512]{1,0:T(8,128)(2,1)S(1)}, u32[]{:S(2)}, u32[]{:S(2)}) collective-permute-start(bf16[512,512]{1,0:T(8,128)(2,1)S(1)} %collective-permute-done.3.refs_4_), channel_id=1, source_target_pairs={{0,2},{8,14},{128,130},{136,142},{256,258},{264,270},{384,386},{39... | collective-permute-start | bytes 1572872 | tf_op jit(solution)/shard_map/ppermute | solution.py:41
  83.0 2.4 %collective-permute-start.1 = (bf16[512,512]{1,0:T(8,128)(2,1)S(1)}, bf16[512,512]{1,0:T(8,128)(2,1)S(1)}, u32[]{:S(2)}, u32[]{:S(2)}) collective-permute-start(bf16[512,512]{1,0:T(8,128)(2,1)S(1)} %collective-permute-done.refs_1_), channel_id=1, source_target_pairs={{0,2},{8,14},{128,130},{136,142},{256,258},{264,270},{384,386},{39... | collective-permute-start | bytes 1572872 | tf_op jit(solution)/shard_map/ppermute | solution.py:41
  87.4 3.8 %collective-permute-start.6 = (bf16[512,512]{1,0:T(8,128)(2,1)S(1)}, bf16[512,512]{1,0:T(8,128)(2,1)S(1)}, u32[]{:S(2)}, u32[]{:S(2)}) collective-permute-start(bf16[512,512]{1,0:T(8,128)(2,1)S(1)} %collective-permute-done.3.refs_4_), channel_id=1, source_target_pairs={{0,6},{8,10},{128,134},{136,138},{256,262},{264,266},{384,390},{39... | collective-permute-start | bytes 1572872 | tf_op jit(solution)/shard_map/ppermute | solution.py:41
  91.2 2.8 %collective-permute-start.5 = (bf16[512,512]{1,0:T(8,128)(2,1)S(1)}, bf16[512,512]{1,0:T(8,128)(2,1)S(1)}, u32[]{:S(2)}, u32[]{:S(2)}) collective-permute-start(bf16[512,512]{1,0:T(8,128)(2,1)S(1)} %collective-permute-done.4.refs_5_), channel_id=1, source_target_pairs={{0,2},{8,14},{128,130},{136,142},{256,258},{264,270},{384,386},{39... | collective-permute-start | bytes 1572872 | tf_op jit(solution)/shard_map/ppermute | solution.py:41
  94.0 6.7 %collective-permute-done.1.refs_2_ = bf16[512,512]{1,0:T(8,128)(2,1)S(1)} collective-permute-done((bf16[512,512]{1,0:T(8,128)(2,1)S(1)}, bf16[512,512]{1,0:T(8,128)(2,1)S(1)}, u32[]{:S(2)}, u32[]{:S(2)}) %collective-permute-start.1) | collective-permute-done | bytes 524320 | tf_op jit(solution)/shard_map/ppermute | solution.py:41
  107.8 5.2 %collective-permute-done.15.refs_12_ = bf16[4,128,512]{2,1,0:T(8,128)(2,1)S(1)} collective-permute-done((bf16[4,128,512]{2,1,0:T(8,128)(2,1)S(1)}, bf16[4,128,512]{2,1,0:T(8,128)(2,1)S(1)}, u32[]{:S(2)}, u32[]{:S(2)}) %collective-permute-start.15) | collective-permute-done | bytes 524320 | tf_op jit(solution)/shard_map/ppermute | solution.py:41
  113.0 2.4 %project.3.own = bf16[512,512]{1,0:T(8,128)(2,1)S(1)} custom-call(bf16[512,512]{1,0:T(8,128)(2,1)S(1)} %fusion.refs_0_, bf16[512,512]{1,0:T(8,128)(2,1)S(1)} %collective-permute-done.refs_1_, bf16[512,512]{1,0:T(8,128)(2,1)S(1)} %collective-permute-done.1.refs_2_, bf16[512,512]{1,0:T(8,128)(2,1)S(1)} %collective-permute-done.2.refs_3_, ...), custom_call_target="tpu_custom_call" | custom-call | flops 2147483648 | bytes 8912896 | tf_op jit(solution)/shard_map/project/pallas_call | solution.py:83
  119.4 2.4 %project.2.q_ref = bf16[512,512]{1,0:T(8,128)(2,1)S(1)} custom-call(bf16[512,512]{1,0:T(8,128)(2,1)S(1)} %fusion.refs_0_, bf16[512,512]{1,0:T(8,128)(2,1)S(1)} %collective-permute-done.refs_1_, bf16[512,512]{1,0:T(8,128)(2,1)S(1)} %collective-permute-done.1.refs_2_, bf16[512,512]{1,0:T(8,128)(2,1)S(1)} %collective-permute-done.2.refs_3_, ...), custom_call_target="tpu_custom_call" | custom-call | flops 2147483648 | bytes 8912896 | tf_op jit(solution)/shard_map/project/pallas_call | solution.py:83
  121.8 9.4 %collective-permute-done.17.e1 = bf16[512,512]{1,0:T(8,128)(2,1)S(1)} collective-permute-done((bf16[512,512]{1,0:T(8,128)(2,1)S(1)}, bf16[512,512]{1,0:T(8,128)(2,1)S(1)}, u32[]{:S(2)}, u32[]{:S(2)}) %collective-permute-start.17) | collective-permute-done | bytes 524320 | tf_op jit(solution)/shard_map/ppermute | solution.py:47
  131.2 5.0 %collective-permute-done.18.e2 = bf16[512,512]{1,0:T(8,128)(2,1)S(1)} collective-permute-done((bf16[512,512]{1,0:T(8,128)(2,1)S(1)}, bf16[512,512]{1,0:T(8,128)(2,1)S(1)}, u32[]{:S(2)}, u32[]{:S(2)}) %collective-permute-start.18) | collective-permute-done | bytes 524320 | tf_op jit(solution)/shard_map/ppermute | solution.py:47
  136.2 6.2 %scores.1 = (bf16[4,1280,256]{2,1,0:T(8,128)(2,1)S(1)}, f32[512,256]{1,0:T(8,128)S(1)}, bf16[512,256]{1,0:T(8,128)(2,1)S(1)}, bf16[512,256]{1,0:T(8,128)(2,1)S(1)}) custom-call(s32[1,32]{1,0:T(1,128)S(1)} %bitcast.12, bf16[512,512]{1,0:T(8,128)(2,1)S(1)} %project.2.q_ref, bf16[512,512]{1,0:T(8,128)(2,1)S(1)} %project.3.own, ...), custom_call_target="tpu_custom_call" | custom-call | flops 2013265920 | bytes 5242880 | tf_op jit(solution)/shard_map/scores/pallas_call | solution.py:220
  142.4 4.3 %collective-permute-start.20 = (bf16[512,256]{1,0:T(8,128)(2,1)S(1)}, bf16[512,256]{1,0:T(8,128)(2,1)S(1)}, u32[]{:S(2)}, u32[]{:S(2)}) collective-permute-start(bf16[512,256]{1,0:T(8,128)(2,1)S(1)} %get-tuple-element.9), channel_id=1, source_target_pairs={{8,0},{16,8},{24,16},{32,24},{40,32},{48,40},{56,48},{64,56},{72,6... | collective-permute-start | bytes 786440 | tf_op jit(solution)/shard_map/ppermute | solution.py:47
  151.6 7.3 %collective-permute-done.19 = bf16[512,256]{1,0:T(8,128)(2,1)S(1)} collective-permute-done((bf16[512,256]{1,0:T(8,128)(2,1)S(1)}, bf16[512,256]{1,0:T(8,128)(2,1)S(1)}, u32[]{:S(2)}, u32[]{:S(2)}) %collective-permute-start.19) | collective-permute-done | bytes 262176 | tf_op jit(solution)/shard_map/ppermute | solution.py:47
  (36 shorter events, 28.3 us)
Async XLA Ops:
  0.6 46.5 %copy-start = (bf16[512,480]{0,1:T(8,128)(2,1)S(1)}, bf16[512,480]{0,1:T(8,128)(2,1)}, u32[]{:S(2)}) copy-start(bf16[512,480]{0,1:T(8,128)(2,1)} %param.6) | copy-start | bytes 1474564
  20.4 12.5 %collective-permute-start.12 = (bf16[4,128,512]{2,1,0:T(8,128)(2,1)S(1)}, bf16[4,128,512]{2,1,0:T(8,128)(2,1)S(1)}, u32[]{:S(2)}, u32[]{:S(2)}) collective-permute-start(bf16[4,128,512]{2,1,0:T(8,128)(2,1)S(1)} %bitcast.10), channel_id=1, source_target_pairs={{0,16},{8,120},{128,144},{136,248},{256,272},{264,376},{384,400},{... | collective-permute-start | bytes 1572872 | tf_op jit(solution)/shard_map/ppermute | solution.py:41
  23.9 14.7 %collective-permute-start.7 = (bf16[4,128,512]{2,1,0:T(8,128)(2,1)S(1)}, bf16[4,128,512]{2,1,0:T(8,128)(2,1)S(1)}, u32[]{:S(2)}, u32[]{:S(2)}) collective-permute-start(bf16[4,128,512]{2,1,0:T(8,128)(2,1)S(1)} %bitcast.8), channel_id=1, source_target_pairs={{0,16},{8,120},{128,144},{136,248},{256,272},{264,376},{384,400},{... | collective-permute-start | bytes 1572872 | tf_op jit(solution)/shard_map/ppermute | solution.py:41
  32.9 12.3 %collective-permute-start.13 = (bf16[4,128,512]{2,1,0:T(8,128)(2,1)S(1)}, bf16[4,128,512]{2,1,0:T(8,128)(2,1)S(1)}, u32[]{:S(2)}, u32[]{:S(2)}) collective-permute-start(bf16[4,128,512]{2,1,0:T(8,128)(2,1)S(1)} %collective-permute-done.12.refs_0_.refs_9_), channel_id=1, source_target_pairs={{0,16},{8,120},{128,144},{136,248},{256,272},{264,376},{384,400},{... | collective-permute-start | bytes 1572872 | tf_op jit(solution)/shard_map/ppermute | solution.py:41
  38.5 20.5 %collective-permute-start.8 = (bf16[4,128,512]{2,1,0:T(8,128)(2,1)S(1)}, bf16[4,128,512]{2,1,0:T(8,128)(2,1)S(1)}, u32[]{:S(2)}, u32[]{:S(2)}) collective-permute-start(bf16[4,128,512]{2,1,0:T(8,128)(2,1)S(1)} %collective-permute-done.7.refs_0_.refs_9_), channel_id=1, source_target_pairs={{0,16},{8,120},{128,144},{136,248},{256,272},{264,376},{384,400},{... | collective-permute-start | bytes 1572872 | tf_op jit(solution)/shard_map/ppermute | solution.py:41
  45.2 16.4 %collective-permute-start.14 = (bf16[4,128,512]{2,1,0:T(8,128)(2,1)S(1)}, bf16[4,128,512]{2,1,0:T(8,128)(2,1)S(1)}, u32[]{:S(2)}, u32[]{:S(2)}) collective-permute-start(bf16[4,128,512]{2,1,0:T(8,128)(2,1)S(1)} %collective-permute-done.13.refs_1_.refs_10_), channel_id=1, source_target_pairs={{0,16},{8,120},{128,144},{136,248},{256,272},{264,376},{384,400},{... | collective-permute-start | bytes 1572872 | tf_op jit(solution)/shard_map/ppermute | solution.py:41
  47.7 32.1 %collective-permute-start.3 = (bf16[512,512]{1,0:T(8,128)(2,1)S(1)}, bf16[512,512]{1,0:T(8,128)(2,1)S(1)}, u32[]{:S(2)}, u32[]{:S(2)}) collective-permute-start(bf16[512,512]{1,0:T(8,128)(2,1)S(1)} %fusion.refs_0_), channel_id=1, source_target_pairs={{0,1},{8,9},{128,129},{136,137},{256,257},{264,265},{384,385},{392... | collective-permute-start | bytes 1572872 | tf_op jit(solution)/shard_map/ppermute | solution.py:41
  55.9 27.0 %collective-permute-start = (bf16[512,512]{1,0:T(8,128)(2,1)S(1)}, bf16[512,512]{1,0:T(8,128)(2,1)S(1)}, u32[]{:S(2)}, u32[]{:S(2)}) collective-permute-start(bf16[512,512]{1,0:T(8,128)(2,1)S(1)} %fusion.refs_0_), channel_id=1, source_target_pairs={{0,2},{8,14},{128,130},{136,142},{256,258},{264,270},{384,386},{39... | collective-permute-start | bytes 1572872 | tf_op jit(solution)/shard_map/ppermute | solution.py:41
  59.1 26.3 %collective-permute-start.9 = (bf16[4,128,512]{2,1,0:T(8,128)(2,1)S(1)}, bf16[4,128,512]{2,1,0:T(8,128)(2,1)S(1)}, u32[]{:S(2)}, u32[]{:S(2)}) collective-permute-start(bf16[4,128,512]{2,1,0:T(8,128)(2,1)S(1)} %collective-permute-done.8.refs_1_.refs_10_), channel_id=1, source_target_pairs={{0,16},{8,120},{128,144},{136,248},{256,272},{264,376},{384,400},{... | collective-permute-start | bytes 1572872 | tf_op jit(solution)/shard_map/ppermute | solution.py:41
  61.7 51.2 %collective-permute-start.16 = (bf16[12,128,512]{2,1,0:T(8,128)(2,1)S(1)}, bf16[12,128,512]{2,1,0:T(8,128)(2,1)S(1)}, u32[]{:S(2)}, u32[]{:S(2)}) collective-permute-start(bf16[12,128,512]{2,1,0:T(8,128)(2,1)S(1)} %join.3), channel_id=1, source_target_pairs={{0,8},{8,0},{128,136},{136,128},{256,264},{264,256},{384,392},{392... | collective-permute-start | bytes 4718600 | tf_op jit(solution)/shard_map/ppermute | solution.py:41
  63.7 23.7 %collective-permute-start.2 = (bf16[512,512]{1,0:T(8,128)(2,1)S(1)}, bf16[512,512]{1,0:T(8,128)(2,1)S(1)}, u32[]{:S(2)}, u32[]{:S(2)}) collective-permute-start(bf16[512,512]{1,0:T(8,128)(2,1)S(1)} %fusion.refs_0_), channel_id=1, source_target_pairs={{0,6},{8,10},{128,134},{136,138},{256,262},{264,266},{384,390},{39... | collective-permute-start | bytes 1572872 | tf_op jit(solution)/shard_map/ppermute | solution.py:41
  79.8 11.3 %collective-permute-start.4 = (bf16[512,512]{1,0:T(8,128)(2,1)S(1)}, bf16[512,512]{1,0:T(8,128)(2,1)S(1)}, u32[]{:S(2)}, u32[]{:S(2)}) collective-permute-start(bf16[512,512]{1,0:T(8,128)(2,1)S(1)} %collective-permute-done.3.refs_4_), channel_id=1, source_target_pairs={{0,2},{8,14},{128,130},{136,142},{256,258},{264,270},{384,386},{39... | collective-permute-start | bytes 1572872 | tf_op jit(solution)/shard_map/ppermute | solution.py:41
  83.0 17.7 %collective-permute-start.1 = (bf16[512,512]{1,0:T(8,128)(2,1)S(1)}, bf16[512,512]{1,0:T(8,128)(2,1)S(1)}, u32[]{:S(2)}, u32[]{:S(2)}) collective-permute-start(bf16[512,512]{1,0:T(8,128)(2,1)S(1)} %collective-permute-done.refs_1_), channel_id=1, source_target_pairs={{0,2},{8,14},{128,130},{136,142},{256,258},{264,270},{384,386},{39... | collective-permute-start | bytes 1572872 | tf_op jit(solution)/shard_map/ppermute | solution.py:41
  85.4 33.9 %collective-permute-start.11 = (bf16[12,128,512]{2,1,0:T(8,128)(2,1)S(1)}, bf16[12,128,512]{2,1,0:T(8,128)(2,1)S(1)}, u32[]{:S(2)}, u32[]{:S(2)}) collective-permute-start(bf16[12,128,512]{2,1,0:T(8,128)(2,1)S(1)} %join.2), channel_id=1, source_target_pairs={{0,8},{8,0},{128,136},{136,128},{256,264},{264,256},{384,392},{392... | collective-permute-start | bytes 4718600 | tf_op jit(solution)/shard_map/ppermute | solution.py:41
  87.4 16.7 %collective-permute-start.6 = (bf16[512,512]{1,0:T(8,128)(2,1)S(1)}, bf16[512,512]{1,0:T(8,128)(2,1)S(1)}, u32[]{:S(2)}, u32[]{:S(2)}) collective-permute-start(bf16[512,512]{1,0:T(8,128)(2,1)S(1)} %collective-permute-done.3.refs_4_), channel_id=1, source_target_pairs={{0,6},{8,10},{128,134},{136,138},{256,262},{264,266},{384,390},{39... | collective-permute-start | bytes 1572872 | tf_op jit(solution)/shard_map/ppermute | solution.py:41
  91.2 16.6 %collective-permute-start.5 = (bf16[512,512]{1,0:T(8,128)(2,1)S(1)}, bf16[512,512]{1,0:T(8,128)(2,1)S(1)}, u32[]{:S(2)}, u32[]{:S(2)}) collective-permute-start(bf16[512,512]{1,0:T(8,128)(2,1)S(1)} %collective-permute-done.4.refs_5_), channel_id=1, source_target_pairs={{0,2},{8,14},{128,130},{136,142},{256,258},{264,270},{384,386},{39... | collective-permute-start | bytes 1572872 | tf_op jit(solution)/shard_map/ppermute | solution.py:41
  100.7 12.3 %collective-permute-start.15 = (bf16[4,128,512]{2,1,0:T(8,128)(2,1)S(1)}, bf16[4,128,512]{2,1,0:T(8,128)(2,1)S(1)}, u32[]{:S(2)}, u32[]{:S(2)}) collective-permute-start(bf16[4,128,512]{2,1,0:T(8,128)(2,1)S(1)} %collective-permute-done.14.refs_2_.refs_11_), channel_id=1, source_target_pairs={{0,16},{8,120},{128,144},{136,248},{256,272},{264,376},{384,400},{... | collective-permute-start | bytes 1572872 | tf_op jit(solution)/shard_map/ppermute | solution.py:41
  104.1 15.3 %collective-permute-start.10 = (bf16[4,128,512]{2,1,0:T(8,128)(2,1)S(1)}, bf16[4,128,512]{2,1,0:T(8,128)(2,1)S(1)}, u32[]{:S(2)}, u32[]{:S(2)}) collective-permute-start(bf16[4,128,512]{2,1,0:T(8,128)(2,1)S(1)} %collective-permute-done.9.refs_2_.refs_11_), channel_id=1, source_target_pairs={{0,16},{8,120},{128,144},{136,248},{256,272},{264,376},{384,400},{... | collective-permute-start | bytes 1572872 | tf_op jit(solution)/shard_map/ppermute | solution.py:41
  115.3 20.9 %copy-start.1 = (bf16[512,512]{1,0:T(8,128)(2,1)S(1)}, bf16[512,512]{1,0:T(8,128)(2,1)}, u32[]{:S(2)}) copy-start(bf16[512,512]{1,0:T(8,128)(2,1)} %g_ref.1) | copy-start | bytes 1572868
  115.4 20.9 %copy-start.2 = (s32[32]{0:T(128)S(1)}, s32[32]{0:T(128)}, u32[]{:S(2)}) copy-start(s32[32]{0:T(128)} %param.11) | copy-start | bytes 388
  115.4 15.9 %collective-permute-start.17 = (bf16[512,512]{1,0:T(8,128)(2,1)S(1)}, bf16[512,512]{1,0:T(8,128)(2,1)S(1)}, u32[]{:S(2)}, u32[]{:S(2)}) collective-permute-start(bf16[512,512]{1,0:T(8,128)(2,1)S(1)} %project.3.own), channel_id=1, source_target_pairs={{0,8},{8,16},{16,24},{24,32},{32,40},{40,48},{48,56},{56,64},{64,7... | collective-permute-start | bytes 1572872 | tf_op jit(solution)/shard_map/ppermute | solution.py:47
  117.4 18.8 %collective-permute-start.18 = (bf16[512,512]{1,0:T(8,128)(2,1)S(1)}, bf16[512,512]{1,0:T(8,128)(2,1)S(1)}, u32[]{:S(2)}, u32[]{:S(2)}) collective-permute-start(bf16[512,512]{1,0:T(8,128)(2,1)S(1)} %project.3.own), channel_id=1, source_target_pairs={{0,16},{8,24},{16,32},{24,40},{32,48},{40,56},{48,64},{56,72},{64,... | collective-permute-start | bytes 1572872 | tf_op jit(solution)/shard_map/ppermute | solution.py:47
  142.4 9.2 %collective-permute-start.20 = (bf16[512,256]{1,0:T(8,128)(2,1)S(1)}, bf16[512,256]{1,0:T(8,128)(2,1)S(1)}, u32[]{:S(2)}, u32[]{:S(2)}) collective-permute-start(bf16[512,256]{1,0:T(8,128)(2,1)S(1)} %get-tuple-element.9), channel_id=1, source_target_pairs={{8,0},{16,8},{24,16},{32,24},{40,32},{48,40},{56,48},{64,56},{72,6... | collective-permute-start | bytes 786440 | tf_op jit(solution)/shard_map/ppermute | solution.py:47
  146.7 12.1 %collective-permute-start.19 = (bf16[512,256]{1,0:T(8,128)(2,1)S(1)}, bf16[512,256]{1,0:T(8,128)(2,1)S(1)}, u32[]{:S(2)}, u32[]{:S(2)}) collective-permute-start(bf16[512,256]{1,0:T(8,128)(2,1)S(1)} %get-tuple-element.8), channel_id=1, source_target_pairs={{16,0},{24,8},{32,16},{40,24},{48,32},{56,40},{64,48},{72,56},{80,... | collective-permute-start | bytes 786440 | tf_op jit(solution)/shard_map/ppermute | solution.py:47

commit v4 on v3

--- a/solution.py
+++ b/solution.py
@@ -64,9 +64,10 @@
             return jnp.where(lax.div(chip, 4) == zh, near[:, pl.ds(at, PAIR)], far[:, pl.ds(at, PAIR)])
 
         left = [columns(d) for d in (0, 4, -1, 1, -2, 2, -3, 3)]
-        right = [own_ref[z], r4[z]]
+        right = [own_ref[z], own_ref[NZL + z], r4[z], r4[NZL + z]]
         for step, ref in enumerate((r1, r2, r3)):
-            right += [ref[z], swapped[NZL * step + z]]
+            at = 2 * NZL * step + z
+            right += [ref[z], ref[NZL + z], swapped[at], swapped[at + NZL]]
         total += jnp.dot(
             jnp.concatenate(left, axis=1),
             jnp.concatenate(right, axis=0),
@@ -112,12 +113,12 @@
 def join_body(*refs):
     *parts, o_ref = refs
     for i, part in enumerate(parts):
-        o_ref[i * NZL : (i + 1) * NZL] = part[...]
+        o_ref[i * 2 * NZL : (i + 1) * 2 * NZL] = part[...]
 
 
 def joined_blocks(blocks):
     full = pl.BlockSpec(memory_space=pltpu.VMEM)
-    shape = (len(blocks) * NZL,) + blocks[0].shape[1:]
+    shape = (len(blocks) * 2 * NZL,) + blocks[0].shape[1:]
     return pl.pallas_call(
         join_body,
         out_shape=jax.ShapeDtypeStruct(shape, BF),
@@ -130,10 +131,14 @@
 
 
 def gather_zcore(w):
-    groups = [
-        [z * 2 * NY + 2 * y + core for z in range(NZL) for core in range(2)] for y in range(NY)
-    ]
-    return lax.all_gather(w, "ctx", axis=0, tiled=False, axis_index_groups=groups)
+    def index(z, y, core):
+        return z * 2 * NY + 2 * y + core
+
+    lines = [[index(z, y, core) for z in range(NZL)] for y in range(NY) for core in range(2)]
+    chips = [[index(z, y, core) for core in range(2)] for z in range(NZL) for y in range(NY)]
+    w = lax.all_gather(w, "ctx", axis=0, tiled=False, axis_index_groups=lines)
+    w = lax.all_gather(w, "ctx", axis=0, tiled=False, axis_index_groups=chips)
+    return w.reshape((2 * NZL,) + w.shape[2:])
 
 
 TILE = 256
@@ -266,9 +271,9 @@
     w = gather_zcore(jnp.concatenate([key_matrix, value_matrix, w_query], axis=1))
     w = jnp.pad(w, ((0, 0), (0, PAD - ROWS), (0, 0)))
     kv_cols = 2 * HEAD_SIZE
-    kv = ring_y(w[:, :, :kv_cols].reshape(NZL, PAIR, kv_cols))
+    kv = ring_y(w[..., :kv_cols])
     kv_a = hop(joined_blocks(kv[1:4]), swap=1)
-    qs = ring_y(w[:, :, kv_cols:].reshape(NZL, PAIR, -1))
+    qs = ring_y(w[..., kv_cols:])
     q_a = hop(joined_blocks(qs[1:4]), swap=1)
 
     joined = project(near, far, kv, kv_a, 1.0)

time: 160 us -> 162 us (1.012)
  blocking collectives: 18.7 us -> 20.6 us
    all_gather x1 -> x2, blocking collectives: 18.7 us -> 20.6 us  [the longest x1 18.1 us: gather_zcore(): w = lax.all_gather(w, 'ctx', axis=0, tiled=False, axis_index_groups=lines)]
where the time goes in v4:
time: 162 us
  waiting for transfers between devices  65.5 us (40%)
  starting transfers between devices  59.4 us (37%)
  blocking collectives  20.6 us (13%)
  Pallas kernels  12.9 us (8%)
  other arithmetic  1.71 us (1%)
    ppermute x17, starting transfers between devices, hop(): return lax.ppermute(block, BOTH, route)  49.2 us
    ppermute x17, waiting for transfers between devices, hop(): return lax.ppermute(block, BOTH, route)  42.6 us
    ppermute x4, waiting for transfers between devices, along_ctx(): return lax.ppermute(block, 'ctx', route)  22.9 us
    all_gather x1, blocking collectives, gather_zcore(): w = lax.all_gather(w, 'ctx', axis=0, tiled=False, axis_index_groups=lines)  18.1 us
    ppermute x4, starting transfers between devices, along_ctx(): return lax.ppermute(block, 'ctx', route)  10.2 us
    pallas_call x1, Pallas kernels, attend(): pl.pallas_call(scores_body, out_shape=(shape((4, REACH, TILE), BF), shape...  6.17 us
    pallas_call x2, Pallas kernels, project(): pl.pallas_call(lambda *refs: project_body(*refs, scale=scale), out_shape=...  4.8 us
  transfers between devices with their start and end apart: 21, of which 12 were waited for; matrix products, arithmetic and copies ran while one was open for 0% of the time, Pallas kernels for 4%

profile of v4, /device:TPU:68, one launch (start us, length us, event | category | flops | bytes accessed | tf_op | source)
XLA Modules:
  0.0 161.7 jit_solution(1077106914663175297)
XLA Ops:
  1.6 18.1 %all-gather.2 = bf16[4,60,1024]{2,1,0:T(8,128)(2,1)S(1)} all-gather(bf16[1,60,1024]{2,1,0:T(8,128)(2,1)S(1)} %maximum_bitcast_fusion), channel_id=2, replica_groups={{0,128,256,384},{8,136,264,392},{16,144,272,400},{24,152,280,408},{32,1..., dimensions={0}, use_global_device_ids=true | all-gather | bytes 614400 | tf_op jit(solution)/shard_map/all_gather | solution.py:139
  19.6 2.5 %all-gather.1 = bf16[8,60,1024]{2,1,0:T(8,128)(2,1)S(1)} all-gather(bf16[4,60,1024]{2,1,0:T(8,128)(2,1)S(1)} %all-gather.2), channel_id=3, replica_groups={{0,8},{16,24},{32,40},{48,56},{64,72},{80,88},{96,104},{112,120},{128,1..., dimensions={0}, use_global_device_ids=true | all-gather | bytes 1474560 | tf_op jit(solution)/shard_map/all_gather | solution.py:140
  22.3 3.5 %collective-permute-start.12 = (bf16[8,64,512]{2,1,0:T(8,128)(2,1)S(1)}, bf16[8,64,512]{2,1,0:T(8,128)(2,1)S(1)}, u32[]{:S(2)}, u32[]{:S(2)}) collective-permute-start(bf16[8,64,512]{2,1,0:T(8,128)(2,1)S(1)} %get-tuple-element.10.refs_8_), channel_id=1, source_target_pairs={{0,16},{8,120},{128,144},{136,248},{256,272},{264,376},{384,400},{... | collective-permute-start | bytes 1572872 | tf_op jit(solution)/shard_map/ppermute | solution.py:41
  25.8 3.5 %collective-permute-start.7 = (bf16[8,64,512]{2,1,0:T(8,128)(2,1)S(1)}, bf16[8,64,512]{2,1,0:T(8,128)(2,1)S(1)}, u32[]{:S(2)}, u32[]{:S(2)}) collective-permute-start(bf16[8,64,512]{2,1,0:T(8,128)(2,1)S(1)} %get-tuple-element.11.refs_8_), channel_id=1, source_target_pairs={{0,16},{8,120},{128,144},{136,248},{256,272},{264,376},{384,400},{... | collective-permute-start | bytes 1572872 | tf_op jit(solution)/shard_map/ppermute | solution.py:41
  29.3 5.5 %collective-permute-done.12.refs_0_.refs_9_ = bf16[8,64,512]{2,1,0:T(8,128)(2,1)S(1)} collective-permute-done((bf16[8,64,512]{2,1,0:T(8,128)(2,1)S(1)}, bf16[8,64,512]{2,1,0:T(8,128)(2,1)S(1)}, u32[]{:S(2)}, u32[]{:S(2)}) %collective-permute-start.12) | collective-permute-done | bytes 524320 | tf_op jit(solution)/shard_map/ppermute | solution.py:41
  36.8 3.6 %collective-permute-done.7.refs_0_.refs_9_ = bf16[8,64,512]{2,1,0:T(8,128)(2,1)S(1)} collective-permute-done((bf16[8,64,512]{2,1,0:T(8,128)(2,1)S(1)}, bf16[8,64,512]{2,1,0:T(8,128)(2,1)S(1)}, u32[]{:S(2)}, u32[]{:S(2)}) %collective-permute-start.7) | collective-permute-done | bytes 524320 | tf_op jit(solution)/shard_map/ppermute | solution.py:41
  42.5 4.6 %collective-permute-done.13.refs_1_.refs_10_ = bf16[8,64,512]{2,1,0:T(8,128)(2,1)S(1)} collective-permute-done((bf16[8,64,512]{2,1,0:T(8,128)(2,1)S(1)}, bf16[8,64,512]{2,1,0:T(8,128)(2,1)S(1)}, u32[]{:S(2)}, u32[]{:S(2)}) %collective-permute-start.13) | collective-permute-done | bytes 524320 | tf_op jit(solution)/shard_map/ppermute | solution.py:41
  49.6 8.2 %collective-permute-start.3 = (bf16[512,512]{1,0:T(8,128)(2,1)S(1)}, bf16[512,512]{1,0:T(8,128)(2,1)S(1)}, u32[]{:S(2)}, u32[]{:S(2)}) collective-permute-start(bf16[512,512]{1,0:T(8,128)(2,1)S(1)} %fusion.refs_0_), channel_id=1, source_target_pairs={{0,1},{8,9},{128,129},{136,137},{256,257},{264,265},{384,385},{392... | collective-permute-start | bytes 1572872 | tf_op jit(solution)/shard_map/ppermute | solution.py:41
  57.8 3.1 %collective-permute-start = (bf16[512,512]{1,0:T(8,128)(2,1)S(1)}, bf16[512,512]{1,0:T(8,128)(2,1)S(1)}, u32[]{:S(2)}, u32[]{:S(2)}) collective-permute-start(bf16[512,512]{1,0:T(8,128)(2,1)S(1)} %fusion.refs_0_), channel_id=1, source_target_pairs={{0,2},{8,14},{128,130},{136,142},{256,258},{264,270},{384,386},{39... | collective-permute-start | bytes 1572872 | tf_op jit(solution)/shard_map/ppermute | solution.py:41
  61.0 2.6 %collective-permute-start.9 = (bf16[8,64,512]{2,1,0:T(8,128)(2,1)S(1)}, bf16[8,64,512]{2,1,0:T(8,128)(2,1)S(1)}, u32[]{:S(2)}, u32[]{:S(2)}) collective-permute-start(bf16[8,64,512]{2,1,0:T(8,128)(2,1)S(1)} %collective-permute-done.8.refs_1_.refs_10_), channel_id=1, source_target_pairs={{0,16},{8,120},{128,144},{136,248},{256,272},{264,376},{384,400},{... | collective-permute-start | bytes 1572872 | tf_op jit(solution)/shard_map/ppermute | solution.py:41
  65.6 2.7 %collective-permute-start.2 = (bf16[512,512]{1,0:T(8,128)(2,1)S(1)}, bf16[512,512]{1,0:T(8,128)(2,1)S(1)}, u32[]{:S(2)}, u32[]{:S(2)}) collective-permute-start(bf16[512,512]{1,0:T(8,128)(2,1)S(1)} %fusion.refs_0_), channel_id=1, source_target_pairs={{0,6},{8,10},{128,134},{136,138},{256,262},{264,266},{384,390},{39... | collective-permute-start | bytes 1572872 | tf_op jit(solution)/shard_map/ppermute | solution.py:41
  68.3 13.7 %collective-permute-done.3.refs_4_ = bf16[512,512]{1,0:T(8,128)(2,1)S(1)} collective-permute-done((bf16[512,512]{1,0:T(8,128)(2,1)S(1)}, bf16[512,512]{1,0:T(8,128)(2,1)S(1)}, u32[]{:S(2)}, u32[]{:S(2)}) %collective-permute-start.3) | collective-permute-done | bytes 524320 | tf_op jit(solution)/shard_map/ppermute | solution.py:41
  82.0 3.1 %collective-permute-start.4 = (bf16[512,512]{1,0:T(8,128)(2,1)S(1)}, bf16[512,512]{1,0:T(8,128)(2,1)S(1)}, u32[]{:S(2)}, u32[]{:S(2)}) collective-permute-start(bf16[512,512]{1,0:T(8,128)(2,1)S(1)} %collective-permute-done.3.refs_4_), channel_id=1, source_target_pairs={{0,2},{8,14},{128,130},{136,142},{256,258},{264,270},{384,386},{39... | collective-permute-start | bytes 1572872 | tf_op jit(solution)/shard_map/ppermute | solution.py:41
  85.1 2.4 %collective-permute-start.1 = (bf16[512,512]{1,0:T(8,128)(2,1)S(1)}, bf16[512,512]{1,0:T(8,128)(2,1)S(1)}, u32[]{:S(2)}, u32[]{:S(2)}) collective-permute-start(bf16[512,512]{1,0:T(8,128)(2,1)S(1)} %collective-permute-done.refs_1_), channel_id=1, source_target_pairs={{0,2},{8,14},{128,130},{136,142},{256,258},{264,270},{384,386},{39... | collective-permute-start | bytes 1572872 | tf_op jit(solution)/shard_map/ppermute | solution.py:41
  89.5 3.5 %collective-permute-start.6 = (bf16[512,512]{1,0:T(8,128)(2,1)S(1)}, bf16[512,512]{1,0:T(8,128)(2,1)S(1)}, u32[]{:S(2)}, u32[]{:S(2)}) collective-permute-start(bf16[512,512]{1,0:T(8,128)(2,1)S(1)} %collective-permute-done.3.refs_4_), channel_id=1, source_target_pairs={{0,6},{8,10},{128,134},{136,138},{256,262},{264,266},{384,390},{39... | collective-permute-start | bytes 1572872 | tf_op jit(solution)/shard_map/ppermute | solution.py:41
  93.0 3.1 %collective-permute-start.5 = (bf16[512,512]{1,0:T(8,128)(2,1)S(1)}, bf16[512,512]{1,0:T(8,128)(2,1)S(1)}, u32[]{:S(2)}, u32[]{:S(2)}) collective-permute-start(bf16[512,512]{1,0:T(8,128)(2,1)S(1)} %collective-permute-done.4.refs_5_), channel_id=1, source_target_pairs={{0,2},{8,14},{128,130},{136,142},{256,258},{264,270},{384,386},{39... | collective-permute-start | bytes 1572872 | tf_op jit(solution)/shard_map/ppermute | solution.py:41
  96.1 6.7 %collective-permute-done.1.refs_2_ = bf16[512,512]{1,0:T(8,128)(2,1)S(1)} collective-permute-done((bf16[512,512]{1,0:T(8,128)(2,1)S(1)}, bf16[512,512]{1,0:T(8,128)(2,1)S(1)}, u32[]{:S(2)}, u32[]{:S(2)}) %collective-permute-start.1) | collective-permute-done | bytes 524320 | tf_op jit(solution)/shard_map/ppermute | solution.py:41
  109.9 5.2 %collective-permute-done.15.refs_12_ = bf16[8,64,512]{2,1,0:T(8,128)(2,1)S(1)} collective-permute-done((bf16[8,64,512]{2,1,0:T(8,128)(2,1)S(1)}, bf16[8,64,512]{2,1,0:T(8,128)(2,1)S(1)}, u32[]{:S(2)}, u32[]{:S(2)}) %collective-permute-start.15) | collective-permute-done | bytes 524320 | tf_op jit(solution)/shard_map/ppermute | solution.py:41
  121.5 2.4 %project.2.q_ref = bf16[512,512]{1,0:T(8,128)(2,1)S(1)} custom-call(bf16[512,512]{1,0:T(8,128)(2,1)S(1)} %fusion.refs_0_, bf16[512,512]{1,0:T(8,128)(2,1)S(1)} %collective-permute-done.refs_1_, bf16[512,512]{1,0:T(8,128)(2,1)S(1)} %collective-permute-done.1.refs_2_, bf16[512,512]{1,0:T(8,128)(2,1)S(1)} %collective-permute-done.2.refs_3_, ...), custom_call_target="tpu_custom_call" | custom-call | flops 2147483648 | bytes 8912896 | tf_op jit(solution)/shard_map/project/pallas_call | solution.py:84
  123.9 9.4 %collective-permute-done.17.e1 = bf16[512,512]{1,0:T(8,128)(2,1)S(1)} collective-permute-done((bf16[512,512]{1,0:T(8,128)(2,1)S(1)}, bf16[512,512]{1,0:T(8,128)(2,1)S(1)}, u32[]{:S(2)}, u32[]{:S(2)}) %collective-permute-start.17) | collective-permute-done | bytes 524320 | tf_op jit(solution)/shard_map/ppermute | solution.py:47
  133.3 5.0 %collective-permute-done.18.e2 = bf16[512,512]{1,0:T(8,128)(2,1)S(1)} collective-permute-done((bf16[512,512]{1,0:T(8,128)(2,1)S(1)}, bf16[512,512]{1,0:T(8,128)(2,1)S(1)}, u32[]{:S(2)}, u32[]{:S(2)}) %collective-permute-start.18) | collective-permute-done | bytes 524320 | tf_op jit(solution)/shard_map/ppermute | solution.py:47
  138.3 6.2 %scores.1 = (bf16[4,1280,256]{2,1,0:T(8,128)(2,1)S(1)}, f32[512,256]{1,0:T(8,128)S(1)}, bf16[512,256]{1,0:T(8,128)(2,1)S(1)}, bf16[512,256]{1,0:T(8,128)(2,1)S(1)}) custom-call(s32[1,32]{1,0:T(1,128)S(1)} %bitcast.6, bf16[512,512]{1,0:T(8,128)(2,1)S(1)} %project.2.q_ref, bf16[512,512]{1,0:T(8,128)(2,1)S(1)} %project.3.own, ...), custom_call_target="tpu_custom_call" | custom-call | flops 2013265920 | bytes 5242880 | tf_op jit(solution)/shard_map/scores/pallas_call | solution.py:225
  144.5 4.3 %collective-permute-start.20 = (bf16[512,256]{1,0:T(8,128)(2,1)S(1)}, bf16[512,256]{1,0:T(8,128)(2,1)S(1)}, u32[]{:S(2)}, u32[]{:S(2)}) collective-permute-start(bf16[512,256]{1,0:T(8,128)(2,1)S(1)} %get-tuple-element.9), channel_id=1, source_target_pairs={{8,0},{16,8},{24,16},{32,24},{40,32},{48,40},{56,48},{64,56},{72,6... | collective-permute-start | bytes 786440 | tf_op jit(solution)/shard_map/ppermute | solution.py:47
  153.7 7.3 %collective-permute-done.19 = bf16[512,256]{1,0:T(8,128)(2,1)S(1)} collective-permute-done((bf16[512,256]{1,0:T(8,128)(2,1)S(1)}, bf16[512,256]{1,0:T(8,128)(2,1)S(1)}, u32[]{:S(2)}, u32[]{:S(2)}) %collective-permute-start.19) | collective-permute-done | bytes 262176 | tf_op jit(solution)/shard_map/ppermute | solution.py:47
  (37 shorter events, 30.7 us)
Async XLA Ops:
  0.6 48.4 %copy-start = (bf16[512,480]{0,1:T(8,128)(2,1)S(1)}, bf16[512,480]{0,1:T(8,128)(2,1)}, u32[]{:S(2)}) copy-start(bf16[512,480]{0,1:T(8,128)(2,1)} %param.6) | copy-start | bytes 1474564
  22.3 12.5 %collective-permute-start.12 = (bf16[8,64,512]{2,1,0:T(8,128)(2,1)S(1)}, bf16[8,64,512]{2,1,0:T(8,128)(2,1)S(1)}, u32[]{:S(2)}, u32[]{:S(2)}) collective-permute-start(bf16[8,64,512]{2,1,0:T(8,128)(2,1)S(1)} %get-tuple-element.10.refs_8_), channel_id=1, source_target_pairs={{0,16},{8,120},{128,144},{136,248},{256,272},{264,376},{384,400},{... | collective-permute-start | bytes 1572872 | tf_op jit(solution)/shard_map/ppermute | solution.py:41
  25.8 14.7 %collective-permute-start.7 = (bf16[8,64,512]{2,1,0:T(8,128)(2,1)S(1)}, bf16[8,64,512]{2,1,0:T(8,128)(2,1)S(1)}, u32[]{:S(2)}, u32[]{:S(2)}) collective-permute-start(bf16[8,64,512]{2,1,0:T(8,128)(2,1)S(1)} %get-tuple-element.11.refs_8_), channel_id=1, source_target_pairs={{0,16},{8,120},{128,144},{136,248},{256,272},{264,376},{384,400},{... | collective-permute-start | bytes 1572872 | tf_op jit(solution)/shard_map/ppermute | solution.py:41
  34.8 12.3 %collective-permute-start.13 = (bf16[8,64,512]{2,1,0:T(8,128)(2,1)S(1)}, bf16[8,64,512]{2,1,0:T(8,128)(2,1)S(1)}, u32[]{:S(2)}, u32[]{:S(2)}) collective-permute-start(bf16[8,64,512]{2,1,0:T(8,128)(2,1)S(1)} %collective-permute-done.12.refs_0_.refs_9_), channel_id=1, source_target_pairs={{0,16},{8,120},{128,144},{136,248},{256,272},{264,376},{384,400},{... | collective-permute-start | bytes 1572872 | tf_op jit(solution)/shard_map/ppermute | solution.py:41
  40.4 20.5 %collective-permute-start.8 = (bf16[8,64,512]{2,1,0:T(8,128)(2,1)S(1)}, bf16[8,64,512]{2,1,0:T(8,128)(2,1)S(1)}, u32[]{:S(2)}, u32[]{:S(2)}) collective-permute-start(bf16[8,64,512]{2,1,0:T(8,128)(2,1)S(1)} %collective-permute-done.7.refs_0_.refs_9_), channel_id=1, source_target_pairs={{0,16},{8,120},{128,144},{136,248},{256,272},{264,376},{384,400},{... | collective-permute-start | bytes 1572872 | tf_op jit(solution)/shard_map/ppermute | solution.py:41
  47.1 16.4 %collective-permute-start.14 = (bf16[8,64,512]{2,1,0:T(8,128)(2,1)S(1)}, bf16[8,64,512]{2,1,0:T(8,128)(2,1)S(1)}, u32[]{:S(2)}, u32[]{:S(2)}) collective-permute-start(bf16[8,64,512]{2,1,0:T(8,128)(2,1)S(1)} %collective-permute-done.13.refs_1_.refs_10_), channel_id=1, source_target_pairs={{0,16},{8,120},{128,144},{136,248},{256,272},{264,376},{384,400},{... | collective-permute-start | bytes 1572872 | tf_op jit(solution)/shard_map/ppermute | solution.py:41
  49.6 32.4 %collective-permute-start.3 = (bf16[512,512]{1,0:T(8,128)(2,1)S(1)}, bf16[512,512]{1,0:T(8,128)(2,1)S(1)}, u32[]{:S(2)}, u32[]{:S(2)}) collective-permute-start(bf16[512,512]{1,0:T(8,128)(2,1)S(1)} %fusion.refs_0_), channel_id=1, source_target_pairs={{0,1},{8,9},{128,129},{136,137},{256,257},{264,265},{384,385},{392... | collective-permute-start | bytes 1572872 | tf_op jit(solution)/shard_map/ppermute | solution.py:41
  57.8 27.2 %collective-permute-start = (bf16[512,512]{1,0:T(8,128)(2,1)S(1)}, bf16[512,512]{1,0:T(8,128)(2,1)S(1)}, u32[]{:S(2)}, u32[]{:S(2)}) collective-permute-start(bf16[512,512]{1,0:T(8,128)(2,1)S(1)} %fusion.refs_0_), channel_id=1, source_target_pairs={{0,2},{8,14},{128,130},{136,142},{256,258},{264,270},{384,386},{39... | collective-permute-start | bytes 1572872 | tf_op jit(solution)/shard_map/ppermute | solution.py:41
  61.0 26.5 %collective-permute-start.9 = (bf16[8,64,512]{2,1,0:T(8,128)(2,1)S(1)}, bf16[8,64,512]{2,1,0:T(8,128)(2,1)S(1)}, u32[]{:S(2)}, u32[]{:S(2)}) collective-permute-start(bf16[8,64,512]{2,1,0:T(8,128)(2,1)S(1)} %collective-permute-done.8.refs_1_.refs_10_), channel_id=1, source_target_pairs={{0,16},{8,120},{128,144},{136,248},{256,272},{264,376},{384,400},{... | collective-permute-start | bytes 1572872 | tf_op jit(solution)/shard_map/ppermute | solution.py:41
  63.6 51.4 %collective-permute-start.16 = (bf16[24,64,512]{2,1,0:T(8,128)(2,1)S(1)}, bf16[24,64,512]{2,1,0:T(8,128)(2,1)S(1)}, u32[]{:S(2)}, u32[]{:S(2)}) collective-permute-start(bf16[24,64,512]{2,1,0:T(8,128)(2,1)S(1)} %join.3), channel_id=1, source_target_pairs={{0,8},{8,0},{128,136},{136,128},{256,264},{264,256},{384,392},{392... | collective-permute-start | bytes 4718600 | tf_op jit(solution)/shard_map/ppermute | solution.py:41
  65.6 23.9 %collective-permute-start.2 = (bf16[512,512]{1,0:T(8,128)(2,1)S(1)}, bf16[512,512]{1,0:T(8,128)(2,1)S(1)}, u32[]{:S(2)}, u32[]{:S(2)}) collective-permute-start(bf16[512,512]{1,0:T(8,128)(2,1)S(1)} %fusion.refs_0_), channel_id=1, source_target_pairs={{0,6},{8,10},{128,134},{136,138},{256,262},{264,266},{384,390},{39... | collective-permute-start | bytes 1572872 | tf_op jit(solution)/shard_map/ppermute | solution.py:41
  82.0 11.1 %collective-permute-start.4 = (bf16[512,512]{1,0:T(8,128)(2,1)S(1)}, bf16[512,512]{1,0:T(8,128)(2,1)S(1)}, u32[]{:S(2)}, u32[]{:S(2)}) collective-permute-start(bf16[512,512]{1,0:T(8,128)(2,1)S(1)} %collective-permute-done.3.refs_4_), channel_id=1, source_target_pairs={{0,2},{8,14},{128,130},{136,142},{256,258},{264,270},{384,386},{39... | collective-permute-start | bytes 1572872 | tf_op jit(solution)/shard_map/ppermute | solution.py:41
  85.1 17.7 %collective-permute-start.1 = (bf16[512,512]{1,0:T(8,128)(2,1)S(1)}, bf16[512,512]{1,0:T(8,128)(2,1)S(1)}, u32[]{:S(2)}, u32[]{:S(2)}) collective-permute-start(bf16[512,512]{1,0:T(8,128)(2,1)S(1)} %collective-permute-done.refs_1_), channel_id=1, source_target_pairs={{0,2},{8,14},{128,130},{136,142},{256,258},{264,270},{384,386},{39... | collective-permute-start | bytes 1572872 | tf_op jit(solution)/shard_map/ppermute | solution.py:41
  87.6 33.9 %collective-permute-start.11 = (bf16[24,64,512]{2,1,0:T(8,128)(2,1)S(1)}, bf16[24,64,512]{2,1,0:T(8,128)(2,1)S(1)}, u32[]{:S(2)}, u32[]{:S(2)}) collective-permute-start(bf16[24,64,512]{2,1,0:T(8,128)(2,1)S(1)} %join.2), channel_id=1, source_target_pairs={{0,8},{8,0},{128,136},{136,128},{256,264},{264,256},{384,392},{392... | collective-permute-start | bytes 4718600 | tf_op jit(solution)/shard_map/ppermute | solution.py:41
  89.5 16.7 %collective-permute-start.6 = (bf16[512,512]{1,0:T(8,128)(2,1)S(1)}, bf16[512,512]{1,0:T(8,128)(2,1)S(1)}, u32[]{:S(2)}, u32[]{:S(2)}) collective-permute-start(bf16[512,512]{1,0:T(8,128)(2,1)S(1)} %collective-permute-done.3.refs_4_), channel_id=1, source_target_pairs={{0,6},{8,10},{128,134},{136,138},{256,262},{264,266},{384,390},{39... | collective-permute-start | bytes 1572872 | tf_op jit(solution)/shard_map/ppermute | solution.py:41
  93.0 16.8 %collective-permute-start.5 = (bf16[512,512]{1,0:T(8,128)(2,1)S(1)}, bf16[512,512]{1,0:T(8,128)(2,1)S(1)}, u32[]{:S(2)}, u32[]{:S(2)}) collective-permute-start(bf16[512,512]{1,0:T(8,128)(2,1)S(1)} %collective-permute-done.4.refs_5_), channel_id=1, source_target_pairs={{0,2},{8,14},{128,130},{136,142},{256,258},{264,270},{384,386},{39... | collective-permute-start | bytes 1572872 | tf_op jit(solution)/shard_map/ppermute | solution.py:41
  102.8 12.3 %collective-permute-start.15 = (bf16[8,64,512]{2,1,0:T(8,128)(2,1)S(1)}, bf16[8,64,512]{2,1,0:T(8,128)(2,1)S(1)}, u32[]{:S(2)}, u32[]{:S(2)}) collective-permute-start(bf16[8,64,512]{2,1,0:T(8,128)(2,1)S(1)} %collective-permute-done.14.refs_2_.refs_11_), channel_id=1, source_target_pairs={{0,16},{8,120},{128,144},{136,248},{256,272},{264,376},{384,400},{... | collective-permute-start | bytes 1572872 | tf_op jit(solution)/shard_map/ppermute | solution.py:41
  106.2 15.3 %collective-permute-start.10 = (bf16[8,64,512]{2,1,0:T(8,128)(2,1)S(1)}, bf16[8,64,512]{2,1,0:T(8,128)(2,1)S(1)}, u32[]{:S(2)}, u32[]{:S(2)}) collective-permute-start(bf16[8,64,512]{2,1,0:T(8,128)(2,1)S(1)} %collective-permute-done.9.refs_2_.refs_11_), channel_id=1, source_target_pairs={{0,16},{8,120},{128,144},{136,248},{256,272},{264,376},{384,400},{... | collective-permute-start | bytes 1572872 | tf_op jit(solution)/shard_map/ppermute | solution.py:41
  117.5 20.9 %copy-start.1 = (bf16[512,512]{1,0:T(8,128)(2,1)S(1)}, bf16[512,512]{1,0:T(8,128)(2,1)}, u32[]{:S(2)}) copy-start(bf16[512,512]{1,0:T(8,128)(2,1)} %g_ref.1) | copy-start | bytes 1572868
  117.5 20.9 %copy-start.2 = (s32[32]{0:T(128)S(1)}, s32[32]{0:T(128)}, u32[]{:S(2)}) copy-start(s32[32]{0:T(128)} %param.11) | copy-start | bytes 388
  117.5 15.9 %collective-permute-start.17 = (bf16[512,512]{1,0:T(8,128)(2,1)S(1)}, bf16[512,512]{1,0:T(8,128)(2,1)S(1)}, u32[]{:S(2)}, u32[]{:S(2)}) collective-permute-start(bf16[512,512]{1,0:T(8,128)(2,1)S(1)} %project.3.own), channel_id=1, source_target_pairs={{0,8},{8,16},{16,24},{24,32},{32,40},{40,48},{48,56},{56,64},{64,7... | collective-permute-start | bytes 1572872 | tf_op jit(solution)/shard_map/ppermute | solution.py:47
  119.5 18.8 %collective-permute-start.18 = (bf16[512,512]{1,0:T(8,128)(2,1)S(1)}, bf16[512,512]{1,0:T(8,128)(2,1)S(1)}, u32[]{:S(2)}, u32[]{:S(2)}) collective-permute-start(bf16[512,512]{1,0:T(8,128)(2,1)S(1)} %project.3.own), channel_id=1, source_target_pairs={{0,16},{8,24},{16,32},{24,40},{32,48},{40,56},{48,64},{56,72},{64,... | collective-permute-start | bytes 1572872 | tf_op jit(solution)/shard_map/ppermute | solution.py:47
  144.5 9.1 %collective-permute-start.20 = (bf16[512,256]{1,0:T(8,128)(2,1)S(1)}, bf16[512,256]{1,0:T(8,128)(2,1)S(1)}, u32[]{:S(2)}, u32[]{:S(2)}) collective-permute-start(bf16[512,256]{1,0:T(8,128)(2,1)S(1)} %get-tuple-element.9), channel_id=1, source_target_pairs={{8,0},{16,8},{24,16},{32,24},{40,32},{48,40},{56,48},{64,56},{72,6... | collective-permute-start | bytes 786440 | tf_op jit(solution)/shard_map/ppermute | solution.py:47
  148.8 12.1 %collective-permute-start.19 = (bf16[512,256]{1,0:T(8,128)(2,1)S(1)}, bf16[512,256]{1,0:T(8,128)(2,1)S(1)}, u32[]{:S(2)}, u32[]{:S(2)}) collective-permute-start(bf16[512,256]{1,0:T(8,128)(2,1)S(1)} %get-tuple-element.8), channel_id=1, source_target_pairs={{16,0},{24,8},{32,16},{40,24},{48,32},{56,40},{64,48},{72,56},{80,... | collective-permute-start | bytes 786440 | tf_op jit(solution)/shard_map/ppermute | solution.py:47

commit v5 on v4

--- a/solution.py
+++ b/solution.py
@@ -25,7 +25,7 @@
     return ctx * (NX * NZH) + x * NZH + z // NZL
 
 
-def hop(block, dx=0, dy=0, dz=0, swap=0, by_core=False):
+def hop(block, dx=0, dy=0, dz=0, swap=0, by_core=False, flip=0):
     route = []
     for x in range(NX):
         for y in range(NY):
@@ -35,7 +35,7 @@
                     route.append(
                         (
                             place(x, y, z, core),
-                            place(x + s * dx, y + s * dy, z + s * dz, core ^ swap),
+                            place(x + s * dx, y + s * dy, (z ^ flip) + s * dz, core ^ swap),
                         )
                     )
     return lax.ppermute(block, BOTH, route)
@@ -51,6 +51,7 @@
     ctx = lax.axis_index("ctx").astype(jnp.int32)
     head = lax.axis_index("head").astype(jnp.int32)
     y = lax.rem(lax.div(ctx, 2), NY)
+    own_z = lax.div(ctx, 2 * NY)
     sign = 1 - 2 * lax.rem(ctx, 2)
     x, zh = lax.div(head, NZH), lax.rem(head, NZH)
     total = jnp.zeros(o_ref.shape, F32)
@@ -64,10 +65,11 @@
             return jnp.where(lax.div(chip, 4) == zh, near[:, pl.ds(at, PAIR)], far[:, pl.ds(at, PAIR)])
 
         left = [columns(d) for d in (0, 4, -1, 1, -2, 2, -3, 3)]
-        right = [own_ref[z], own_ref[NZL + z], r4[z], r4[NZL + z]]
+        j = lax.bitwise_xor(z, own_z)
+        right = [own_ref[j], own_ref[NZL + j], r4[j], r4[NZL + j]]
         for step, ref in enumerate((r1, r2, r3)):
-            at = 2 * NZL * step + z
-            right += [ref[z], ref[NZL + z], swapped[at], swapped[at + NZL]]
+            at = 2 * NZL * step + j
+            right += [ref[j], ref[NZL + j], swapped[at], swapped[at + NZL]]
         total += jnp.dot(
             jnp.concatenate(left, axis=1),
             jnp.concatenate(right, axis=0),
@@ -112,13 +114,14 @@
 
 def join_body(*refs):
     *parts, o_ref = refs
+    n = parts[0].shape[0]
     for i, part in enumerate(parts):
-        o_ref[i * 2 * NZL : (i + 1) * 2 * NZL] = part[...]
+        o_ref[i * n : (i + 1) * n] = part[...]
 
 
 def joined_blocks(blocks):
     full = pl.BlockSpec(memory_space=pltpu.VMEM)
-    shape = (len(blocks) * 2 * NZL,) + blocks[0].shape[1:]
+    shape = (len(blocks) * blocks[0].shape[0],) + blocks[0].shape[1:]
     return pl.pallas_call(
         join_body,
         out_shape=jax.ShapeDtypeStruct(shape, BF),
@@ -131,13 +134,12 @@
 
 
 def gather_zcore(w):
-    def index(z, y, core):
-        return z * 2 * NY + 2 * y + core
-
-    lines = [[index(z, y, core) for z in range(NZL)] for y in range(NY) for core in range(2)]
-    chips = [[index(z, y, core) for core in range(2)] for z in range(NZL) for y in range(NY)]
-    w = lax.all_gather(w, "ctx", axis=0, tiled=False, axis_index_groups=lines)
-    w = lax.all_gather(w, "ctx", axis=0, tiled=False, axis_index_groups=chips)
+    w = w[None]
+    line = joined_blocks([w] + [hop(w, flip=j) for j in (1, 2, 3)])
+    chips = [
+        [z * 2 * NY + 2 * y + core for core in range(2)] for z in range(NZL) for y in range(NY)
+    ]
+    w = lax.all_gather(line, "ctx", axis=0, tiled=False, axis_index_groups=chips)
     return w.reshape((2 * NZL,) + w.shape[2:])
 
 

time: 162 us -> 165 us (1.019)
  blocking collectives: 20.6 us -> 2.56 us
  starting transfers between devices: 59.4 us -> 70.2 us
  waiting for transfers between devices: 65.5 us -> 74.9 us
    all_gather x2 -> x1, blocking collectives: 20.6 us -> 2.56 us  [gather_zcore(): lax.all_gather(line, 'ctx', axis=0, tiled=False, axis_index_groups=chips)]
    ppermute x17 -> x20, starting transfers between devices: 49.2 us -> 60.1 us  [hop(): return lax.ppermute(block, BOTH, route)]
    ppermute x17 -> x20, waiting for transfers between devices: 42.6 us -> 52 us  [hop(): return lax.ppermute(block, BOTH, route)]
  transfers between devices with their start and end apart: 21 -> 24, of which waited for: 12 -> 14; matrix products, arithmetic and copies ran while one was open for 0% -> 0% of each run, Pallas kernels for 4% -> 4%
where the time goes in v5:
time: 165 us; the launch traced here: 164 us
  waiting for transfers between devices  74.9 us (45%)
  starting transfers between devices  70.2 us (43%)
  Pallas kernels  12.9 us (8%)
  blocking collectives  2.56 us (2%)
  other arithmetic  1.71 us (1%)
    ppermute x20, starting transfers between devices, hop(): return lax.ppermute(block, BOTH, route)  60.1 us
    ppermute x20, waiting for transfers between devices, hop(): return lax.ppermute(block, BOTH, route)  52 us
    ppermute x4, waiting for transfers between devices, along_ctx(): return lax.ppermute(block, 'ctx', route)  22.9 us
    ppermute x4, starting transfers between devices, along_ctx(): return lax.ppermute(block, 'ctx', route)  10.2 us
    pallas_call x1, Pallas kernels, attend(): pl.pallas_call(scores_body, out_shape=(shape((4, REACH, TILE), BF), shape...  6.17 us
    pallas_call x2, Pallas kernels, project(): pl.pallas_call(lambda *refs: project_body(*refs, scale=scale), out_shape=...  4.8 us
  transfers between devices with their start and end apart: 24, of which 14 were waited for; matrix products, arithmetic and copies ran while one was open for 0% of the time, Pallas kernels for 4%

profile of v5, /device:TPU:68, one launch (start us, length us, event | category | flops | bytes accessed | tf_op | source)
XLA Modules:
  0.0 164.0 jit_solution(13932390652562531632)
XLA Ops:
  3.5 6.1 %collective-permute-start.8 = (bf16[1,60,1024]{2,1,0:T(8,128)(2,1)S(1)}, bf16[1,60,1024]{2,1,0:T(8,128)(2,1)S(1)}, u32[]{:S(2)}, u32[]{:S(2)}) collective-permute-start(bf16[1,60,1024]{2,1,0:T(8,128)(2,1)S(1)} %maximum_bitcast_fusion.refs_0_), channel_id=1, source_target_pairs={{0,256},{8,264},{128,384},{136,392},{256,0},{264,8},{384,128},{392... | collective-permute-start | bytes 368648 | tf_op jit(solution)/shard_map/ppermute | solution.py:41
  12.1 7.0 %collective-permute-done.8.refs_2_ = bf16[1,60,1024]{2,1,0:T(8,128)(2,1)S(1)} collective-permute-done((bf16[1,60,1024]{2,1,0:T(8,128)(2,1)S(1)}, bf16[1,60,1024]{2,1,0:T(8,128)(2,1)S(1)}, u32[]{:S(2)}, u32[]{:S(2)}) %collective-permute-start.8) | collective-permute-done | bytes 122912 | tf_op jit(solution)/shard_map/ppermute | solution.py:41
  19.1 2.6 %collective-permute-done.9.refs_3_ = bf16[1,60,1024]{2,1,0:T(8,128)(2,1)S(1)} collective-permute-done((bf16[1,60,1024]{2,1,0:T(8,128)(2,1)S(1)}, bf16[1,60,1024]{2,1,0:T(8,128)(2,1)S(1)}, u32[]{:S(2)}, u32[]{:S(2)}) %collective-permute-start.9) | collective-permute-done | bytes 122912 | tf_op jit(solution)/shard_map/ppermute | solution.py:41
  21.7 2.6 %all-gather = bf16[8,60,1024]{2,1,0:T(8,128)(2,1)S(1)} all-gather(bf16[4,60,1024]{2,1,0:T(8,128)(2,1)S(1)} %join.3), channel_id=2, replica_groups={{0,8},{16,24},{32,40},{48,56},{64,72},{80,88},{96,104},{112,120},{128,1..., dimensions={0}, use_global_device_ids=true | all-gather | bytes 1474560 | tf_op jit(solution)/shard_map/all_gather | solution.py:142
  24.4 3.5 %collective-permute-start.15 = (bf16[8,64,512]{2,1,0:T(8,128)(2,1)S(1)}, bf16[8,64,512]{2,1,0:T(8,128)(2,1)S(1)}, u32[]{:S(2)}, u32[]{:S(2)}) collective-permute-start(bf16[8,64,512]{2,1,0:T(8,128)(2,1)S(1)} %get-tuple-element.10.refs_8_), channel_id=1, source_target_pairs={{0,16},{8,120},{128,144},{136,248},{256,272},{264,376},{384,400},{... | collective-permute-start | bytes 1572872 | tf_op jit(solution)/shard_map/ppermute | solution.py:41
  27.9 3.5 %collective-permute-start.10 = (bf16[8,64,512]{2,1,0:T(8,128)(2,1)S(1)}, bf16[8,64,512]{2,1,0:T(8,128)(2,1)S(1)}, u32[]{:S(2)}, u32[]{:S(2)}) collective-permute-start(bf16[8,64,512]{2,1,0:T(8,128)(2,1)S(1)} %get-tuple-element.11.refs_8_), channel_id=1, source_target_pairs={{0,16},{8,120},{128,144},{136,248},{256,272},{264,376},{384,400},{... | collective-permute-start | bytes 1572872 | tf_op jit(solution)/shard_map/ppermute | solution.py:41
  31.3 5.5 %collective-permute-done.15.refs_0_.refs_9_ = bf16[8,64,512]{2,1,0:T(8,128)(2,1)S(1)} collective-permute-done((bf16[8,64,512]{2,1,0:T(8,128)(2,1)S(1)}, bf16[8,64,512]{2,1,0:T(8,128)(2,1)S(1)}, u32[]{:S(2)}, u32[]{:S(2)}) %collective-permute-start.15) | collective-permute-done | bytes 524320 | tf_op jit(solution)/shard_map/ppermute | solution.py:41
  38.9 3.6 %collective-permute-done.10.refs_0_.refs_9_ = bf16[8,64,512]{2,1,0:T(8,128)(2,1)S(1)} collective-permute-done((bf16[8,64,512]{2,1,0:T(8,128)(2,1)S(1)}, bf16[8,64,512]{2,1,0:T(8,128)(2,1)S(1)}, u32[]{:S(2)}, u32[]{:S(2)}) %collective-permute-start.10) | collective-permute-done | bytes 524320 | tf_op jit(solution)/shard_map/ppermute | solution.py:41
  44.5 4.6 %collective-permute-done.16.refs_1_.refs_10_ = bf16[8,64,512]{2,1,0:T(8,128)(2,1)S(1)} collective-permute-done((bf16[8,64,512]{2,1,0:T(8,128)(2,1)S(1)}, bf16[8,64,512]{2,1,0:T(8,128)(2,1)S(1)}, u32[]{:S(2)}, u32[]{:S(2)}) %collective-permute-start.16) | collective-permute-done | bytes 524320 | tf_op jit(solution)/shard_map/ppermute | solution.py:41
  51.7 8.6 %collective-permute-start.3 = (bf16[512,512]{1,0:T(8,128)(2,1)S(1)}, bf16[512,512]{1,0:T(8,128)(2,1)S(1)}, u32[]{:S(2)}, u32[]{:S(2)}) collective-permute-start(bf16[512,512]{1,0:T(8,128)(2,1)S(1)} %fusion.refs_0_), channel_id=1, source_target_pairs={{0,1},{8,9},{128,129},{136,137},{256,257},{264,265},{384,385},{392... | collective-permute-start | bytes 1572872 | tf_op jit(solution)/shard_map/ppermute | solution.py:41
  60.3 3.1 %collective-permute-start = (bf16[512,512]{1,0:T(8,128)(2,1)S(1)}, bf16[512,512]{1,0:T(8,128)(2,1)S(1)}, u32[]{:S(2)}, u32[]{:S(2)}) collective-permute-start(bf16[512,512]{1,0:T(8,128)(2,1)S(1)} %fusion.refs_0_), channel_id=1, source_target_pairs={{0,2},{8,14},{128,130},{136,142},{256,258},{264,270},{384,386},{39... | collective-permute-start | bytes 1572872 | tf_op jit(solution)/shard_map/ppermute | solution.py:41
  63.4 2.6 %collective-permute-start.12 = (bf16[8,64,512]{2,1,0:T(8,128)(2,1)S(1)}, bf16[8,64,512]{2,1,0:T(8,128)(2,1)S(1)}, u32[]{:S(2)}, u32[]{:S(2)}) collective-permute-start(bf16[8,64,512]{2,1,0:T(8,128)(2,1)S(1)} %collective-permute-done.11.refs_1_.refs_10_), channel_id=1, source_target_pairs={{0,16},{8,120},{128,144},{136,248},{256,272},{264,376},{384,400},{... | collective-permute-start | bytes 1572872 | tf_op jit(solution)/shard_map/ppermute | solution.py:41
  68.0 2.7 %collective-permute-start.2 = (bf16[512,512]{1,0:T(8,128)(2,1)S(1)}, bf16[512,512]{1,0:T(8,128)(2,1)S(1)}, u32[]{:S(2)}, u32[]{:S(2)}) collective-permute-start(bf16[512,512]{1,0:T(8,128)(2,1)S(1)} %fusion.refs_0_), channel_id=1, source_target_pairs={{0,6},{8,10},{128,134},{136,138},{256,262},{264,266},{384,390},{39... | collective-permute-start | bytes 1572872 | tf_op jit(solution)/shard_map/ppermute | solution.py:41
  70.8 13.5 %collective-permute-done.3.refs_4_ = bf16[512,512]{1,0:T(8,128)(2,1)S(1)} collective-permute-done((bf16[512,512]{1,0:T(8,128)(2,1)S(1)}, bf16[512,512]{1,0:T(8,128)(2,1)S(1)}, u32[]{:S(2)}, u32[]{:S(2)}) %collective-permute-start.3) | collective-permute-done | bytes 524320 | tf_op jit(solution)/shard_map/ppermute | solution.py:41
  84.3 3.1 %collective-permute-start.4 = (bf16[512,512]{1,0:T(8,128)(2,1)S(1)}, bf16[512,512]{1,0:T(8,128)(2,1)S(1)}, u32[]{:S(2)}, u32[]{:S(2)}) collective-permute-start(bf16[512,512]{1,0:T(8,128)(2,1)S(1)} %collective-permute-done.3.refs_4_), channel_id=1, source_target_pairs={{0,2},{8,14},{128,130},{136,142},{256,258},{264,270},{384,386},{39... | collective-permute-start | bytes 1572872 | tf_op jit(solution)/shard_map/ppermute | solution.py:41
  91.9 3.4 %collective-permute-start.6 = (bf16[512,512]{1,0:T(8,128)(2,1)S(1)}, bf16[512,512]{1,0:T(8,128)(2,1)S(1)}, u32[]{:S(2)}, u32[]{:S(2)}) collective-permute-start(bf16[512,512]{1,0:T(8,128)(2,1)S(1)} %collective-permute-done.3.refs_4_), channel_id=1, source_target_pairs={{0,6},{8,10},{128,134},{136,138},{256,262},{264,266},{384,390},{39... | collective-permute-start | bytes 1572872 | tf_op jit(solution)/shard_map/ppermute | solution.py:41
  95.4 3.1 %collective-permute-start.5 = (bf16[512,512]{1,0:T(8,128)(2,1)S(1)}, bf16[512,512]{1,0:T(8,128)(2,1)S(1)}, u32[]{:S(2)}, u32[]{:S(2)}) collective-permute-start(bf16[512,512]{1,0:T(8,128)(2,1)S(1)} %collective-permute-done.4.refs_5_), channel_id=1, source_target_pairs={{0,2},{8,14},{128,130},{136,142},{256,258},{264,270},{384,386},{39... | collective-permute-start | bytes 1572872 | tf_op jit(solution)/shard_map/ppermute | solution.py:41
  98.5 6.6 %collective-permute-done.1.refs_2_ = bf16[512,512]{1,0:T(8,128)(2,1)S(1)} collective-permute-done((bf16[512,512]{1,0:T(8,128)(2,1)S(1)}, bf16[512,512]{1,0:T(8,128)(2,1)S(1)}, u32[]{:S(2)}, u32[]{:S(2)}) %collective-permute-start.1) | collective-permute-done | bytes 524320 | tf_op jit(solution)/shard_map/ppermute | solution.py:41
  112.2 5.2 %collective-permute-done.18.refs_12_ = bf16[8,64,512]{2,1,0:T(8,128)(2,1)S(1)} collective-permute-done((bf16[8,64,512]{2,1,0:T(8,128)(2,1)S(1)}, bf16[8,64,512]{2,1,0:T(8,128)(2,1)S(1)}, u32[]{:S(2)}, u32[]{:S(2)}) %collective-permute-start.18) | collective-permute-done | bytes 524320 | tf_op jit(solution)/shard_map/ppermute | solution.py:41
  126.2 9.4 %collective-permute-done.20.e1 = bf16[512,512]{1,0:T(8,128)(2,1)S(1)} collective-permute-done((bf16[512,512]{1,0:T(8,128)(2,1)S(1)}, bf16[512,512]{1,0:T(8,128)(2,1)S(1)}, u32[]{:S(2)}, u32[]{:S(2)}) %collective-permute-start.20) | collective-permute-done | bytes 524320 | tf_op jit(solution)/shard_map/ppermute | solution.py:47
  135.6 5.0 %collective-permute-done.21.e2 = bf16[512,512]{1,0:T(8,128)(2,1)S(1)} collective-permute-done((bf16[512,512]{1,0:T(8,128)(2,1)S(1)}, bf16[512,512]{1,0:T(8,128)(2,1)S(1)}, u32[]{:S(2)}, u32[]{:S(2)}) %collective-permute-start.21) | collective-permute-done | bytes 524320 | tf_op jit(solution)/shard_map/ppermute | solution.py:47
  140.7 6.2 %scores.1 = (bf16[4,1280,256]{2,1,0:T(8,128)(2,1)S(1)}, f32[512,256]{1,0:T(8,128)S(1)}, bf16[512,256]{1,0:T(8,128)(2,1)S(1)}, bf16[512,256]{1,0:T(8,128)(2,1)S(1)}) custom-call(s32[1,32]{1,0:T(1,128)S(1)} %bitcast.6, bf16[512,512]{1,0:T(8,128)(2,1)S(1)} %project.2.q_ref, bf16[512,512]{1,0:T(8,128)(2,1)S(1)} %project.3.own, ...), custom_call_target="tpu_custom_call" | custom-call | flops 2013265920 | bytes 5242880 | tf_op jit(solution)/shard_map/scores/pallas_call | solution.py:227
  146.8 4.3 %collective-permute-start.23 = (bf16[512,256]{1,0:T(8,128)(2,1)S(1)}, bf16[512,256]{1,0:T(8,128)(2,1)S(1)}, u32[]{:S(2)}, u32[]{:S(2)}) collective-permute-start(bf16[512,256]{1,0:T(8,128)(2,1)S(1)} %get-tuple-element.9), channel_id=1, source_target_pairs={{8,0},{16,8},{24,16},{32,24},{40,32},{48,40},{56,48},{64,56},{72,6... | collective-permute-start | bytes 786440 | tf_op jit(solution)/shard_map/ppermute | solution.py:47
  156.0 7.3 %collective-permute-done.22 = bf16[512,256]{1,0:T(8,128)(2,1)S(1)} collective-permute-done((bf16[512,256]{1,0:T(8,128)(2,1)S(1)}, bf16[512,256]{1,0:T(8,128)(2,1)S(1)}, u32[]{:S(2)}, u32[]{:S(2)}) %collective-permute-start.22) | collective-permute-done | bytes 262176 | tf_op jit(solution)/shard_map/ppermute | solution.py:47
  (43 shorter events, 40.0 us)
Async XLA Ops:
  1.6 10.5 %collective-permute-start.7 = (bf16[1,60,1024]{2,1,0:T(8,128)(2,1)S(1)}, bf16[1,60,1024]{2,1,0:T(8,128)(2,1)S(1)}, u32[]{:S(2)}, u32[]{:S(2)}) collective-permute-start(bf16[1,60,1024]{2,1,0:T(8,128)(2,1)S(1)} %maximum_bitcast_fusion.refs_0_), channel_id=1, source_target_pairs={{0,128},{8,136},{128,0},{136,8},{256,384},{264,392},{384,256},{392... | collective-permute-start | bytes 368648 | tf_op jit(solution)/shard_map/ppermute | solution.py:41
  3.5 15.6 %collective-permute-start.8 = (bf16[1,60,1024]{2,1,0:T(8,128)(2,1)S(1)}, bf16[1,60,1024]{2,1,0:T(8,128)(2,1)S(1)}, u32[]{:S(2)}, u32[]{:S(2)}) collective-permute-start(bf16[1,60,1024]{2,1,0:T(8,128)(2,1)S(1)} %maximum_bitcast_fusion.refs_0_), channel_id=1, source_target_pairs={{0,256},{8,264},{128,384},{136,392},{256,0},{264,8},{384,128},{392... | collective-permute-start | bytes 368648 | tf_op jit(solution)/shard_map/ppermute | solution.py:41
  9.6 12.1 %collective-permute-start.9 = (bf16[1,60,1024]{2,1,0:T(8,128)(2,1)S(1)}, bf16[1,60,1024]{2,1,0:T(8,128)(2,1)S(1)}, u32[]{:S(2)}, u32[]{:S(2)}) collective-permute-start(bf16[1,60,1024]{2,1,0:T(8,128)(2,1)S(1)} %maximum_bitcast_fusion.refs_0_), channel_id=1, source_target_pairs={{0,384},{8,392},{128,256},{136,264},{256,128},{264,136},{384,0},{3... | collective-permute-start | bytes 368648 | tf_op jit(solution)/shard_map/ppermute | solution.py:41
  24.4 12.5 %collective-permute-start.15 = (bf16[8,64,512]{2,1,0:T(8,128)(2,1)S(1)}, bf16[8,64,512]{2,1,0:T(8,128)(2,1)S(1)}, u32[]{:S(2)}, u32[]{:S(2)}) collective-permute-start(bf16[8,64,512]{2,1,0:T(8,128)(2,1)S(1)} %get-tuple-element.10.refs_8_), channel_id=1, source_target_pairs={{0,16},{8,120},{128,144},{136,248},{256,272},{264,376},{384,400},{... | collective-permute-start | bytes 1572872 | tf_op jit(solution)/shard_map/ppermute | solution.py:41
  27.9 14.7 %collective-permute-start.10 = (bf16[8,64,512]{2,1,0:T(8,128)(2,1)S(1)}, bf16[8,64,512]{2,1,0:T(8,128)(2,1)S(1)}, u32[]{:S(2)}, u32[]{:S(2)}) collective-permute-start(bf16[8,64,512]{2,1,0:T(8,128)(2,1)S(1)} %get-tuple-element.11.refs_8_), channel_id=1, source_target_pairs={{0,16},{8,120},{128,144},{136,248},{256,272},{264,376},{384,400},{... | collective-permute-start | bytes 1572872 | tf_op jit(solution)/shard_map/ppermute | solution.py:41
  36.9 12.3 %collective-permute-start.16 = (bf16[8,64,512]{2,1,0:T(8,128)(2,1)S(1)}, bf16[8,64,512]{2,1,0:T(8,128)(2,1)S(1)}, u32[]{:S(2)}, u32[]{:S(2)}) collective-permute-start(bf16[8,64,512]{2,1,0:T(8,128)(2,1)S(1)} %collective-permute-done.15.refs_0_.refs_9_), channel_id=1, source_target_pairs={{0,16},{8,120},{128,144},{136,248},{256,272},{264,376},{384,400},{... | collective-permute-start | bytes 1572872 | tf_op jit(solution)/shard_map/ppermute | solution.py:41
  42.5 20.9 %collective-permute-start.11 = (bf16[8,64,512]{2,1,0:T(8,128)(2,1)S(1)}, bf16[8,64,512]{2,1,0:T(8,128)(2,1)S(1)}, u32[]{:S(2)}, u32[]{:S(2)}) collective-permute-start(bf16[8,64,512]{2,1,0:T(8,128)(2,1)S(1)} %collective-permute-done.10.refs_0_.refs_9_), channel_id=1, source_target_pairs={{0,16},{8,120},{128,144},{136,248},{256,272},{264,376},{384,400},{... | collective-permute-start | bytes 1572872 | tf_op jit(solution)/shard_map/ppermute | solution.py:41
  49.2 16.8 %collective-permute-start.17 = (bf16[8,64,512]{2,1,0:T(8,128)(2,1)S(1)}, bf16[8,64,512]{2,1,0:T(8,128)(2,1)S(1)}, u32[]{:S(2)}, u32[]{:S(2)}) collective-permute-start(bf16[8,64,512]{2,1,0:T(8,128)(2,1)S(1)} %collective-permute-done.16.refs_1_.refs_10_), channel_id=1, source_target_pairs={{0,16},{8,120},{128,144},{136,248},{256,272},{264,376},{384,400},{... | collective-permute-start | bytes 1572872 | tf_op jit(solution)/shard_map/ppermute | solution.py:41
  51.7 32.6 %collective-permute-start.3 = (bf16[512,512]{1,0:T(8,128)(2,1)S(1)}, bf16[512,512]{1,0:T(8,128)(2,1)S(1)}, u32[]{:S(2)}, u32[]{:S(2)}) collective-permute-start(bf16[512,512]{1,0:T(8,128)(2,1)S(1)} %fusion.refs_0_), channel_id=1, source_target_pairs={{0,1},{8,9},{128,129},{136,137},{256,257},{264,265},{384,385},{392... | collective-permute-start | bytes 1572872 | tf_op jit(solution)/shard_map/ppermute | solution.py:41
  60.3 27.1 %collective-permute-start = (bf16[512,512]{1,0:T(8,128)(2,1)S(1)}, bf16[512,512]{1,0:T(8,128)(2,1)S(1)}, u32[]{:S(2)}, u32[]{:S(2)}) collective-permute-start(bf16[512,512]{1,0:T(8,128)(2,1)S(1)} %fusion.refs_0_), channel_id=1, source_target_pairs={{0,2},{8,14},{128,130},{136,142},{256,258},{264,270},{384,386},{39... | collective-permute-start | bytes 1572872 | tf_op jit(solution)/shard_map/ppermute | solution.py:41
  63.4 26.4 %collective-permute-start.12 = (bf16[8,64,512]{2,1,0:T(8,128)(2,1)S(1)}, bf16[8,64,512]{2,1,0:T(8,128)(2,1)S(1)}, u32[]{:S(2)}, u32[]{:S(2)}) collective-permute-start(bf16[8,64,512]{2,1,0:T(8,128)(2,1)S(1)} %collective-permute-done.11.refs_1_.refs_10_), channel_id=1, source_target_pairs={{0,16},{8,120},{128,144},{136,248},{256,272},{264,376},{384,400},{... | collective-permute-start | bytes 1572872 | tf_op jit(solution)/shard_map/ppermute | solution.py:41
  66.1 51.3 %collective-permute-start.19 = (bf16[24,64,512]{2,1,0:T(8,128)(2,1)S(1)}, bf16[24,64,512]{2,1,0:T(8,128)(2,1)S(1)}, u32[]{:S(2)}, u32[]{:S(2)}) collective-permute-start(bf16[24,64,512]{2,1,0:T(8,128)(2,1)S(1)} %join.5), channel_id=1, source_target_pairs={{0,8},{8,0},{128,136},{136,128},{256,264},{264,256},{384,392},{392... | collective-permute-start | bytes 4718600 | tf_op jit(solution)/shard_map/ppermute | solution.py:41
  68.0 23.9 %collective-permute-start.2 = (bf16[512,512]{1,0:T(8,128)(2,1)S(1)}, bf16[512,512]{1,0:T(8,128)(2,1)S(1)}, u32[]{:S(2)}, u32[]{:S(2)}) collective-permute-start(bf16[512,512]{1,0:T(8,128)(2,1)S(1)} %fusion.refs_0_), channel_id=1, source_target_pairs={{0,6},{8,10},{128,134},{136,138},{256,262},{264,266},{384,390},{39... | collective-permute-start | bytes 1572872 | tf_op jit(solution)/shard_map/ppermute | solution.py:41
  84.3 11.1 %collective-permute-start.4 = (bf16[512,512]{1,0:T(8,128)(2,1)S(1)}, bf16[512,512]{1,0:T(8,128)(2,1)S(1)}, u32[]{:S(2)}, u32[]{:S(2)}) collective-permute-start(bf16[512,512]{1,0:T(8,128)(2,1)S(1)} %collective-permute-done.3.refs_4_), channel_id=1, source_target_pairs={{0,2},{8,14},{128,130},{136,142},{256,258},{264,270},{384,386},{39... | collective-permute-start | bytes 1572872 | tf_op jit(solution)/shard_map/ppermute | solution.py:41
  87.4 17.7 %collective-permute-start.1 = (bf16[512,512]{1,0:T(8,128)(2,1)S(1)}, bf16[512,512]{1,0:T(8,128)(2,1)S(1)}, u32[]{:S(2)}, u32[]{:S(2)}) collective-permute-start(bf16[512,512]{1,0:T(8,128)(2,1)S(1)} %collective-permute-done.refs_1_), channel_id=1, source_target_pairs={{0,2},{8,14},{128,130},{136,142},{256,258},{264,270},{384,386},{39... | collective-permute-start | bytes 1572872 | tf_op jit(solution)/shard_map/ppermute | solution.py:41
  89.9 33.8 %collective-permute-start.14 = (bf16[24,64,512]{2,1,0:T(8,128)(2,1)S(1)}, bf16[24,64,512]{2,1,0:T(8,128)(2,1)S(1)}, u32[]{:S(2)}, u32[]{:S(2)}) collective-permute-start(bf16[24,64,512]{2,1,0:T(8,128)(2,1)S(1)} %join.4), channel_id=1, source_target_pairs={{0,8},{8,0},{128,136},{136,128},{256,264},{264,256},{384,392},{392... | collective-permute-start | bytes 4718600 | tf_op jit(solution)/shard_map/ppermute | solution.py:41
  91.9 16.7 %collective-permute-start.6 = (bf16[512,512]{1,0:T(8,128)(2,1)S(1)}, bf16[512,512]{1,0:T(8,128)(2,1)S(1)}, u32[]{:S(2)}, u32[]{:S(2)}) collective-permute-start(bf16[512,512]{1,0:T(8,128)(2,1)S(1)} %collective-permute-done.3.refs_4_), channel_id=1, source_target_pairs={{0,6},{8,10},{128,134},{136,138},{256,262},{264,266},{384,390},{39... | collective-permute-start | bytes 1572872 | tf_op jit(solution)/shard_map/ppermute | solution.py:41
  95.4 16.9 %collective-permute-start.5 = (bf16[512,512]{1,0:T(8,128)(2,1)S(1)}, bf16[512,512]{1,0:T(8,128)(2,1)S(1)}, u32[]{:S(2)}, u32[]{:S(2)}) collective-permute-start(bf16[512,512]{1,0:T(8,128)(2,1)S(1)} %collective-permute-done.4.refs_5_), channel_id=1, source_target_pairs={{0,2},{8,14},{128,130},{136,142},{256,258},{264,270},{384,386},{39... | collective-permute-start | bytes 1572872 | tf_op jit(solution)/shard_map/ppermute | solution.py:41
  105.1 12.3 %collective-permute-start.18 = (bf16[8,64,512]{2,1,0:T(8,128)(2,1)S(1)}, bf16[8,64,512]{2,1,0:T(8,128)(2,1)S(1)}, u32[]{:S(2)}, u32[]{:S(2)}) collective-permute-start(bf16[8,64,512]{2,1,0:T(8,128)(2,1)S(1)} %collective-permute-done.17.refs_2_.refs_11_), channel_id=1, source_target_pairs={{0,16},{8,120},{128,144},{136,248},{256,272},{264,376},{384,400},{... | collective-permute-start | bytes 1572872 | tf_op jit(solution)/shard_map/ppermute | solution.py:41
  108.6 15.2 %collective-permute-start.13 = (bf16[8,64,512]{2,1,0:T(8,128)(2,1)S(1)}, bf16[8,64,512]{2,1,0:T(8,128)(2,1)S(1)}, u32[]{:S(2)}, u32[]{:S(2)}) collective-permute-start(bf16[8,64,512]{2,1,0:T(8,128)(2,1)S(1)} %collective-permute-done.12.refs_2_.refs_11_), channel_id=1, source_target_pairs={{0,16},{8,120},{128,144},{136,248},{256,272},{264,376},{384,400},{... | collective-permute-start | bytes 1572872 | tf_op jit(solution)/shard_map/ppermute | solution.py:41
  119.8 15.9 %collective-permute-start.20 = (bf16[512,512]{1,0:T(8,128)(2,1)S(1)}, bf16[512,512]{1,0:T(8,128)(2,1)S(1)}, u32[]{:S(2)}, u32[]{:S(2)}) collective-permute-start(bf16[512,512]{1,0:T(8,128)(2,1)S(1)} %project.3.own), channel_id=1, source_target_pairs={{0,8},{8,16},{16,24},{24,32},{32,40},{40,48},{48,56},{56,64},{64,7... | collective-permute-start | bytes 1572872 | tf_op jit(solution)/shard_map/ppermute | solution.py:47
  121.8 18.8 %collective-permute-start.21 = (bf16[512,512]{1,0:T(8,128)(2,1)S(1)}, bf16[512,512]{1,0:T(8,128)(2,1)S(1)}, u32[]{:S(2)}, u32[]{:S(2)}) collective-permute-start(bf16[512,512]{1,0:T(8,128)(2,1)S(1)} %project.3.own), channel_id=1, source_target_pairs={{0,16},{8,24},{16,32},{24,40},{32,48},{40,56},{48,64},{56,72},{64,... | collective-permute-start | bytes 1572872 | tf_op jit(solution)/shard_map/ppermute | solution.py:47
  146.8 9.1 %collective-permute-start.23 = (bf16[512,256]{1,0:T(8,128)(2,1)S(1)}, bf16[512,256]{1,0:T(8,128)(2,1)S(1)}, u32[]{:S(2)}, u32[]{:S(2)}) collective-permute-start(bf16[512,256]{1,0:T(8,128)(2,1)S(1)} %get-tuple-element.9), channel_id=1, source_target_pairs={{8,0},{16,8},{24,16},{32,24},{40,32},{48,40},{56,48},{64,56},{72,6... | collective-permute-start | bytes 786440 | tf_op jit(solution)/shard_map/ppermute | solution.py:47
  151.1 12.1 %collective-permute-start.22 = (bf16[512,256]{1,0:T(8,128)(2,1)S(1)}, bf16[512,256]{1,0:T(8,128)(2,1)S(1)}, u32[]{:S(2)}, u32[]{:S(2)}) collective-permute-start(bf16[512,256]{1,0:T(8,128)(2,1)S(1)} %get-tuple-element.8), channel_id=1, source_target_pairs={{16,0},{24,8},{32,16},{40,24},{48,32},{56,40},{64,48},{72,56},{80,... | collective-permute-start | bytes 786440 | tf_op jit(solution)/shard_map/ppermute | solution.py:47
  (3 other events, 92.2 us)
